TPU v7x, 32 devices: a whole 2x2x4 slice. The times are simulated.
32 devices in a mesh: slab: 16 (over z, y, x), col: 2 (over core).
Axes of the slice: x: 2, y: 2, z: 4, core: 2. Of those that a mesh axis runs over, the one named last changes fastest.
Arguments:
- direction: float32 [2048, 4096], P('slab', 'col'), may hold values from -6 to 6
- kappa: float32 [2048, 4096], P('slab', 'col'), may hold values from 0.04 to 0.24
- land_mask: int32 [2048, 4096], P('slab', 'col'), may hold values 0 or 1
- owned_segments: int32 [256], replicated, may hold values from -1 to 127, as said below
- seg_anchor: int32 [128, 2], replicated, may hold values from 0 to 31, as said below
- interp_index: int32 [128, 32], replicated, may hold values from 0 to 15
- interp_table: bfloat16 [16, 64, 64], replicated, may hold values from -0.75 to 0.75
- precision: bfloat16 [2048, 2048], replicated, as said below
- obs_scale: float32 [256, 2048], P(('slab', 'col')), may hold values from 0.4 to 2
Outputs:
- product: float32 [2048, 4096], P('slab', 'col')
Inputs may be any that keep to these rules, and one draw needn't show every extreme that they name: `owned_segments`: slots d * 8 to (d + 1) * 8 - 1 belong to device d = slab index * 2 + col index, used slots first; each segment stands in exactly one slot, empty slots hold -1; a device's segments have column tiles held by devices of its own col index; the two devices of one col index at slab indices 2t and 2t + 1 hold 8 segments together; some device fills all 8 slots; at most 8 segments of one device share a first row tile, and some device has that many. `seg_anchor`: number the used slots of one col index in order of slab index, then slot, as ranks r = 0, 1, ...; the segment at rank r has first row tile 32 * ((r + r // (the number of slab indices)) % 1). `precision`: Symmetric.
All inputs are finite; a program needn't handle non-finite values. No bound on the sum of `land_mask` on one device may be relied on, other than what follows from the above.
Results may differ from a plain program's by a relative error of at most 0.0019.
Values may be sent and summed in bfloat16 or wider, within the bound.
No kernel may reach another device: no remote copies, remote signals or barrier semaphores. Data moves between devices by JAX's collectives and lax.ppermute only.
A program may use at most 128 MiB of HBM per device.

v0:
```python
import functools

import jax
import jax.numpy as jnp
from jax import lax
from jax.experimental import pallas as pl
from jax.experimental.pallas import tpu as pltpu
from jax.sharding import PartitionSpec as P

TILE_C = 128
SWEEPS = 4
HALO = 8
PAD = 16
CAP = 3


def lane_iota(shape):
    return lax.broadcasted_iota(jnp.int32, shape, len(shape) - 1)


def row_iota(shape):
    return lax.broadcasted_iota(jnp.int32, shape, len(shape) - 2)


def from_left(own, left):
    lanes = own.shape[-1]
    return pltpu.roll(jnp.where(lane_iota(own.shape) == lanes - 1, left, own), 1, 1)


def from_right(own, right):
    lanes = own.shape[-1]
    return pltpu.roll(jnp.where(lane_iota(own.shape) == 0, right, own), lanes - 1, 1)


def face(own, other):
    return jnp.where((own > 0) & (other > 0), 0.5 * (own + other), 0.0)


def sweeps(tiles, rows, bufs, own_ref, fn_ref, fw_ref, fe_ref, finish):
    for step in range(SWEEPS):
        src, dst = bufs[step % 2], bufs[1 - step % 2]
        last = step == SWEEPS - 1
        first_row = PAD if last else HALO
        length = (rows - 2 * (PAD - HALO) if last else rows) // 2

        for half in range(2):
            start = first_row + half * length
            body = pl.ds(start, length)

            def tile(c, right, u_left, u, src=src, dst=dst, last=last, start=start, body=body):
                u_right = src[right, body, :]
                up = src[c, pl.ds(start - 1, length), :]
                down = src[c, pl.ds(start + 1, length), :]
                out = own_ref[c, body, :] * u + fn_ref[c, body, :] * up
                out = out + fn_ref[c, pl.ds(start + 1, length), :] * down
                out = out + fw_ref[c, body, :] * from_left(u, u_left)
                out = out + fe_ref[c, body, :] * from_right(u, u_right)
                if last:
                    finish(c, start - PAD, out)
                else:
                    dst[c, body, :] = out
                return u, u_right

            def step_tile(c, carry):
                return tile(c, c + 1, *carry)

            carry = src[tiles - 1, body, :], src[0, body, :]
            carry = lax.fori_loop(0, tiles - 1, step_tile, carry, unroll=4)
            if not last:
                tile(tiles - 1, 0, *carry)


def smooth_first_kernel(
    dir_ref, kap_ref, mask_ref, nbr_ref, top_ref, bot_ref,
    out_ref, own_ref, fn_ref, fw_ref, fe_ref, u0, u1, kbuf,
):
    tiles, height, lanes = u0.shape
    own = dir_ref.shape[0]
    rows = own + 2 * HALO
    edge = (HALO, lanes)
    zero = jnp.zeros(edge, jnp.float32)

    def halos(c):
        cols = pl.ds(pl.multiple_of(c * lanes, lanes), lanes)
        low = row_iota(edge) < HALO // 2
        top = top_ref[:, cols]
        bot = bot_ref[:, cols]
        u0[c, pl.ds(0, HALO), :] = zero
        u1[c, pl.ds(0, HALO), :] = zero
        kbuf[c, pl.ds(0, HALO), :] = zero
        u0[c, pl.ds(HALO, HALO), :] = jnp.where(low, 0.0, pltpu.roll(top, HALO // 2, 0))
        kbuf[c, pl.ds(HALO, HALO), :] = jnp.where(low, 0.0, top)
        u0[c, pl.ds(PAD + own, HALO), :] = jnp.where(low, bot, 0.0)
        kbuf[c, pl.ds(PAD + own, HALO), :] = jnp.where(low, pltpu.roll(bot, HALO // 2, 0), 0.0)
        end = pl.ds(PAD + own + HALO, HALO)
        u0[c, end, :] = zero
        u1[c, end, :] = zero
        kbuf[c, end, :] = zero
        fn_ref[c, end, :] = zero

    def fill(c, carry):
        cols = pl.ds(pl.multiple_of(c * lanes, lanes), lanes)
        maskf = mask_ref[:, cols].astype(jnp.float32)
        u0[c, pl.ds(PAD, own), :] = dir_ref[:, cols] * maskf
        kbuf[c, pl.ds(PAD, own), :] = kap_ref[:, cols] * maskf
        halos(c)
        return carry

    lax.fori_loop(0, tiles - 1, fill, 0)
    u0[tiles - 1, pl.ds(PAD, own), :] = nbr_ref[0]
    kbuf[tiles - 1, pl.ds(PAD, own), :] = nbr_ref[1]
    halos(tiles - 1)

    def faces(c, right, k_left, k):
        body = pl.ds(HALO, rows)
        k_right = kbuf[right, body, :]
        north = face(k, kbuf[c, pl.ds(HALO - 1, rows), :])
        south = face(k, kbuf[c, pl.ds(HALO + 1, rows), :])
        west = face(k, from_left(k, k_left))
        east = face(k, from_right(k, k_right))
        fn_ref[c, body, :] = north
        fw_ref[c, body, :] = west
        fe_ref[c, body, :] = east
        own_ref[c, body, :] = 1.0 - ((north + south) + (west + east))
        return k, k_right

    body = pl.ds(HALO, rows)
    carry = kbuf[tiles - 1, body, :], kbuf[0, body, :]
    carry = lax.fori_loop(0, tiles - 1, lambda c, carry: faces(c, c + 1, *carry), carry)
    faces(tiles - 1, 0, *carry)

    def finish(c, row, value):
        out_ref[c, pl.ds(row, value.shape[0]), :] = value.astype(jnp.bfloat16)

    sweeps(tiles, rows, (u0, u1), own_ref, fn_ref, fw_ref, fe_ref, finish)


def smooth_last_kernel(
    ret_ref, nbr_ref, own_ref, fn_ref, fw_ref, fe_ref, dir_ref, mask_ref, out_ref, u0, u1
):
    tiles, height, lanes = u0.shape
    own = dir_ref.shape[0]
    rows = own + 2 * HALO
    zero = jnp.zeros((HALO, lanes), jnp.float32)

    def ends(c):
        for buf in (u0, u1):
            buf[c, pl.ds(0, HALO), :] = zero
            buf[c, pl.ds(PAD + own + HALO, HALO), :] = zero

    def fill(c, carry):
        u0[c, pl.ds(HALO, rows), :] = ret_ref[c].astype(jnp.float32)
        ends(c)
        return carry

    lax.fori_loop(0, tiles - 1, fill, 0)
    u0[tiles - 1, pl.ds(HALO, rows), :] = nbr_ref[...].astype(jnp.float32)
    ends(tiles - 1)

    def finish(c, row, value):
        cols = pl.ds(pl.multiple_of(c * lanes, lanes), lanes)
        part = pl.ds(row, value.shape[0])
        maskf = mask_ref[part, cols].astype(jnp.float32)
        out_ref[part, cols] = maskf * (dir_ref[part, cols] * maskf + value)

    sweeps(tiles, rows, (u0, u1), own_ref, fn_ref, fw_ref, fe_ref, finish)


def outbox_kernel(owned_ref, anchor_ref, scale_ref, out_ref, *, seg_tiles, col_tiles, span):
    seg_max = scale_ref.shape[0]
    me = lax.axis_index("slab") * lax.axis_size("col") + lax.axis_index("col")
    owners = []
    for i in range(seg_max):
        seg = owned_ref[me * seg_max + i]
        safe = jnp.maximum(seg, 0)
        lane = anchor_ref[2 * safe] // seg_tiles
        owner = lane * span + lax.rem(anchor_ref[2 * safe + 1], col_tiles)
        owner = jnp.where(seg >= 0, owner, -1)
        place = jnp.int32(0)
        for other in owners:
            place = place + jnp.where(other == owner, 1, 0)
        owners.append(owner)

        @pl.when((seg >= 0) & (place < CAP))
        def _(i=i, owner=owner, place=place):
            out_ref[owner * CAP + place] = scale_ref[i : i + 1, :]


def segments_kernel(
    info_ref, index_ref, x_ref, ahead_ref, behind_ref, prec_ref, few_ref, all_ref,
    out_ref, turned, weighted, zbuf, scale_row, adj, grid, scale_sem, *, width, batch,
):
    parts, chunk, lanes = out_ref.shape
    order = prec_ref.shape[0]
    blocks = order // lanes
    count = info_ref[0]
    full = info_ref[1]
    groups = (count + batch - 1) // batch

    def scale_copy(source, row, slot, j):
        return pltpu.make_async_copy(source.at[row], scale_row.at[slot, j], scale_sem.at[slot, j])

    def fetch(g, slot):
        for j in range(batch):
            e = g * batch + j

            @pl.when((e < count) & (full == 0))
            def _(e=e, j=j):
                scale_copy(few_ref, info_ref[3 + 3 * e], slot, j).start()

            @pl.when((e < count) & (full != 0))
            def _(e=e, j=j):
                scale_copy(all_ref, info_ref[4 + 3 * e], slot, j).start()

    fetch(0, 0)

    def turn(q, carry):
        part = pl.ds(pl.multiple_of(q * lanes, lanes), lanes)
        turned[:, part] = x_ref[part, :].astype(jnp.float32).T.astype(jnp.bfloat16)
        adj[:, part] = jnp.zeros((lanes, lanes), jnp.float32)
        return carry

    lax.fori_loop(0, blocks, turn, 0, unroll=4)

    def work(g, size):
        slot = lax.rem(g, 2)
        ids = [info_ref[2 + 3 * (g * batch + j)] for j in range(size)]
        for j in range(size):
            scale_copy(few_ref, 0, slot, j).wait()
        fetch(g + 1, 1 - slot)

        def pair_of(table, q):
            sides = []
            for j in range(size):
                low = table[0, index_ref[ids[j], 2 * q]]
                high = table[1, index_ref[ids[j], 2 * q + 1]]
                sides.append(jnp.concatenate([low, high], axis=0))
            return sides

        def interp(q, carry):
            part = pl.ds(pl.multiple_of(q * lanes, lanes), lanes)
            right = jnp.concatenate(pair_of(ahead_ref, q), axis=1)
            seg = jnp.dot(turned[:, part], right, preferred_element_type=jnp.float32)
            seg = seg.astype(jnp.bfloat16).astype(jnp.float32)
            for j in range(size):
                value = seg[:, j * lanes : (j + 1) * lanes] * scale_row[slot, j, :, part]
                weighted[j * lanes : (j + 1) * lanes, part] = value.astype(jnp.bfloat16)
            return carry

        lax.fori_loop(0, blocks, interp, 0, unroll=4)

        for i in range(order // width):
            cols = pl.ds(i * width, width)
            prod = jnp.dot(
                weighted[: size * lanes, :], prec_ref[:, cols],
                preferred_element_type=jnp.float32,
            )
            for j in range(size):
                rows = slice(j * lanes, (j + 1) * lanes)
                zbuf[rows, cols] = (prod[rows] * scale_row[slot, j, :, cols]).astype(jnp.bfloat16)

        def back(q, carry):
            part = pl.ds(pl.multiple_of(q * lanes, lanes), lanes)
            left = jnp.concatenate(
                [zbuf[j * lanes : (j + 1) * lanes, part] for j in range(size)], axis=1
            )
            right = jnp.concatenate(pair_of(behind_ref, q), axis=0)
            adj[:, part] = adj[:, part] + jnp.dot(left, right, preferred_element_type=jnp.float32)
            return carry

        lax.fori_loop(0, blocks, back, 0, unroll=4)

    def whole_group(g, carry):
        work(g, batch)
        return carry

    lax.fori_loop(0, count // batch, whole_group, 0)
    for size in range(1, batch):

        @pl.when(lax.rem(count, batch) == size)
        def _(size=size):
            work(count // batch, size)

    zero = jnp.zeros((HALO, lanes), jnp.float32)
    grid[pl.ds(0, HALO), :] = zero
    grid[pl.ds(order + HALO, HALO), :] = zero

    def unturn(q, carry):
        part = pl.ds(pl.multiple_of(q * lanes, lanes), lanes)
        grid[pl.ds(pl.multiple_of(q * lanes + HALO, HALO), lanes), :] = adj[:, part].T
        return carry

    lax.fori_loop(0, blocks, unturn, 0, unroll=4)
    own = chunk - 2 * HALO
    for s in range(parts):
        out_ref[s] = grid[pl.ds(s * own, chunk), :].astype(jnp.bfloat16)


def vmem_need(rows):
    return min(2 * rows * TILE_C * 4, 60 << 20)


def vmem_spec():
    return pl.BlockSpec(memory_space=pltpu.VMEM)


def any_spec():
    return pl.BlockSpec(memory_space=pl.ANY)


def smem_spec():
    return pl.BlockSpec(memory_space=pltpu.SMEM)


def per_device(
    direction, kappa, land_mask, owned_segments, seg_anchor,
    interp_index, interp_table, precision, obs_scale,
):
    rows_dev, cols_dev = direction.shape
    blocks, tile_r, _ = interp_table.shape
    order = precision.shape[0]
    segs, seg_tiles = interp_index.shape
    seg_max = obs_scale.shape[0]
    lanes = TILE_C
    col_tiles = cols_dev // lanes
    slab_count = lax.axis_size("slab")
    col_count = lax.axis_size("col")
    dev_count = slab_count * col_count
    span = order // rows_dev
    assert span == col_tiles and col_count == 2 and slab_count % span == 0
    groups = [list(range(i, i + span)) for i in range(0, slab_count, span)]
    if len(groups) == 1:
        groups = None
    my_slab = lax.axis_index("slab")
    my_col = lax.axis_index("col")
    my_device = my_slab * col_count + my_col
    is_low = my_col == 0

    def edge_cols(array):
        return jnp.where(is_low, array[:, cols_dev - lanes :], array[:, :lanes])

    edge_mask = edge_cols(land_mask).astype(jnp.float32)
    edge = jnp.stack([edge_cols(direction) * edge_mask, edge_cols(kappa) * edge_mask])
    nbr = lax.ppermute(edge, "col", [(0, 1), (1, 0)])
    near = jnp.where(
        is_low, lane_iota((1, lanes)) < SWEEPS, lane_iota((1, lanes)) >= lanes - SWEEPS
    )
    nbr = jnp.where(near[None], nbr, 0.0)

    def edge_rows(start):
        part = slice(start, start + SWEEPS)
        maskf = land_mask[part].astype(jnp.float32)
        field = jnp.concatenate([direction[part] * maskf, nbr[0, part]], axis=1)
        coeff = jnp.concatenate([kappa[part] * maskf, nbr[1, part]], axis=1)
        return jnp.concatenate([field, coeff], axis=0)

    first_rows, last_rows = edge_rows(0), edge_rows(rows_dev - SWEEPS)
    even = my_slab % 2 == 0
    pairs_a = [(i, i ^ 1) for i in range(slab_count)]
    pairs_b = [(i, i + 1) for i in range(1, slab_count - 1, 2)]
    pairs_b = pairs_b + [(j, i) for i, j in pairs_b]
    send_a = jnp.where(even, last_rows, first_rows)
    send_b = jnp.where(even, first_rows, last_rows)
    got_a = lax.ppermute(send_a, "slab", pairs_a)
    got_b = lax.ppermute(send_b, "slab", pairs_b)
    owned_segments, seg_anchor, send_a = lax.optimization_barrier(
        (owned_segments, seg_anchor, send_a)
    )
    top = jnp.where(even, got_b, got_a)
    bot = jnp.where(even, got_a, got_b)

    slots = dev_count * seg_max
    slot_ids = jnp.arange(slots, dtype=jnp.int32)
    used = owned_segments >= 0
    seg_hot = owned_segments[:, None] == jnp.arange(segs, dtype=jnp.int32)[None, :]
    anchor_row = jnp.sum(jnp.where(seg_hot, seg_anchor[None, :, 0], 0), axis=1)
    anchor_col = jnp.sum(jnp.where(seg_hot, seg_anchor[None, :, 1], 0), axis=1)
    owner_slab = anchor_row // seg_tiles * span + anchor_col % col_tiles
    owner = owner_slab * col_count + anchor_col // col_tiles
    owner = jnp.where(used, owner, -1)
    by_dev = owner.reshape(dev_count, seg_max)
    slot_in = jnp.arange(seg_max, dtype=jnp.int32)
    before = slot_in[None, :] < slot_in[:, None]
    same = (by_dev[:, :, None] == by_dev[:, None, :]) & before[None]
    place = jnp.sum(same.astype(jnp.int32), axis=2).reshape(slots)
    overflow = jnp.max(jnp.where(used, place, 0)) >= CAP
    mine = owner == my_device
    rank = jnp.cumsum(mine.astype(jnp.int32)) - 1
    count = jnp.sum(mine.astype(jnp.int32))
    longest = segs
    pick = mine[None, :] & (rank[None, :] == jnp.arange(longest, dtype=jnp.int32)[:, None])
    src_slab = slot_ids // (seg_max * col_count)
    columns = [
        owned_segments,
        src_slab * CAP + jnp.minimum(place, CAP - 1),
        src_slab * seg_max + slot_ids % seg_max,
    ]
    listed = jnp.stack(
        [jnp.sum(jnp.where(pick, col[None, :], 0), axis=1) for col in columns], axis=1
    )
    info = jnp.concatenate(
        [count[None], overflow.astype(jnp.int32)[None], listed.reshape(-1)]
    )

    my_owner = lax.dynamic_slice_in_dim(owner_slab, my_device * seg_max, seg_max)
    my_used = lax.dynamic_slice_in_dim(used, my_device * seg_max, seg_max)

    def outbox(cap, position):
        target = jnp.arange(slab_count * cap, dtype=jnp.int32)
        hit = (
            (my_owner * cap + position)[None, :] == target[:, None]
        ) & (my_used & (position < cap))[None, :]
        slot = jnp.sum(jnp.where(hit, slot_in[None, :], 0), axis=1)
        return obs_scale[slot].reshape(slab_count * cap, 1, order)

    def swap(array, groups=None):
        return lax.all_to_all(
            array, "slab", split_axis=0, concat_axis=0, tiled=True, axis_index_groups=groups
        )

    few = swap(
        pl.pallas_call(
            functools.partial(outbox_kernel, seg_tiles=seg_tiles, col_tiles=col_tiles, span=span),
            out_shape=jax.ShapeDtypeStruct((slab_count * CAP, 1, order), jnp.float32),
            in_specs=[smem_spec(), smem_spec(), vmem_spec()],
            out_specs=vmem_spec(),
            compiler_params=pltpu.CompilerParams(vmem_limit_bytes=2 << 20),
            name="outbox",
        )(owned_segments, seg_anchor.reshape(-1), obs_scale)
    )
    everything = lax.cond(
        overflow,
        lambda: swap(outbox(seg_max, slot_in)),
        lambda: jnp.zeros((slab_count * seg_max, 1, order), jnp.float32),
    )

    tiles = col_tiles + 1
    height = rows_dev + 2 * PAD
    buf = pltpu.VMEM((tiles, height, lanes), jnp.float32)
    face_shape = jax.ShapeDtypeStruct((tiles, height, lanes), jnp.float32)
    smoothed, own, fn, fw, fe = pl.pallas_call(
        smooth_first_kernel,
        out_shape=(
            jax.ShapeDtypeStruct((col_tiles, rows_dev, lanes), jnp.bfloat16),
            face_shape, face_shape, face_shape, face_shape,
        ),
        in_specs=[vmem_spec()] * 6,
        out_specs=(vmem_spec(),) * 5,
        scratch_shapes=[buf, buf, buf],
        compiler_params=pltpu.CompilerParams(vmem_limit_bytes=vmem_need(8 * tiles * height)),
        cost_estimate=pl.CostEstimate(flops=40000000, bytes_accessed=8 << 20, transcendentals=0),
        name="smooth_first",
    )(direction, kappa, land_mask, nbr, top, bot)

    gathered = swap(smoothed, groups)

    chunk = rows_dev + 2 * HALO
    width = min(512, order)
    batch = 4

    def sides(table):
        empty = jnp.zeros_like(table)
        return jnp.stack(
            [jnp.concatenate([table, empty], axis=2), jnp.concatenate([empty, table], axis=2)]
        )

    returning = pl.pallas_call(
        functools.partial(segments_kernel, width=width, batch=batch),
        out_shape=jax.ShapeDtypeStruct((span, chunk, lanes), jnp.bfloat16),
        in_specs=[smem_spec(), smem_spec(), vmem_spec(), vmem_spec(), vmem_spec(), vmem_spec()]
        + [any_spec()] * 2,
        out_specs=vmem_spec(),
        scratch_shapes=[
            pltpu.VMEM((lanes, order), jnp.bfloat16),
            pltpu.VMEM((batch * lanes, order), jnp.bfloat16),
            pltpu.VMEM((batch * lanes, order), jnp.bfloat16),
            pltpu.VMEM((2, batch, 1, order), jnp.float32),
            pltpu.VMEM((lanes, order), jnp.float32),
            pltpu.VMEM((order + 2 * HALO, lanes), jnp.float32),
            pltpu.SemaphoreType.DMA((2, batch)),
        ],
        compiler_params=pltpu.CompilerParams(vmem_limit_bytes=vmem_need(order * order // 256)),
        cost_estimate=pl.CostEstimate(
            flops=8 * 2 * order * order * lanes, bytes_accessed=12 << 20, transcendentals=0
        ),
        name="segments",
    )(
        info, interp_index, gathered.reshape(order, lanes),
        sides(interp_table.transpose(0, 2, 1)), sides(interp_table), precision, few, everything,
    )

    returned = swap(returning, groups)

    if groups is not None:
        returned = lane_edges(returned, slab_count, span, my_slab, rows_dev)

    border = jnp.where(is_low, returned[col_tiles - 1], returned[0])
    border = lax.ppermute(border, "col", [(0, 1), (1, 0)])
    return pl.pallas_call(
        smooth_last_kernel,
        out_shape=jax.ShapeDtypeStruct((rows_dev, cols_dev), jnp.float32),
        in_specs=[vmem_spec()] * 8,
        out_specs=vmem_spec(),
        scratch_shapes=[buf, buf],
        compiler_params=pltpu.CompilerParams(vmem_limit_bytes=vmem_need(8 * tiles * height)),
        cost_estimate=pl.CostEstimate(flops=40000000, bytes_accessed=8 << 20, transcendentals=0),
        name="smooth_last",
    )(returned, border, own, fn, fw, fe, direction, land_mask)


def lane_edges(returned, slab_count, span, my_slab, rows_dev):
    up = [(i, i + 1) for i in range(span - 1, slab_count - 1, span)]
    down = [(j, i) for i, j in up]
    own_last = returned[:, rows_dev : rows_dev + HALO]
    own_first = returned[:, HALO : 2 * HALO]
    above = lax.ppermute(own_last, "slab", up)
    below = lax.ppermute(own_first, "slab", down)
    first = (my_slab % span == 0)
    last = (my_slab % span == span - 1)
    head = jnp.where(first, above, returned[:, :HALO])
    tail = jnp.where(last, below, returned[:, rows_dev + HALO :])
    return jnp.concatenate([head, returned[:, HALO : rows_dev + HALO], tail], axis=1)


def solution(mesh):
    in_specs = (
        P("slab", "col"),
        P("slab", "col"),
        P("slab", "col"),
        P(),
        P(),
        P(),
        P(),
        P(),
        P(("slab", "col"), None),
    )
    return jax.shard_map(
        per_device, mesh=mesh, in_specs=in_specs, out_specs=P("slab", "col"), check_vma=False
    )
```

profile of v0, /device:TPU:0, one launch (start us, length us, event | category | flops | bytes accessed | tf_op | source)
XLA Modules:
  0.0 110.7 jit_solution(3721388857113160222)
XLA Ops:
  0.0 1.1 multiply_bitcast_fusion.1
  2.7 1.8 %copy.28 = bf16[16,64,64]{1,2,0:T(8,128)(2,1)} copy(bf16[16,64,64]{2,1,0:T(8,128)(2,1)} %param.17) | data formatting | bytes 262144 | tf_op args[6]
  5.7 2.6 %collective-permute-start.2 = (f32[8,2176]{1,0:T(8,128)S(1)}, f32[8,2176]{1,0:T(8,128)S(1)}, u32[]{:S(2)}, u32[]{:S(2)}) collective-permute-start(f32[8,2176]{1,0:T(8,128)S(1)} %get-tuple-element.78), channel_id=1, source_target_pairs={{0,2},{2,0},{4,6},{6,4},{8,10},{10,8},{12,14},{14,12},{16,18},{18,... | collective-permute-start | bytes 208904 | tf_op jit(solution)/shard_map/ppermute | solution.py:364
  8.5 1.2 %convert_reduce_fusion.1 = (s32[]{:T(128)}, pred[256]{0:T(512)(128)(4,1)}, s32[256]{0:T(256)S(1)}, s32[256]{0:T(256)S(1)}, pred[256]{0:T(512)(128)(4,1)S(1)}) fusion(s32[]{:T(128)} %add.87, s32[256]{0:T(256)S(1)} %get-tuple-element.57, s32[256]{0:T(256)S(1)} %get-tuple-element.56, s32[256]{0:T(256)S(1)} %copy-done.13), kind=kLoop, calls=%fused_computation.64 | loop fusion | flops 11007 | bytes 5640 | tf_op jit(solution)/shard_map/reduce_sum | solution.py:389
  10.1 1.3 %select_reduce_fusion.6 = (s32[]{:T(128)}, s32[256]{0:T(256)}, s32[256]{0:T(256)}) fusion(pred[256]{0:T(512)(128)(4,1)S(1)} %get-tuple-element.62, s32[256]{0:T(256)S(1)} %reshape.122), kind=kLoop, calls=%fused_computation.71 | loop fusion | flops 5375 | bytes 3332 | tf_op jit(solution)/shard_map/reduce_max | solution.py:386
  12.2 1.3 %collective-permute-start.1 = (f32[8,2176]{1,0:T(8,128)S(1)}, f32[8,2176]{1,0:T(8,128)}, u32[]{:S(2)}, u32[]{:S(2)}) collective-permute-start(f32[8,2176]{1,0:T(8,128)S(1)} %get-tuple-element.77), channel_id=1, source_target_pairs={{2,4},{6,8},{10,12},{14,16},{18,20},{22,24},{26,28},{4,2},{8,6},{1... | collective-permute-start | bytes 208904 | tf_op jit(solution)/shard_map/ppermute | solution.py:365
  13.5 1.5 %outbox.1 = f32[48,1,2048]{2,1,0:T(1,128)} custom-call(s32[256]{0:T(256)S(1)} %copy-done.13, s32[256]{0:T(256)S(1)} %reshape.127.anchor_ref, f32[8,2048]{1,0:T(8,128)S(1)} %copy-done.15), custom_call_target="tpu_custom_call" | custom-call | tf_op jit(solution)/shard_map/outbox/pallas_call | solution.py:422
  15.0 1.5 %conditional.1 = (f32[128,1,2048]{2,1,0:T(1,128)}) conditional(s32[]{:T(128)} %convert_element_type.25, () %tuple.15, (s32[]{:T(128)}, s32[256]{0:T(256)S(1)}, s32[8]{0:T(128)S(1)}, pred[256]{0:T(512)(128)(4,1)S(1)}, s32[8]{0:T(128)S(1)}, /*index=5*/s32[8]{0:T(128)S(1)}, f32[8,2048]{1,0:T(8,128)S(1)}) %tuple.42), branch_computations={%region_10.11_spmd, %region_11.13_spmd} | conditional | flops 5412 | bytes 6298390 | solution.py:431
  15.0 1.5 %broadcast.163 = f32[128,1,2048]{2,1,0:T(1,128)} broadcast(f32[]{:T(128)} %constant.93.clone), dimensions={} | broadcast | bytes 1048580 | tf_op jit(solution)/shard_map/broadcast.5
  16.6 8.2 %all-to-all-start.2 = ((f32[48,1,2048]{2,1,0:T(1,128)}), f32[48,1,2048]{2,1,0:T(1,128)}, u32[]{:S(2)}, u32[]{:S(2)}) async-start(f32[48,1,2048]{2,1,0:T(1,128)} %outbox.1), calls=%async_computation.2 | async-start | bytes 786432 | tf_op jit(solution)/shard_map/all_to_all | solution.py:417
  24.8 2.0 %pad_bitcast_fusion.3 = (bf16[1,16,64,128]{3,2,1,0:T(8,128)(2,1)}, bf16[1,16,64,128]{3,2,1,0:T(8,128)(2,1)}) fusion(bf16[16,64,64]{2,1,0:T(8,128)(2,1)} %bitcast.44), kind=kLoop, calls=%fused_computation.14 | loop fusion | bytes 655360 | tf_op jit(solution)/shard_map/stack | solution.py:463
  28.6 8.3 %smooth_first.1 = (bf16[16,128,128]{2,1,0:T(8,128)(2,1)S(1)}, f32[17,160,128]{2,1,0:T(8,128)S(1)}, f32[17,160,128]{2,1,0:T(8,128)S(1)}, f32[17,160,128]{2,1,0:T(8,128)S(1)}, f32[17,160,128]{2,1,0:T(8,128)S(1)}) custom-call(f32[128,2048]{1,0:T(8,128)S(1)} %copy-done, f32[128,2048]{1,0:T(8,128)S(1)} %copy-done.2, s32[128,2048]{1,0:T(8,128)S(1)} %copy-done.1, ...), custom_call_target="tpu_custom_call" | custom-call | flops 40000000 | bytes 8388608 | tf_op jit(solution)/shard_map/smooth_first/pallas_call | solution.py:441
  36.9 1.1 copy-done.3
  38.0 1.1 copy-done.5
  39.1 1.1 copy-done.7
  40.2 1.1 %copy-done.9 = f32[17,160,128]{2,1,0:T(8,128)} copy-done((f32[17,160,128]{2,1,0:T(8,128)}, f32[17,160,128]{2,1,0:T(8,128)S(1)}, u32[]{:S(2)}) %copy-start.9) | copy-done | bytes 1392664
  42.1 6.9 %all-to-all-start.1 = ((bf16[16,128,128]{2,1,0:T(8,128)(2,1)}), bf16[16,128,128]{2,1,0:T(8,128)(2,1)S(1)}, u32[]{:S(2)}, u32[]{:S(2)}) async-start(bf16[16,128,128]{2,1,0:T(8,128)(2,1)} %copy-done.11), calls=%async_computation.1 | async-start | bytes 1048576 | tf_op jit(solution)/shard_map/all_to_all | solution.py:417
  49.0 2.1 %pad_maximum_fusion = (bf16[2,16,64,128]{3,2,1,0:T(8,128)(2,1)S(1)}, bf16[2,16,64,128]{3,2,1,0:T(8,128)(2,1)}) fusion(bf16[1,16,64,128]{3,2,1,0:T(8,128)(2,1)} %get-tuple-element.74, bf16[1,16,64,128]{3,2,1,0:T(8,128)(2,1)} %get-tuple-element.73, bf16[1,16,64,128]{3,2,1,0:T(8,128)(2,1)} %get-tuple-element.72, bf16[1,16,64,128]{3,2,1,0:T(8,128)(2,1)} %get-tuple-element.71), kind=kLoop, calls=%fused_computation.9 | loop fusion | flops 524288 | bytes 2097152 | tf_op jit(solution)/shard_map/stack | solution.py:463
  52.9 10.7 %all-to-all-done.1 = bf16[16,128,128]{2,1,0:T(8,128)(2,1)S(1)} async-done(((bf16[16,128,128]{2,1,0:T(8,128)(2,1)}), bf16[16,128,128]{2,1,0:T(8,128)(2,1)S(1)}, u32[]{:S(2)}, u32[]{:S(2)}) %all-to-all-start.1) | async-done | bytes 524320 | tf_op jit(solution)/shard_map/all_to_all | solution.py:417
  64.7 3.4 %copy-done.14 = bf16[2048,2048]{1,0:T(8,128)(2,1)S(1)} copy-done((bf16[2048,2048]{1,0:T(8,128)(2,1)S(1)}, bf16[2048,2048]{1,0:T(8,128)(2,1)}, u32[]{:S(2)}) %copy-start.14) | copy-done | bytes 8388632
  68.0 3.1 %segments.1 = bf16[16,144,128]{2,1,0:T(8,128)(2,1)S(1)} custom-call(s32[386]{0:T(512)S(1)} %pad_add_fusion.1.info_ref, s32[128,32]{1,0:T(8,128)S(1)} %copy.30.index_ref, bf16[2048,128]{1,0:T(8,128)(2,1)S(1)} %bitcast.42, bf16[2,16,64,128]{3,2,1,0:T(8,128)(2,1)S(1)} %get-tuple-element.88.ahead_ref, bf16[2,16,64,128]{3,2,1,0:T(8,128)(2,1)S(1)} %copy-done.12, ...), custom_call_target="tpu_custom_call" | custom-call | flops 8589934592 | bytes 12582912 | tf_op jit(solution)/shard_map/segments/pallas_call | solution.py:467
  71.1 31.9 %all_to_all.20.ret_ref = bf16[16,144,128]{2,1,0:T(8,128)(2,1)S(1)} all-to-all(bf16[16,144,128]{2,1,0:T(8,128)(2,1)S(1)} %segments.1), channel_id=1, replica_groups=mesh['slab'=16,'col'=2] {'slab'}, dimensions={0} | all-to-all | bytes 1179648 | tf_op jit(solution)/shard_map/all_to_all | solution.py:417
  103.1 1.2 %collective-permute-done.3.nbr_ref = bf16[144,128]{1,0:T(8,128)(2,1)S(1)} collective-permute-done((bf16[144,128]{1,0:T(8,128)(2,1)S(1)}, bf16[144,128]{1,0:T(8,128)(2,1)S(1)}, u32[]{:S(2)}, u32[]{:S(2)}) %collective-permute-start.3) | collective-permute-done | bytes 36896 | tf_op jit(solution)/shard_map/ppermute | solution.py:498
  104.4 6.3 %smooth_last.1 = f32[128,2048]{1,0:T(8,128)} custom-call(bf16[16,144,128]{2,1,0:T(8,128)(2,1)S(1)} %all_to_all.20.ret_ref, bf16[144,128]{1,0:T(8,128)(2,1)S(1)} %collective-permute-done.3.nbr_ref, f32[17,160,128]{2,1,0:T(8,128)S(1)} %copy-done.4, f32[17,160,128]{2,1,0:T(8,128)S(1)} %copy-done.6, f32[17,160,128]{2,1,0:T(8,128)S(1)} %copy-done.8, ...), custom_call_target="tpu_custom_call" | custom-call | flops 40000000 | bytes 8388608 | tf_op jit(solution)/shard_map/smooth_last/pallas_call | solution.py:499
  (75 shorter events, 9.0 us)
Async XLA Ops:
  0.0 4.5 %copy-start.16 = (bf16[16,64,64]{2,1,0:T(8,128)(2,1)S(1)}, bf16[16,64,64]{2,1,0:T(8,128)(2,1)}, u32[]{:S(2)}) copy-start(bf16[16,64,64]{2,1,0:T(8,128)(2,1)} %param.17) | copy-start | bytes 393220
  0.0 5.6 %copy-start.17 = (s32[128,2]{0,1:T(2,128)S(1)}, s32[128,2]{0,1:T(2,128)}, u32[]{:S(2)}) copy-start(s32[128,2]{0,1:T(2,128)} %param.15) | copy-start | bytes 3076
  1.1 7.2 %copy-start.13 = (s32[256]{0:T(256)S(1)}, s32[256]{0:T(256)}, u32[]{:S(2)}) copy-start(s32[256]{0:T(256)} %owned_ref) | copy-start | bytes 3076
  1.1 12.4 %copy-start.15 = (f32[8,2048]{1,0:T(8,128)S(1)}, f32[8,2048]{1,0:T(8,128)}, u32[]{:S(2)}) copy-start(f32[8,2048]{1,0:T(8,128)} %scale_ref.1) | copy-start | bytes 196612
  1.1 4.4 %collective-permute-start = (f32[2,128,128]{2,1,0:T(8,128)S(1)}, f32[2,128,128]{2,1,0:T(8,128)S(1)}, u32[]{:S(2)}, u32[]{:S(2)}) collective-permute-start(f32[2,128,128]{2,1,0:T(8,128)S(1)} %pad_maximum_fusion.2), channel_id=1, source_target_pairs={{0,1},{1,0},{2,3},{3,2},{4,5},{5,4},{6,7},{7,6},{8,9},{9,8},{10,11... | collective-permute-start | bytes 393224 | tf_op jit(solution)/shard_map/ppermute | solution.py:344
  5.7 22.0 %collective-permute-start.2 = (f32[8,2176]{1,0:T(8,128)S(1)}, f32[8,2176]{1,0:T(8,128)S(1)}, u32[]{:S(2)}, u32[]{:S(2)}) collective-permute-start(f32[8,2176]{1,0:T(8,128)S(1)} %get-tuple-element.78), channel_id=1, source_target_pairs={{0,2},{2,0},{4,6},{6,4},{8,10},{10,8},{12,14},{14,12},{16,18},{18,... | collective-permute-start | bytes 208904 | tf_op jit(solution)/shard_map/ppermute | solution.py:364
  12.2 15.4 %collective-permute-start.1 = (f32[8,2176]{1,0:T(8,128)S(1)}, f32[8,2176]{1,0:T(8,128)}, u32[]{:S(2)}, u32[]{:S(2)}) collective-permute-start(f32[8,2176]{1,0:T(8,128)S(1)} %get-tuple-element.77), channel_id=1, source_target_pairs={{2,4},{6,8},{10,12},{14,16},{18,20},{22,24},{26,28},{4,2},{8,6},{1... | collective-permute-start | bytes 208904 | tf_op jit(solution)/shard_map/ppermute | solution.py:365
  15.0 13.5 %copy-start.1 = (s32[128,2048]{1,0:T(8,128)S(1)}, s32[128,2048]{1,0:T(8,128)}, u32[]{:S(2)}) copy-start(s32[128,2048]{1,0:T(8,128)} %mask_ref.3) | copy-start | bytes 3145732
  15.0 13.5 %copy-start.2 = (f32[128,2048]{1,0:T(8,128)S(1)}, f32[128,2048]{1,0:T(8,128)}, u32[]{:S(2)}) copy-start(f32[128,2048]{1,0:T(8,128)} %kap_ref.1) | copy-start | bytes 3145732
  16.6 12.0 %copy-start = (f32[128,2048]{1,0:T(8,128)S(1)}, f32[128,2048]{1,0:T(8,128)}, u32[]{:S(2)}) copy-start(f32[128,2048]{1,0:T(8,128)} %dir_ref.3) | copy-start | bytes 3145732
  16.6 25.5 %all-to-all-start.2 = ((f32[48,1,2048]{2,1,0:T(1,128)}), f32[48,1,2048]{2,1,0:T(1,128)}, u32[]{:S(2)}, u32[]{:S(2)}) async-start(f32[48,1,2048]{2,1,0:T(1,128)} %outbox.1), calls=%async_computation.2 | async-start | bytes 786432 | tf_op jit(solution)/shard_map/all_to_all | solution.py:417
  36.9 1.1 copy-start.3
  38.0 1.1 copy-start.5
  40.2 1.1 %copy-start.9 = (f32[17,160,128]{2,1,0:T(8,128)}, f32[17,160,128]{2,1,0:T(8,128)S(1)}, u32[]{:S(2)}) copy-start(f32[17,160,128]{2,1,0:T(8,128)S(1)} %get-tuple-element.52.fe_ref) | copy-start | bytes 4177924
  42.1 9.0 %copy-start.20 = (pred[256]{0:T(512)(128)(4,1)S(1)}, pred[256]{0:T(512)(128)(4,1)}, u32[]{:S(2)}) copy-start(pred[256]{0:T(512)(128)(4,1)} %get-tuple-element.59) | copy-start | bytes 772
  42.1 9.6 %copy-start.18 = (s32[256]{0:T(256)S(1)}, s32[256]{0:T(256)}, u32[]{:S(2)}) copy-start(s32[256]{0:T(256)} %get-tuple-element.84) | copy-start | bytes 3076
  42.1 9.6 %copy-start.19 = (s32[256]{0:T(256)S(1)}, s32[256]{0:T(256)}, u32[]{:S(2)}) copy-start(s32[256]{0:T(256)} %get-tuple-element.87) | copy-start | bytes 3076
  42.1 21.5 %all-to-all-start.1 = ((bf16[16,128,128]{2,1,0:T(8,128)(2,1)}), bf16[16,128,128]{2,1,0:T(8,128)(2,1)S(1)}, u32[]{:S(2)}, u32[]{:S(2)}) async-start(bf16[16,128,128]{2,1,0:T(8,128)(2,1)} %copy-done.11), calls=%async_computation.1 | async-start | bytes 1048576 | tf_op jit(solution)/shard_map/all_to_all | solution.py:417
  64.7 3.4 %copy-start.14 = (bf16[2048,2048]{1,0:T(8,128)(2,1)S(1)}, bf16[2048,2048]{1,0:T(8,128)(2,1)}, u32[]{:S(2)}) copy-start(bf16[2048,2048]{1,0:T(8,128)(2,1)} %prec_ref.1) | copy-start | bytes 25165828
  68.0 36.3 %copy-start.4 = (f32[17,160,128]{2,1,0:T(8,128)S(1)}, f32[17,160,128]{2,1,0:T(8,128)}, u32[]{:S(2)}) copy-start(f32[17,160,128]{2,1,0:T(8,128)} %copy-done.3) | copy-start | bytes 4177924
  68.0 36.3 %copy-start.6 = (f32[17,160,128]{2,1,0:T(8,128)S(1)}, f32[17,160,128]{2,1,0:T(8,128)}, u32[]{:S(2)}) copy-start(f32[17,160,128]{2,1,0:T(8,128)} %copy-done.5) | copy-start | bytes 4177924
  68.0 36.3 %copy-start.8 = (f32[17,160,128]{2,1,0:T(8,128)S(1)}, f32[17,160,128]{2,1,0:T(8,128)}, u32[]{:S(2)}) copy-start(f32[17,160,128]{2,1,0:T(8,128)} %copy-done.7) | copy-start | bytes 4177924
  68.0 36.3 %copy-start.10 = (f32[17,160,128]{2,1,0:T(8,128)S(1)}, f32[17,160,128]{2,1,0:T(8,128)}, u32[]{:S(2)}) copy-start(f32[17,160,128]{2,1,0:T(8,128)} %copy-done.9) | copy-start | bytes 4177924
  103.1 1.3 %collective-permute-start.3 = (bf16[144,128]{1,0:T(8,128)(2,1)S(1)}, bf16[144,128]{1,0:T(8,128)(2,1)S(1)}, u32[]{:S(2)}, u32[]{:S(2)}) collective-permute-start(bf16[144,128]{1,0:T(8,128)(2,1)S(1)} %fusion.5), channel_id=1, source_target_pairs={{0,1},{1,0},{2,3},{3,2},{4,5},{5,4},{6,7},{7,6},{8,9},{9,8},{10,11... | collective-permute-start | bytes 110600 | tf_op jit(solution)/shard_map/ppermute | solution.py:498
  (3 other events, 2.9 us)
where the time goes:
time: 112 us; the launch traced here: 111 us
  blocking collectives  31.9 us (28%)
  starting transfers between devices  19.6 us (18%)
  Pallas kernels  19.2 us (17%)
  local copies, waits for them, and re-layouts  17.9 us (16%)
  waiting for transfers between devices  11.9 us (11%)
  other arithmetic  9.28 us (8%)
    all_to_all x1, blocking collectives, swap(): lax.all_to_all(array, 'slab', split_axis=0, concat_axis=0, tiled=True, ax...  31.9 us
    all_to_all x2, starting transfers between devices, swap(): lax.all_to_all(array, 'slab', split_axis=0, concat_axis=0, tiled=True, ax...  15.1 us
    unnamed x44, local copies, waits for them, and re-layouts  12.3 us
    all_to_all x2, waiting for transfers between devices, swap(): lax.all_to_all(array, 'slab', split_axis=0, concat_axis=0, tiled=True, ax...  10.7 us
    pallas_call x1, Pallas kernels, per_device(): pl.pallas_call(smooth_first_kernel, out_shape=(jax.ShapeDtypeStruct((col_...  8.29 us
    pallas_call x1, Pallas kernels, per_device(): pl.pallas_call(smooth_last_kernel, out_shape=jax.ShapeDtypeStruct((rows_d...  6.31 us
    pallas_call x1, Pallas kernels, per_device(): pl.pallas_call(functools.partial(segments_kernel, width=width, batch=batc...  3.07 us
    another operation x2, local copies, waits for them, and re-layouts, sides(): jnp.stack([jnp.concatenate([table, empty], axis=2), jnp.concatenate([empt...  3.01 us
  transfers between devices with their start and end apart: 6, of which 2 were waited for; matrix products, arithmetic and copies ran while one was open for 15% of the time, Pallas kernels for 9%

commit v1 on v0

--- a/solution.py
+++ b/solution.py
@@ -7,6 +7,7 @@
 from jax.experimental.pallas import tpu as pltpu
 from jax.sharding import PartitionSpec as P
 
+
 TILE_C = 128
 SWEEPS = 4
 HALO = 8
@@ -36,7 +37,7 @@
     return jnp.where((own > 0) & (other > 0), 0.5 * (own + other), 0.0)
 
 
-def sweeps(tiles, rows, bufs, own_ref, fn_ref, fw_ref, fe_ref, finish):
+def sweeps(tiles, rows, bufs, own_ref, fn_ref, fw_ref, fe_ref, finish, half_done=None):
     for step in range(SWEEPS):
         src, dst = bufs[step % 2], bufs[1 - step % 2]
         last = step == SWEEPS - 1
@@ -68,48 +69,52 @@
             carry = lax.fori_loop(0, tiles - 1, step_tile, carry, unroll=4)
             if not last:
                 tile(tiles - 1, 0, *carry)
+            elif half_done is not None:
+                half_done(start - PAD, length)
 
 
 def smooth_first_kernel(
-    dir_ref, kap_ref, mask_ref, nbr_ref, top_ref, bot_ref,
-    out_ref, own_ref, fn_ref, fw_ref, fe_ref, u0, u1, kbuf,
+    dir_ref, kap_ref, mask_ref, nbr_ref, got_a_ref, got_b_ref,
+    out_ref, own_out, fn_out, fw_out, fe_out,
+    done, own_ref, fn_ref, fw_ref, fe_ref, u0, u1, kbuf, sems,
 ):
-    tiles, height, lanes = u0.shape
+    tiles, _, lanes = u0.shape
     own = dir_ref.shape[0]
     rows = own + 2 * HALO
     edge = (HALO, lanes)
     zero = jnp.zeros(edge, jnp.float32)
-
-    def halos(c):
-        cols = pl.ds(pl.multiple_of(c * lanes, lanes), lanes)
-        low = row_iota(edge) < HALO // 2
-        top = top_ref[:, cols]
-        bot = bot_ref[:, cols]
-        u0[c, pl.ds(0, HALO), :] = zero
-        u1[c, pl.ds(0, HALO), :] = zero
-        kbuf[c, pl.ds(0, HALO), :] = zero
-        u0[c, pl.ds(HALO, HALO), :] = jnp.where(low, 0.0, pltpu.roll(top, HALO // 2, 0))
-        kbuf[c, pl.ds(HALO, HALO), :] = jnp.where(low, 0.0, top)
-        u0[c, pl.ds(PAD + own, HALO), :] = jnp.where(low, bot, 0.0)
-        kbuf[c, pl.ds(PAD + own, HALO), :] = jnp.where(low, pltpu.roll(bot, HALO // 2, 0), 0.0)
-        end = pl.ds(PAD + own + HALO, HALO)
-        u0[c, end, :] = zero
-        u1[c, end, :] = zero
-        kbuf[c, end, :] = zero
-        fn_ref[c, end, :] = zero
+    even = lax.rem(lax.axis_index("slab"), 2) == 0
+    low = row_iota(edge) < HALO // 2
+
+    def ends(c):
+        for part in (pl.ds(0, HALO), pl.ds(PAD + own + HALO, HALO)):
+            u0[c, part, :] = zero
+            u1[c, part, :] = zero
+            kbuf[c, part, :] = zero
+        fn_ref[c, pl.ds(PAD + own + HALO, HALO), :] = zero
 
     def fill(c, carry):
         cols = pl.ds(pl.multiple_of(c * lanes, lanes), lanes)
         maskf = mask_ref[:, cols].astype(jnp.float32)
         u0[c, pl.ds(PAD, own), :] = dir_ref[:, cols] * maskf
         kbuf[c, pl.ds(PAD, own), :] = kap_ref[:, cols] * maskf
-        halos(c)
+        got_a, got_b = got_a_ref[:, cols], got_b_ref[:, cols]
+        top = jnp.where(even, got_b, got_a)
+        bot = jnp.where(even, got_a, got_b)
+        u0[c, pl.ds(HALO, HALO), :] = jnp.where(low, 0.0, pltpu.roll(top, HALO // 2, 0))
+        kbuf[c, pl.ds(HALO, HALO), :] = jnp.where(low, 0.0, top)
+        u0[c, pl.ds(PAD + own, HALO), :] = jnp.where(low, bot, 0.0)
+        kbuf[c, pl.ds(PAD + own, HALO), :] = jnp.where(low, pltpu.roll(bot, HALO // 2, 0), 0.0)
+        ends(c)
         return carry
 
     lax.fori_loop(0, tiles - 1, fill, 0)
-    u0[tiles - 1, pl.ds(PAD, own), :] = nbr_ref[0]
-    kbuf[tiles - 1, pl.ds(PAD, own), :] = nbr_ref[1]
-    halos(tiles - 1)
+    body = pl.ds(HALO, rows)
+    lane = lane_iota((rows, lanes))
+    near = jnp.where(lax.axis_index("col") == 0, lanes - 1 - lane, lane) >= lanes - SWEEPS
+    u0[tiles - 1, body, :] = nbr_ref[0]
+    kbuf[tiles - 1, body, :] = jnp.where(near, nbr_ref[1], 0.0)
+    ends(tiles - 1)
 
     def faces(c, right, k_left, k):
         body = pl.ds(HALO, rows)
@@ -128,17 +133,35 @@
     carry = kbuf[tiles - 1, body, :], kbuf[0, body, :]
     carry = lax.fori_loop(0, tiles - 1, lambda c, carry: faces(c, c + 1, *carry), carry)
     faces(tiles - 1, 0, *carry)
+    copies = [
+        pltpu.make_async_copy(ref, out, sems.at[i])
+        for i, (ref, out) in enumerate(
+            ((own_ref, own_out), (fn_ref, fn_out), (fw_ref, fw_out), (fe_ref, fe_out))
+        )
+    ]
+    for copy in copies:
+        copy.start()
 
     def finish(c, row, value):
-        out_ref[c, pl.ds(row, value.shape[0]), :] = value.astype(jnp.bfloat16)
-
-    sweeps(tiles, rows, (u0, u1), own_ref, fn_ref, fw_ref, fe_ref, finish)
+        done[c, pl.ds(row, value.shape[0]), :] = value.astype(jnp.bfloat16)
+
+    def half_done(row, length):
+        part = pl.ds(row, length)
+        copy = pltpu.make_async_copy(
+            done.at[:, part, :], out_ref.at[:, part, :], sems.at[len(copies)]
+        )
+        copies.append(copy)
+        copy.start()
+
+    sweeps(tiles, rows, (u0, u1), own_ref, fn_ref, fw_ref, fe_ref, finish, half_done)
+    for copy in copies:
+        copy.wait()
 
 
 def smooth_last_kernel(
     ret_ref, nbr_ref, own_ref, fn_ref, fw_ref, fe_ref, dir_ref, mask_ref, out_ref, u0, u1
 ):
-    tiles, height, lanes = u0.shape
+    tiles, _, lanes = u0.shape
     own = dir_ref.shape[0]
     rows = own + 2 * HALO
     zero = jnp.zeros((HALO, lanes), jnp.float32)
@@ -187,15 +210,15 @@
 
 
 def segments_kernel(
-    info_ref, index_ref, x_ref, ahead_ref, behind_ref, prec_ref, few_ref, all_ref,
-    out_ref, turned, weighted, zbuf, scale_row, adj, grid, scale_sem, *, width, batch,
+    info_ref, index_ref, x_ref, ahead_ref, behind_ref, prec_in, few_ref, all_ref,
+    out_ref, prec_ref, turned, weighted, zbuf, scale_row, adj, grid, prec_sem, scale_sem,
+    *, width, batch,
 ):
     parts, chunk, lanes = out_ref.shape
     order = prec_ref.shape[0]
     blocks = order // lanes
     count = info_ref[0]
     full = info_ref[1]
-    groups = (count + batch - 1) // batch
 
     def scale_copy(source, row, slot, j):
         return pltpu.make_async_copy(source.at[row], scale_row.at[slot, j], scale_sem.at[slot, j])
@@ -212,7 +235,13 @@
             def _(e=e, j=j):
                 scale_copy(all_ref, info_ref[4 + 3 * e], slot, j).start()
 
+    def prec_copy(i):
+        cols = pl.ds(i * width, width)
+        return pltpu.make_async_copy(prec_in.at[:, cols], prec_ref.at[:, cols], prec_sem.at[i])
+
     fetch(0, 0)
+    for i in range(order // width):
+        prec_copy(i).start()
 
     def turn(q, carry):
         part = pl.ds(pl.multiple_of(q * lanes, lanes), lanes)
@@ -251,6 +280,11 @@
 
         for i in range(order // width):
             cols = pl.ds(i * width, width)
+
+            @pl.when(g == 0)
+            def _(i=i):
+                prec_copy(i).wait()
+
             prod = jnp.dot(
                 weighted[: size * lanes, :], prec_ref[:, cols],
                 preferred_element_type=jnp.float32,
@@ -281,6 +315,11 @@
         def _(size=size):
             work(count // batch, size)
 
+    @pl.when(count == 0)
+    def _():
+        for i in range(order // width):
+            prec_copy(i).wait()
+
     zero = jnp.zeros((HALO, lanes), jnp.float32)
     grid[pl.ds(0, HALO), :] = zero
     grid[pl.ds(order + HALO, HALO), :] = zero
@@ -304,71 +343,18 @@
     return pl.BlockSpec(memory_space=pltpu.VMEM)
 
 
-def any_spec():
-    return pl.BlockSpec(memory_space=pl.ANY)
+def hbm_spec():
+    return pl.BlockSpec(memory_space=pltpu.HBM)
 
 
 def smem_spec():
     return pl.BlockSpec(memory_space=pltpu.SMEM)
 
 
-def per_device(
-    direction, kappa, land_mask, owned_segments, seg_anchor,
-    interp_index, interp_table, precision, obs_scale,
+def owner_tables(
+    owned_segments, seg_anchor, seg_tiles, seg_max, dev_count, col_count, span, col_tiles, my_device
 ):
-    rows_dev, cols_dev = direction.shape
-    blocks, tile_r, _ = interp_table.shape
-    order = precision.shape[0]
-    segs, seg_tiles = interp_index.shape
-    seg_max = obs_scale.shape[0]
-    lanes = TILE_C
-    col_tiles = cols_dev // lanes
-    slab_count = lax.axis_size("slab")
-    col_count = lax.axis_size("col")
-    dev_count = slab_count * col_count
-    span = order // rows_dev
-    assert span == col_tiles and col_count == 2 and slab_count % span == 0
-    groups = [list(range(i, i + span)) for i in range(0, slab_count, span)]
-    if len(groups) == 1:
-        groups = None
-    my_slab = lax.axis_index("slab")
-    my_col = lax.axis_index("col")
-    my_device = my_slab * col_count + my_col
-    is_low = my_col == 0
-
-    def edge_cols(array):
-        return jnp.where(is_low, array[:, cols_dev - lanes :], array[:, :lanes])
-
-    edge_mask = edge_cols(land_mask).astype(jnp.float32)
-    edge = jnp.stack([edge_cols(direction) * edge_mask, edge_cols(kappa) * edge_mask])
-    nbr = lax.ppermute(edge, "col", [(0, 1), (1, 0)])
-    near = jnp.where(
-        is_low, lane_iota((1, lanes)) < SWEEPS, lane_iota((1, lanes)) >= lanes - SWEEPS
-    )
-    nbr = jnp.where(near[None], nbr, 0.0)
-
-    def edge_rows(start):
-        part = slice(start, start + SWEEPS)
-        maskf = land_mask[part].astype(jnp.float32)
-        field = jnp.concatenate([direction[part] * maskf, nbr[0, part]], axis=1)
-        coeff = jnp.concatenate([kappa[part] * maskf, nbr[1, part]], axis=1)
-        return jnp.concatenate([field, coeff], axis=0)
-
-    first_rows, last_rows = edge_rows(0), edge_rows(rows_dev - SWEEPS)
-    even = my_slab % 2 == 0
-    pairs_a = [(i, i ^ 1) for i in range(slab_count)]
-    pairs_b = [(i, i + 1) for i in range(1, slab_count - 1, 2)]
-    pairs_b = pairs_b + [(j, i) for i, j in pairs_b]
-    send_a = jnp.where(even, last_rows, first_rows)
-    send_b = jnp.where(even, first_rows, last_rows)
-    got_a = lax.ppermute(send_a, "slab", pairs_a)
-    got_b = lax.ppermute(send_b, "slab", pairs_b)
-    owned_segments, seg_anchor, send_a = lax.optimization_barrier(
-        (owned_segments, seg_anchor, send_a)
-    )
-    top = jnp.where(even, got_b, got_a)
-    bot = jnp.where(even, got_a, got_b)
-
+    segs = seg_anchor.shape[0]
     slots = dev_count * seg_max
     slot_ids = jnp.arange(slots, dtype=jnp.int32)
     used = owned_segments >= 0
@@ -401,38 +387,85 @@
     info = jnp.concatenate(
         [count[None], overflow.astype(jnp.int32)[None], listed.reshape(-1)]
     )
-
-    my_owner = lax.dynamic_slice_in_dim(owner_slab, my_device * seg_max, seg_max)
-    my_used = lax.dynamic_slice_in_dim(used, my_device * seg_max, seg_max)
-
-    def outbox(cap, position):
-        target = jnp.arange(slab_count * cap, dtype=jnp.int32)
-        hit = (
-            (my_owner * cap + position)[None, :] == target[:, None]
-        ) & (my_used & (position < cap))[None, :]
-        slot = jnp.sum(jnp.where(hit, slot_in[None, :], 0), axis=1)
-        return obs_scale[slot].reshape(slab_count * cap, 1, order)
+    return info, overflow, owner_slab, used, slot_in
+
+
+def sides(table):
+    empty = jnp.zeros_like(table)
+    return jnp.stack(
+        [jnp.concatenate([table, empty], axis=2), jnp.concatenate([empty, table], axis=2)]
+    )
+
+
+def per_device(
+    direction, kappa, land_mask, owned_segments, seg_anchor,
+    interp_index, interp_table, precision, obs_scale,
+):
+    rows_dev, cols_dev = direction.shape
+    order = precision.shape[0]
+    _, seg_tiles = interp_index.shape
+    seg_max = obs_scale.shape[0]
+    lanes = TILE_C
+    col_tiles = cols_dev // lanes
+    slab_count = lax.axis_size("slab")
+    col_count = lax.axis_size("col")
+    dev_count = slab_count * col_count
+    span = order // rows_dev
+    assert span == col_tiles and col_count == 2 and slab_count % span == 0
+    groups = [list(range(i, i + span)) for i in range(0, slab_count, span)]
+    if len(groups) == 1:
+        groups = None
+    my_slab = lax.axis_index("slab")
+    my_col = lax.axis_index("col")
+    my_device = my_slab * col_count + my_col
+    is_low = my_col == 0
+
+    def edge_rows(start):
+        part = slice(start, start + SWEEPS)
+        maskf = land_mask[part].astype(jnp.float32)
+        return jnp.concatenate([direction[part] * maskf, kappa[part] * maskf], axis=0)
+
+    first_rows, last_rows = edge_rows(0), edge_rows(rows_dev - SWEEPS)
+    even = my_slab % 2 == 0
+    pairs_a = [(i, i ^ 1) for i in range(slab_count)]
+    pairs_b = [(i, i + 1) for i in range(1, slab_count - 1, 2)]
+    pairs_b = pairs_b + [(j, i) for i, j in pairs_b]
+    send_a = jnp.where(even, last_rows, first_rows)
+    send_b = jnp.where(even, first_rows, last_rows)
+    got_b = lax.ppermute(send_b, "slab", pairs_b)
+    got_a = lax.ppermute(send_a, "slab", pairs_a)
 
     def swap(array, groups=None):
         return lax.all_to_all(
             array, "slab", split_axis=0, concat_axis=0, tiled=True, axis_index_groups=groups
         )
 
-    few = swap(
-        pl.pallas_call(
-            functools.partial(outbox_kernel, seg_tiles=seg_tiles, col_tiles=col_tiles, span=span),
-            out_shape=jax.ShapeDtypeStruct((slab_count * CAP, 1, order), jnp.float32),
-            in_specs=[smem_spec(), smem_spec(), vmem_spec()],
-            out_specs=vmem_spec(),
-            compiler_params=pltpu.CompilerParams(vmem_limit_bytes=2 << 20),
-            name="outbox",
-        )(owned_segments, seg_anchor.reshape(-1), obs_scale)
-    )
-    everything = lax.cond(
-        overflow,
-        lambda: swap(outbox(seg_max, slot_in)),
-        lambda: jnp.zeros((slab_count * seg_max, 1, order), jnp.float32),
-    )
+    scales_out = pl.pallas_call(
+        functools.partial(outbox_kernel, seg_tiles=seg_tiles, col_tiles=col_tiles, span=span),
+        out_shape=jax.ShapeDtypeStruct((slab_count * CAP, 1, order), jnp.float32),
+        in_specs=[smem_spec(), smem_spec(), vmem_spec()],
+        out_specs=vmem_spec(),
+        compiler_params=pltpu.CompilerParams(vmem_limit_bytes=2 << 20),
+        name="outbox",
+    )(owned_segments, seg_anchor.reshape(-1), obs_scale)
+    few = swap(scales_out)
+
+    def edge_cols(array):
+        return jnp.where(is_low, array[:, cols_dev - lanes :], array[:, :lanes])
+
+    edge_mask = edge_cols(land_mask).astype(jnp.float32)
+    above = edge_cols(jnp.where(even, got_b, got_a))
+    below = edge_cols(jnp.where(even, got_a, got_b))
+    blank = jnp.zeros((HALO - SWEEPS, lanes), jnp.float32)
+
+    def with_halo(array, part):
+        return jnp.concatenate([blank, above[part], array, below[part], blank], axis=0)
+
+    edge = jnp.stack([
+        with_halo(edge_cols(direction) * edge_mask, slice(0, SWEEPS)),
+        with_halo(edge_cols(kappa) * edge_mask, slice(SWEEPS, 2 * SWEEPS)),
+    ])
+    nbr = lax.ppermute(edge, "col", [(0, 1), (1, 0)])
 
     tiles = col_tiles + 1
     height = rows_dev + 2 * PAD
@@ -445,48 +478,79 @@
             face_shape, face_shape, face_shape, face_shape,
         ),
         in_specs=[vmem_spec()] * 6,
-        out_specs=(vmem_spec(),) * 5,
-        scratch_shapes=[buf, buf, buf],
-        compiler_params=pltpu.CompilerParams(vmem_limit_bytes=vmem_need(8 * tiles * height)),
+        out_specs=(hbm_spec(),) * 5,
+        scratch_shapes=[pltpu.VMEM((col_tiles, rows_dev, lanes), jnp.bfloat16)]
+        + [buf] * 7
+        + [pltpu.SemaphoreType.DMA((6,))],
         cost_estimate=pl.CostEstimate(flops=40000000, bytes_accessed=8 << 20, transcendentals=0),
         name="smooth_first",
-    )(direction, kappa, land_mask, nbr, top, bot)
-
+    )(direction, kappa, land_mask, nbr, got_a, got_b)
+
+    smoothed, owned_segments, seg_anchor, interp_index, interp_table, obs_scale = (
+        lax.optimization_barrier(
+            (smoothed, owned_segments, seg_anchor, interp_index, interp_table, obs_scale)
+        )
+    )
     gathered = swap(smoothed, groups)
+
+    info, overflow, owner_slab, used, slot_in = owner_tables(
+        owned_segments, seg_anchor, seg_tiles, seg_max, dev_count, col_count, span,
+        col_tiles, my_device,
+    )
+    ahead, behind = sides(interp_table.transpose(0, 2, 1)), sides(interp_table)
+
+    my_owner = lax.dynamic_slice_in_dim(owner_slab, my_device * seg_max, seg_max)
+    my_used = lax.dynamic_slice_in_dim(used, my_device * seg_max, seg_max)
+
+    def outbox(cap, position):
+        target = jnp.arange(slab_count * cap, dtype=jnp.int32)
+        hit = (
+            (my_owner * cap + position)[None, :] == target[:, None]
+        ) & (my_used & (position < cap))[None, :]
+        slot = jnp.sum(jnp.where(hit, slot_in[None, :], 0), axis=1)
+        return obs_scale[slot].reshape(slab_count * cap, 1, order)
+
+    many = (slab_count * seg_max, 1, order)
+    overflow = overflow & (gathered[0, 0, 0] < jnp.inf)
+    everything = lax.cond(
+        overflow,
+        lambda: swap(outbox(seg_max, slot_in)),
+        lambda: pl.pallas_call(
+            lambda out_ref: None,
+            out_shape=jax.ShapeDtypeStruct(many, jnp.float32),
+            out_specs=hbm_spec(),
+            name="unread",
+        )(),
+    )
 
     chunk = rows_dev + 2 * HALO
     width = min(512, order)
     batch = 4
 
-    def sides(table):
-        empty = jnp.zeros_like(table)
-        return jnp.stack(
-            [jnp.concatenate([table, empty], axis=2), jnp.concatenate([empty, table], axis=2)]
-        )
-
     returning = pl.pallas_call(
         functools.partial(segments_kernel, width=width, batch=batch),
         out_shape=jax.ShapeDtypeStruct((span, chunk, lanes), jnp.bfloat16),
-        in_specs=[smem_spec(), smem_spec(), vmem_spec(), vmem_spec(), vmem_spec(), vmem_spec()]
-        + [any_spec()] * 2,
+        in_specs=[smem_spec(), smem_spec(), vmem_spec(), vmem_spec(), vmem_spec()]
+        + [hbm_spec()] * 3,
         out_specs=vmem_spec(),
         scratch_shapes=[
+            pltpu.VMEM((order, order), jnp.bfloat16),
             pltpu.VMEM((lanes, order), jnp.bfloat16),
             pltpu.VMEM((batch * lanes, order), jnp.bfloat16),
             pltpu.VMEM((batch * lanes, order), jnp.bfloat16),
             pltpu.VMEM((2, batch, 1, order), jnp.float32),
             pltpu.VMEM((lanes, order), jnp.float32),
             pltpu.VMEM((order + 2 * HALO, lanes), jnp.float32),
+            pltpu.SemaphoreType.DMA((order // width,)),
             pltpu.SemaphoreType.DMA((2, batch)),
         ],
-        compiler_params=pltpu.CompilerParams(vmem_limit_bytes=vmem_need(order * order // 256)),
         cost_estimate=pl.CostEstimate(
             flops=8 * 2 * order * order * lanes, bytes_accessed=12 << 20, transcendentals=0
         ),
         name="segments",
     )(
         info, interp_index, gathered.reshape(order, lanes),
-        sides(interp_table.transpose(0, 2, 1)), sides(interp_table), precision, few, everything,
+        ahead, behind, precision, few, everything,
     )
 
     returned = swap(returning, groups)
@@ -534,6 +598,7 @@
         P(),
         P(("slab", "col"), None),
     )
+
     return jax.shard_map(
         per_device, mesh=mesh, in_specs=in_specs, out_specs=P("slab", "col"), check_vma=False
     )

time: 112 us -> 113 us (level)
  Pallas kernels: 19.2 us -> 30 us
  waiting for transfers between devices: 11.9 us -> 22.4 us
  local copies, waits for them, and re-layouts: 17.9 us -> 8.42 us
  blocking collectives: 31.9 us -> 25.5 us
  starting transfers between devices: 19.6 us -> 16.8 us
  other arithmetic: 9.28 us -> 7.56 us
    pallas_call x1, Pallas kernels: 3.07 us -> 11.9 us  [per_device(): pl.pallas_call(functools.partial(segments_kernel, width=width, batch=batc...]
    all_to_all x2, waiting for transfers between devices: 10.7 us -> 19.1 us  [swap(): lax.all_to_all(array, 'slab', split_axis=0, concat_axis=0, tiled=True, ax...]
    unnamed x44 -> x33, local copies, waits for them, and re-layouts: 12.3 us -> 5.6 us
    all_to_all x1, blocking collectives: 31.9 us -> 25.5 us  [swap(): lax.all_to_all(array, 'slab', split_axis=0, concat_axis=0, tiled=True, ax...]
    all_to_all x2, starting transfers between devices: 15.1 us -> 10.2 us  [swap(): lax.all_to_all(array, 'slab', split_axis=0, concat_axis=0, tiled=True, ax...]
    ppermute x1, starting transfers between devices: 2.56 us -> 5.79 us  [per_device(): got_a = lax.ppermute(send_a, 'slab', pairs_a)]
    another operation x2, local copies, waits for them, and re-layouts: 3.01 us -> 0.32 us  [sides(): jnp.stack([jnp.concatenate([table, empty], axis=2), jnp.concatenate([empt...]
    ppermute x1, waiting for transfers between devices: 0.01 us -> 2.07 us  [per_device(): got_a = lax.ppermute(send_a, 'slab', pairs_a)]
  transfers between devices with their start and end apart: 6 -> 6, of which waited for: 2 -> 4; matrix products, arithmetic and copies ran while one was open for 15% -> 8% of each run, Pallas kernels for 9% -> 1%
where the time goes in v1:
time: 113 us; the launch traced here: 112 us
  Pallas kernels  30 us (27%)
  blocking collectives  25.5 us (23%)
  waiting for transfers between devices  22.4 us (20%)
  starting transfers between devices  16.8 us (15%)
  local copies, waits for them, and re-layouts  8.42 us (7%)
  other arithmetic  7.56 us (7%)
  between operations  1.69 us (1%)
    all_to_all x1, blocking collectives, swap(): lax.all_to_all(array, 'slab', split_axis=0, concat_axis=0, tiled=True, ax...  25.5 us
    all_to_all x2, waiting for transfers between devices, swap(): lax.all_to_all(array, 'slab', split_axis=0, concat_axis=0, tiled=True, ax...  19.1 us
    pallas_call x1, Pallas kernels, per_device(): pl.pallas_call(functools.partial(segments_kernel, width=width, batch=batc...  11.9 us
    pallas_call x1, Pallas kernels, per_device(): pl.pallas_call(smooth_first_kernel, out_shape=(jax.ShapeDtypeStruct((col_...  10.3 us
    all_to_all x2, starting transfers between devices, swap(): lax.all_to_all(array, 'slab', split_axis=0, concat_axis=0, tiled=True, ax...  10.2 us
    pallas_call x1, Pallas kernels, per_device(): pl.pallas_call(smooth_last_kernel, out_shape=jax.ShapeDtypeStruct((rows_d...  6.28 us
    ppermute x1, starting transfers between devices, per_device(): got_a = lax.ppermute(send_a, 'slab', pairs_a)  5.79 us
    unnamed x33, local copies, waits for them, and re-layouts  5.6 us
  transfers between devices with their start and end apart: 6, of which 4 were waited for; matrix products, arithmetic and copies ran while one was open for 8% of the time, Pallas kernels for 1%

profile of v1, /device:TPU:0, one launch (start us, length us, event | category | flops | bytes accessed | tf_op | source)
XLA Modules:
  0.0 112.3 jit_solution(11607476749105683232)
XLA Ops:
  0.0 1.1 convert_multiply_fusion.2
  1.8 5.8 %collective-permute-start.1 = (f32[8,2048]{1,0:T(8,128)S(1)}, f32[8,2048]{1,0:T(8,128)S(1)}, u32[]{:S(2)}, u32[]{:S(2)}) collective-permute-start(f32[8,2048]{1,0:T(8,128)S(1)} %get-tuple-element.85), channel_id=1, source_target_pairs={{0,2},{2,0},{4,6},{6,4},{8,10},{10,8},{12,14},{14,12},{16,18},{18,... | collective-permute-start | bytes 196616 | tf_op jit(solution)/shard_map/ppermute | solution.py:436
  7.6 1.0 convert_multiply_fusion
  8.6 2.1 %collective-permute-done.1.got_a_ref = f32[8,2048]{1,0:T(8,128)S(1)} collective-permute-done((f32[8,2048]{1,0:T(8,128)S(1)}, f32[8,2048]{1,0:T(8,128)S(1)}, u32[]{:S(2)}, u32[]{:S(2)}) %collective-permute-start.1) | collective-permute-done | bytes 65568 | tf_op jit(solution)/shard_map/ppermute | solution.py:436
  11.2 1.5 %outbox.1 = f32[48,1,2048]{2,1,0:T(1,128)} custom-call(s32[256]{0:T(256)S(1)} %copy-done.6, s32[256]{0:T(256)S(1)} %reshape.117.anchor_ref, f32[8,2048]{1,0:T(8,128)S(1)} %copy-done.7), custom_call_target="tpu_custom_call" | custom-call | tf_op jit(solution)/shard_map/outbox/pallas_call | solution.py:443
  13.4 10.3 %smooth_first.1 = (bf16[16,128,128]{2,1,0:T(8,128)(2,1)}, f32[17,160,128]{2,1,0:T(8,128)}, f32[17,160,128]{2,1,0:T(8,128)}, f32[17,160,128]{2,1,0:T(8,128)}, f32[17,160,128]{2,1,0:T(8,128)}) custom-call(f32[128,2048]{1,0:T(8,128)} %dir_ref.3, f32[128,2048]{1,0:T(8,128)} %kap_ref.1, s32[128,2048]{1,0:T(8,128)} %mask_ref.3, f32[2,144,128]{2,1,0:T(8,128)} %copy-done.13, ...), custom_call_target="tpu_custom_call" | custom-call | flops 40000000 | bytes 8388608 | tf_op jit(solution)/shard_map/smooth_first/pallas_call | solution.py:474
  23.7 5.9 %all-to-all-start.1 = ((bf16[16,128,128]{2,1,0:T(8,128)(2,1)}), bf16[16,128,128]{2,1,0:T(8,128)(2,1)S(1)}, u32[]{:S(2)}, u32[]{:S(2)}) async-start(bf16[16,128,128]{2,1,0:T(8,128)(2,1)} %get-tuple-element.54), calls=%async_computation.1 | async-start | bytes 1048576 | tf_op jit(solution)/shard_map/all_to_all | solution.py:439
  29.8 0.7 convert_reduce_fusion.1
  31.0 0.7 select_reduce_fusion.6
  32.4 12.7 %all-to-all-done.1 = bf16[16,128,128]{2,1,0:T(8,128)(2,1)S(1)} async-done(((bf16[16,128,128]{2,1,0:T(8,128)(2,1)}), bf16[16,128,128]{2,1,0:T(8,128)(2,1)S(1)}, u32[]{:S(2)}, u32[]{:S(2)}) %all-to-all-start.1) | async-done | bytes 524320 | tf_op jit(solution)/shard_map/all_to_all | solution.py:439
  46.3 4.3 %all-to-all-start.2 = ((f32[48,1,2048]{2,1,0:T(1,128)}), f32[48,1,2048]{2,1,0:T(1,128)S(1)}, u32[]{:S(2)}, u32[]{:S(2)}) async-start(f32[48,1,2048]{2,1,0:T(1,128)} %outbox.1), calls=%async_computation.2 | async-start | bytes 786432 | tf_op jit(solution)/shard_map/all_to_all | solution.py:439
  52.0 0.7 copy.32.index_ref
  52.7 1.3 %pad_add_fusion.1.info_ref = s32[386]{0:T(512)} fusion(s32[384]{0:T(512)S(1)} %reshape.115, s32[1]{0:T(128)} %bitcast.8, s32[1]{0:T(128)} %bitcast.7), kind=kLoop, calls=%fused_computation.44 | loop fusion | flops 772 | bytes 3088 | tf_op jit(solution)/shard_map/concatenate | solution.py:387
  54.4 0.9 pad_maximum_fusion.1.behind_ref
  55.2 0.9 pad_maximum_fusion.ahead_ref
  56.1 6.4 %all-to-all-done.2.few_ref = f32[48,1,2048]{2,1,0:T(1,128)S(1)} async-done(((f32[48,1,2048]{2,1,0:T(1,128)}), f32[48,1,2048]{2,1,0:T(1,128)S(1)}, u32[]{:S(2)}, u32[]{:S(2)}) %all-to-all-start.2) | async-done | bytes 393248 | tf_op jit(solution)/shard_map/all_to_all | solution.py:439
  62.5 0.7 copy-done.10
  63.3 11.9 %segments.1 = bf16[16,144,128]{2,1,0:T(8,128)(2,1)} custom-call(s32[386]{0:T(512)} %pad_add_fusion.1.info_ref, s32[128,32]{1,0:T(8,128)} %copy.32.index_ref, bf16[2048,128]{1,0:T(8,128)(2,1)} %bitcast.35, bf16[2,16,64,128]{3,2,1,0:T(8,128)(2,1)} %pad_maximum_fusion.ahead_ref, bf16[2,16,64,128]{3,2,1,0:T(8,128)(2,1)} %pad_maximum_fusion.1.behind_ref, ...), custom_call_target="tpu_custom_call" | custom-call | flops 8589934592 | bytes 12582912 | tf_op jit(solution)/shard_map/segments/pallas_call | solution.py:530
  75.2 25.5 %all_to_all.20.ret_ref = bf16[16,144,128]{2,1,0:T(8,128)(2,1)S(1)} all-to-all(bf16[16,144,128]{2,1,0:T(8,128)(2,1)} %segments.1), channel_id=1, replica_groups=mesh['slab'=16,'col'=2] {'slab'}, dimensions={0} | all-to-all | bytes 1179648 | tf_op jit(solution)/shard_map/all_to_all | solution.py:439
  100.8 1.2 %collective-permute-done.3.nbr_ref = bf16[144,128]{1,0:T(8,128)(2,1)S(1)} collective-permute-done((bf16[144,128]{1,0:T(8,128)(2,1)S(1)}, bf16[144,128]{1,0:T(8,128)(2,1)S(1)}, u32[]{:S(2)}, u32[]{:S(2)}) %collective-permute-start.3) | collective-permute-done | bytes 36896 | tf_op jit(solution)/shard_map/ppermute | solution.py:562
  102.0 1.3 %copy-done.3 = f32[17,160,128]{2,1,0:T(8,128)S(1)} copy-done((f32[17,160,128]{2,1,0:T(8,128)S(1)}, f32[17,160,128]{2,1,0:T(8,128)}, u32[]{:S(2)}) %copy-start.3) | copy-done | bytes 1392664
  103.3 1.3 %copy-done.4 = f32[17,160,128]{2,1,0:T(8,128)S(1)} copy-done((f32[17,160,128]{2,1,0:T(8,128)S(1)}, f32[17,160,128]{2,1,0:T(8,128)}, u32[]{:S(2)}) %copy-start.4) | copy-done | bytes 1392664
  104.7 1.3 %copy-done.5 = f32[17,160,128]{2,1,0:T(8,128)S(1)} copy-done((f32[17,160,128]{2,1,0:T(8,128)S(1)}, f32[17,160,128]{2,1,0:T(8,128)}, u32[]{:S(2)}) %copy-start.5) | copy-done | bytes 1392664
  106.0 6.3 %smooth_last.1 = f32[128,2048]{1,0:T(8,128)} custom-call(bf16[16,144,128]{2,1,0:T(8,128)(2,1)S(1)} %all_to_all.20.ret_ref, bf16[144,128]{1,0:T(8,128)(2,1)S(1)} %collective-permute-done.3.nbr_ref, f32[17,160,128]{2,1,0:T(8,128)S(1)} %copy-done.2, f32[17,160,128]{2,1,0:T(8,128)S(1)} %copy-done.3, f32[17,160,128]{2,1,0:T(8,128)S(1)} %copy-done.4, ...), custom_call_target="tpu_custom_call" | custom-call | flops 40000000 | bytes 8388608 | tf_op jit(solution)/shard_map/smooth_last/pallas_call | solution.py:563
  (71 shorter events, 4.8 us)
Async XLA Ops:
  0.0 11.0 %copy-start.15 = (s32[128,2]{0,1:T(2,128)S(1)}, s32[128,2]{0,1:T(2,128)}, u32[]{:S(2)}) copy-start(s32[128,2]{0,1:T(2,128)} %param.15) | copy-start | bytes 3076
  0.0 11.2 %copy-start.6 = (s32[256]{0:T(256)S(1)}, s32[256]{0:T(256)}, u32[]{:S(2)}) copy-start(s32[256]{0:T(256)} %owned_ref.1) | copy-start | bytes 3076
  0.0 11.2 %copy-start.7 = (f32[8,2048]{1,0:T(8,128)S(1)}, f32[8,2048]{1,0:T(8,128)}, u32[]{:S(2)}) copy-start(f32[8,2048]{1,0:T(8,128)} %scale_ref.1) | copy-start | bytes 196612
  1.1 7.5 %collective-permute-start = (f32[8,2048]{1,0:T(8,128)S(1)}, f32[8,2048]{1,0:T(8,128)S(1)}, u32[]{:S(2)}, u32[]{:S(2)}) collective-permute-start(f32[8,2048]{1,0:T(8,128)S(1)} %get-tuple-element.86), channel_id=1, source_target_pairs={{2,4},{6,8},{10,12},{14,16},{18,20},{22,24},{26,28},{4,2},{8,6},{1... | collective-permute-start | bytes 196616 | tf_op jit(solution)/shard_map/ppermute | solution.py:435
  1.8 8.9 %collective-permute-start.1 = (f32[8,2048]{1,0:T(8,128)S(1)}, f32[8,2048]{1,0:T(8,128)S(1)}, u32[]{:S(2)}, u32[]{:S(2)}) collective-permute-start(f32[8,2048]{1,0:T(8,128)S(1)} %get-tuple-element.85), channel_id=1, source_target_pairs={{0,2},{2,0},{4,6},{6,4},{8,10},{10,8},{12,14},{14,12},{16,18},{18,... | collective-permute-start | bytes 196616 | tf_op jit(solution)/shard_map/ppermute | solution.py:436
  8.6 4.1 %copy-start.11 = (f32[8,2048]{1,0:T(8,128)}, f32[8,2048]{1,0:T(8,128)S(1)}, u32[]{:S(2)}) copy-start(f32[8,2048]{1,0:T(8,128)S(1)} %collective-permute-done.got_b_ref) | copy-start | bytes 196612
  10.7 2.1 %copy-start.12 = (f32[8,2048]{1,0:T(8,128)}, f32[8,2048]{1,0:T(8,128)S(1)}, u32[]{:S(2)}) copy-start(f32[8,2048]{1,0:T(8,128)S(1)} %collective-permute-done.1.got_a_ref) | copy-start | bytes 196612
  10.9 1.9 %collective-permute-start.2 = (f32[2,144,128]{2,1,0:T(8,128)S(1)}, f32[2,144,128]{2,1,0:T(8,128)S(1)}, u32[]{:S(2)}, u32[]{:S(2)}) collective-permute-start(f32[2,144,128]{2,1,0:T(8,128)S(1)} %pad_maximum_fusion.2), channel_id=1, source_target_pairs={{0,1},{1,0},{2,3},{3,2},{4,5},{5,4},{6,7},{7,6},{8,9},{9,8},{10,11... | collective-permute-start | bytes 442376 | tf_op jit(solution)/shard_map/ppermute | solution.py:468
  12.8 0.7 copy-start.13
  23.7 21.4 %all-to-all-start.1 = ((bf16[16,128,128]{2,1,0:T(8,128)(2,1)}), bf16[16,128,128]{2,1,0:T(8,128)(2,1)S(1)}, u32[]{:S(2)}, u32[]{:S(2)}) async-start(bf16[16,128,128]{2,1,0:T(8,128)(2,1)} %get-tuple-element.54), calls=%async_computation.1 | async-start | bytes 1048576 | tf_op jit(solution)/shard_map/all_to_all | solution.py:439
  45.1 1.2 %copy-start.9 = (bf16[16,128,128]{2,1,0:T(8,128)(2,1)}, bf16[16,128,128]{2,1,0:T(8,128)(2,1)S(1)}, u32[]{:S(2)}) copy-start(bf16[16,128,128]{2,1,0:T(8,128)(2,1)S(1)} %all-to-all-done.1) | copy-start | bytes 1572868
  46.3 5.2 %copy-start.8 = (bf16[16,64,64]{2,1,0:T(8,128)(2,1)S(1)}, bf16[16,64,64]{2,1,0:T(8,128)(2,1)}, u32[]{:S(2)}) copy-start(bf16[16,64,64]{2,1,0:T(8,128)(2,1)} %param.17) | copy-start | bytes 393220
  46.3 5.7 %copy-start.14 = (s32[128,32]{0,1:T(8,128)S(1)}, s32[128,32]{0,1:T(8,128)}, u32[]{:S(2)}) copy-start(s32[128,32]{0,1:T(8,128)} %param.16) | copy-start | bytes 49156
  46.3 16.2 %all-to-all-start.2 = ((f32[48,1,2048]{2,1,0:T(1,128)}), f32[48,1,2048]{2,1,0:T(1,128)S(1)}, u32[]{:S(2)}, u32[]{:S(2)}) async-start(f32[48,1,2048]{2,1,0:T(1,128)} %outbox.1), calls=%async_computation.2 | async-start | bytes 786432 | tf_op jit(solution)/shard_map/all_to_all | solution.py:439
  62.5 0.7 copy-start.10
  63.3 38.7 %copy-start.1 = (s32[128,2048]{1,0:T(8,128)S(1)}, s32[128,2048]{1,0:T(8,128)}, u32[]{:S(2)}) copy-start(s32[128,2048]{1,0:T(8,128)} %mask_ref.3) | copy-start | bytes 3145732
  63.3 38.7 %copy-start.2 = (f32[17,160,128]{2,1,0:T(8,128)S(1)}, f32[17,160,128]{2,1,0:T(8,128)}, u32[]{:S(2)}) copy-start(f32[17,160,128]{2,1,0:T(8,128)} %get-tuple-element.57.own_ref) | copy-start | bytes 4177924
  75.2 26.8 %copy-start = (f32[128,2048]{1,0:T(8,128)S(1)}, f32[128,2048]{1,0:T(8,128)}, u32[]{:S(2)}) copy-start(f32[128,2048]{1,0:T(8,128)} %dir_ref.3) | copy-start | bytes 3145732
  100.7 1.3 %collective-permute-start.3 = (bf16[144,128]{1,0:T(8,128)(2,1)S(1)}, bf16[144,128]{1,0:T(8,128)(2,1)S(1)}, u32[]{:S(2)}, u32[]{:S(2)}) collective-permute-start(bf16[144,128]{1,0:T(8,128)(2,1)S(1)} %fusion.5), channel_id=1, source_target_pairs={{0,1},{1,0},{2,3},{3,2},{4,5},{5,4},{6,7},{7,6},{8,9},{9,8},{10,11... | collective-permute-start | bytes 110600 | tf_op jit(solution)/shard_map/ppermute | solution.py:562
  102.0 1.3 %copy-start.3 = (f32[17,160,128]{2,1,0:T(8,128)S(1)}, f32[17,160,128]{2,1,0:T(8,128)}, u32[]{:S(2)}) copy-start(f32[17,160,128]{2,1,0:T(8,128)} %get-tuple-element.58.fn_ref) | copy-start | bytes 4177924
  103.3 1.3 %copy-start.4 = (f32[17,160,128]{2,1,0:T(8,128)S(1)}, f32[17,160,128]{2,1,0:T(8,128)}, u32[]{:S(2)}) copy-start(f32[17,160,128]{2,1,0:T(8,128)} %get-tuple-element.59.fw_ref) | copy-start | bytes 4177924
  104.7 1.3 %copy-start.5 = (f32[17,160,128]{2,1,0:T(8,128)S(1)}, f32[17,160,128]{2,1,0:T(8,128)}, u32[]{:S(2)}) copy-start(f32[17,160,128]{2,1,0:T(8,128)} %get-tuple-element.60.fe_ref) | copy-start | bytes 4177924

commit v2 on v1

--- a/solution.py
+++ b/solution.py
@@ -12,6 +12,7 @@
 SWEEPS = 4
 HALO = 8
 PAD = 16
+CHUNKS = 4
 CAP = 3
 
 
@@ -37,15 +38,16 @@
     return jnp.where((own > 0) & (other > 0), 0.5 * (own + other), 0.0)
 
 
-def sweeps(tiles, rows, bufs, own_ref, fn_ref, fw_ref, fe_ref, finish, half_done=None):
+def sweeps(tiles, rows, bufs, own_ref, fn_ref, fw_ref, fe_ref, finish, ready=None, part_done=None):
     for step in range(SWEEPS):
         src, dst = bufs[step % 2], bufs[1 - step % 2]
         last = step == SWEEPS - 1
         first_row = PAD if last else HALO
-        length = (rows - 2 * (PAD - HALO) if last else rows) // 2
-
-        for half in range(2):
-            start = first_row + half * length
+        parts = 2 if last else 3
+        length = (rows - 2 * (PAD - HALO) if last else rows) // parts
+
+        for index in range(parts):
+            start = first_row + index * length
             body = pl.ds(start, length)
 
             def tile(c, right, u_left, u, src=src, dst=dst, last=last, start=start, body=body):
@@ -66,19 +68,47 @@
                 return tile(c, c + 1, *carry)
 
             carry = src[tiles - 1, body, :], src[0, body, :]
-            carry = lax.fori_loop(0, tiles - 1, step_tile, carry, unroll=4)
+            if ready is not None and step == 0 and index == 0:
+                for k in range(CHUNKS):
+                    ready(k)
+                    low, high = chunk_of(tiles - 1, k)
+                    carry = lax.fori_loop(low, high, step_tile, carry, unroll=True)
+            else:
+                carry = lax.fori_loop(0, tiles - 1, step_tile, carry, unroll=8)
             if not last:
                 tile(tiles - 1, 0, *carry)
-            elif half_done is not None:
-                half_done(start - PAD, length)
+            elif part_done is not None:
+                part_done(start - PAD, length)
+
+
+def chunk_of(tiles, k):
+    return k * tiles // CHUNKS, (k + 1) * tiles // CHUNKS
+
+
+def column_chunks(refs, scratch, sems, tiles, lanes):
+    copies = []
+    for k in range(CHUNKS):
+        low, high = chunk_of(tiles, k)
+        cols = pl.ds(low * lanes, (high - low) * lanes)
+        copies.append([
+            pltpu.make_async_copy(ref.at[:, cols], buf.at[:, cols], sems.at[i, k])
+            for i, (ref, buf) in enumerate(zip(refs, scratch))
+        ])
+    return copies
 
 
 def smooth_first_kernel(
-    dir_ref, kap_ref, mask_ref, nbr_ref, got_a_ref, got_b_ref,
+    dir_in, kap_in, mask_in, nbr_ref, got_a_ref, got_b_ref,
     out_ref, own_out, fn_out, fw_out, fe_out,
-    done, own_ref, fn_ref, fw_ref, fe_ref, u0, u1, kbuf, sems,
+    dir_ref, kap_ref, mask_ref, done, own_ref, fn_ref, fw_ref, fe_ref, u0, u1, kbuf,
+    load_sems, sems,
 ):
     tiles, _, lanes = u0.shape
+    loads = column_chunks(
+        (dir_in, kap_in, mask_in), (dir_ref, kap_ref, mask_ref), load_sems, tiles - 1, lanes
+    )
+    for load in sum(loads, []):
+        load.start()
     own = dir_ref.shape[0]
     rows = own + 2 * HALO
     edge = (HALO, lanes)
@@ -108,7 +138,10 @@
         ends(c)
         return carry
 
-    lax.fori_loop(0, tiles - 1, fill, 0)
+    for k in range(CHUNKS):
+        for load in loads[k]:
+            load.wait()
+        lax.fori_loop(*chunk_of(tiles - 1, k), fill, 0)
     body = pl.ds(HALO, rows)
     lane = lane_iota((rows, lanes))
     near = jnp.where(lax.axis_index("col") == 0, lanes - 1 - lane, lane) >= lanes - SWEEPS
@@ -145,7 +178,7 @@
     def finish(c, row, value):
         done[c, pl.ds(row, value.shape[0]), :] = value.astype(jnp.bfloat16)
 
-    def half_done(row, length):
+    def part_done(row, length):
         part = pl.ds(row, length)
         copy = pltpu.make_async_copy(
             done.at[:, part, :], out_ref.at[:, part, :], sems.at[len(copies)]
@@ -153,15 +186,28 @@
         copies.append(copy)
         copy.start()
 
-    sweeps(tiles, rows, (u0, u1), own_ref, fn_ref, fw_ref, fe_ref, finish, half_done)
+    sweeps(tiles, rows, (u0, u1), own_ref, fn_ref, fw_ref, fe_ref, finish, part_done=part_done)
     for copy in copies:
         copy.wait()
 
 
 def smooth_last_kernel(
-    ret_ref, nbr_ref, own_ref, fn_ref, fw_ref, fe_ref, dir_ref, mask_ref, out_ref, u0, u1
+    ret_ref, nbr_ref, own_in, fn_in, fw_in, fe_in, dir_in, mask_in, out_ref,
+    own_ref, fn_ref, fw_ref, fe_ref, dir_ref, mask_ref, u0, u1, load_sems, sems,
 ):
     tiles, _, lanes = u0.shape
+    pairs = ((own_in, own_ref), (fn_in, fn_ref), (fw_in, fw_ref), (fe_in, fe_ref))
+    faces = []
+    for k in range(CHUNKS):
+        low, high = chunk_of(tiles - 1, k)
+        part = pl.ds(low, high - low + (1 if k == CHUNKS - 1 else 0))
+        faces.append([
+            pltpu.make_async_copy(ref.at[part], buf.at[part], sems.at[i, k])
+            for i, (ref, buf) in enumerate(pairs)
+        ])
+    loads = column_chunks((dir_in, mask_in), (dir_ref, mask_ref), load_sems, tiles - 1, lanes)
+    for load in sum(faces + loads, []):
+        load.start()
     own = dir_ref.shape[0]
     rows = own + 2 * HALO
     zero = jnp.zeros((HALO, lanes), jnp.float32)
@@ -186,7 +232,14 @@
         maskf = mask_ref[part, cols].astype(jnp.float32)
         out_ref[part, cols] = maskf * (dir_ref[part, cols] * maskf + value)
 
-    sweeps(tiles, rows, (u0, u1), own_ref, fn_ref, fw_ref, fe_ref, finish)
+    def ready(k):
+        for load in faces[k]:
+            load.wait()
+        if k == CHUNKS - 1:
+            for load in sum(loads, []):
+                load.wait()
+
+    sweeps(tiles, rows, (u0, u1), own_ref, fn_ref, fw_ref, fe_ref, finish, ready=ready)
 
 
 def outbox_kernel(owned_ref, anchor_ref, scale_ref, out_ref, *, seg_tiles, col_tiles, span):
@@ -196,8 +249,8 @@
     for i in range(seg_max):
         seg = owned_ref[me * seg_max + i]
         safe = jnp.maximum(seg, 0)
-        lane = anchor_ref[2 * safe] // seg_tiles
-        owner = lane * span + lax.rem(anchor_ref[2 * safe + 1], col_tiles)
+        lane = anchor_ref[0, safe] // seg_tiles
+        owner = lane * span + lax.rem(anchor_ref[1, safe], col_tiles)
         owner = jnp.where(seg >= 0, owner, -1)
         place = jnp.int32(0)
         for other in owners:
@@ -239,9 +292,9 @@
         cols = pl.ds(i * width, width)
         return pltpu.make_async_copy(prec_in.at[:, cols], prec_ref.at[:, cols], prec_sem.at[i])
 
-    fetch(0, 0)
     for i in range(order // width):
         prec_copy(i).start()
+    fetch(0, 0)
 
     def turn(q, carry):
         part = pl.ds(pl.multiple_of(q * lanes, lanes), lanes)
@@ -261,8 +314,8 @@
         def pair_of(table, q):
             sides = []
             for j in range(size):
-                low = table[0, index_ref[ids[j], 2 * q]]
-                high = table[1, index_ref[ids[j], 2 * q + 1]]
+                low = table[0, index_ref[2 * q, ids[j]]]
+                high = table[1, index_ref[2 * q + 1, ids[j]]]
                 sides.append(jnp.concatenate([low, high], axis=0))
             return sides
 
@@ -333,10 +386,6 @@
     own = chunk - 2 * HALO
     for s in range(parts):
         out_ref[s] = grid[pl.ds(s * own, chunk), :].astype(jnp.bfloat16)
-
-
-def vmem_need(rows):
-    return min(2 * rows * TILE_C * 4, 60 << 20)
 
 
 def vmem_spec():
@@ -447,7 +496,7 @@
         out_specs=vmem_spec(),
         compiler_params=pltpu.CompilerParams(vmem_limit_bytes=2 << 20),
         name="outbox",
-    )(owned_segments, seg_anchor.reshape(-1), obs_scale)
+    )(owned_segments, seg_anchor.T, obs_scale)
     few = swap(scales_out)
 
     def edge_cols(array):
@@ -470,6 +519,8 @@
     tiles = col_tiles + 1
     height = rows_dev + 2 * PAD
     buf = pltpu.VMEM((tiles, height, lanes), jnp.float32)
+    own_float = pltpu.VMEM((rows_dev, cols_dev), jnp.float32)
+    own_int = pltpu.VMEM((rows_dev, cols_dev), jnp.int32)
     face_shape = jax.ShapeDtypeStruct((tiles, height, lanes), jnp.float32)
     smoothed, own, fn, fw, fe = pl.pallas_call(
         smooth_first_kernel,
@@ -477,11 +528,12 @@
             jax.ShapeDtypeStruct((col_tiles, rows_dev, lanes), jnp.bfloat16),
             face_shape, face_shape, face_shape, face_shape,
         ),
-        in_specs=[vmem_spec()] * 6,
+        in_specs=[hbm_spec()] * 3 + [vmem_spec()] * 3,
         out_specs=(hbm_spec(),) * 5,
-        scratch_shapes=[pltpu.VMEM((col_tiles, rows_dev, lanes), jnp.bfloat16)]
+        scratch_shapes=[own_float, own_float, own_int]
+        + [pltpu.VMEM((col_tiles, rows_dev, lanes), jnp.bfloat16)]
         + [buf] * 7
-        + [pltpu.SemaphoreType.DMA((6,))],
+        + [pltpu.SemaphoreType.DMA((3, CHUNKS)), pltpu.SemaphoreType.DMA((6,))],
         cost_estimate=pl.CostEstimate(flops=40000000, bytes_accessed=8 << 20, transcendentals=0),
         name="smooth_first",
     )(direction, kappa, land_mask, nbr, got_a, got_b)
@@ -544,12 +596,13 @@
             pltpu.SemaphoreType.DMA((order // width,)),
             pltpu.SemaphoreType.DMA((2, batch)),
         ],
+        compiler_params=pltpu.CompilerParams(vmem_limit_bytes=57 << 20),
         cost_estimate=pl.CostEstimate(
             flops=8 * 2 * order * order * lanes, bytes_accessed=12 << 20, transcendentals=0
         ),
         name="segments",
     )(
-        info, interp_index, gathered.reshape(order, lanes),
+        info, interp_index.T, gathered.reshape(order, lanes),
         ahead, behind, precision, few, everything,
     )
 
@@ -563,10 +616,11 @@
     return pl.pallas_call(
         smooth_last_kernel,
         out_shape=jax.ShapeDtypeStruct((rows_dev, cols_dev), jnp.float32),
-        in_specs=[vmem_spec()] * 8,
+        in_specs=[vmem_spec()] * 2 + [hbm_spec()] * 6,
         out_specs=vmem_spec(),
-        scratch_shapes=[buf, buf],
-        compiler_params=pltpu.CompilerParams(vmem_limit_bytes=vmem_need(8 * tiles * height)),
+        scratch_shapes=[buf] * 4
+        + [own_float, own_int, buf, buf]
+        + [pltpu.SemaphoreType.DMA((2, CHUNKS)), pltpu.SemaphoreType.DMA((4, CHUNKS))],
         cost_estimate=pl.CostEstimate(flops=40000000, bytes_accessed=8 << 20, transcendentals=0),
         name="smooth_last",
     )(returned, border, own, fn, fw, fe, direction, land_mask)

time: 113 us -> 115 us (1.018)
  Pallas kernels: 30 us -> 35.5 us
  local copies, waits for them, and re-layouts: 8.42 us -> 4 us
    unnamed x33 -> x22, local copies, waits for them, and re-layouts: 5.6 us -> 2.04 us
    pallas_call x1, Pallas kernels: 6.28 us -> 9.81 us  [per_device(): pl.pallas_call(smooth_last_kernel, out_shape=jax.ShapeDtypeStruct((rows_d...]
    pallas_call x1, Pallas kernels: 11.9 us -> 13.9 us  [per_device(): pl.pallas_call(functools.partial(segments_kernel, width=width, batch=batc...]
  transfers between devices with their start and end apart: 6 -> 6, of which waited for: 4 -> 4; matrix products, arithmetic and copies ran while one was open for 8% -> 7% of each run, Pallas kernels for 1% -> 1%
where the time goes in v2:
time: 115 us; the launch traced here: 114 us
  Pallas kernels  35.5 us (31%)
  blocking collectives  25.3 us (22%)
  waiting for transfers between devices  23.3 us (20%)
  starting transfers between devices  16.8 us (15%)
  other arithmetic  7.51 us (7%)
  local copies, waits for them, and re-layouts  4 us (3%)
  between operations  1.68 us (1%)
    all_to_all x1, blocking collectives, swap(): lax.all_to_all(array, 'slab', split_axis=0, concat_axis=0, tiled=True, ax...  25.3 us
    all_to_all x2, waiting for transfers between devices, swap(): lax.all_to_all(array, 'slab', split_axis=0, concat_axis=0, tiled=True, ax...  20 us
    pallas_call x1, Pallas kernels, per_device(): pl.pallas_call(functools.partial(segments_kernel, width=width, batch=batc...  13.9 us
    pallas_call x1, Pallas kernels, per_device(): pl.pallas_call(smooth_first_kernel, out_shape=(jax.ShapeDtypeStruct((col_...  10.3 us
    all_to_all x2, starting transfers between devices, swap(): lax.all_to_all(array, 'slab', split_axis=0, concat_axis=0, tiled=True, ax...  10.2 us
    pallas_call x1, Pallas kernels, per_device(): pl.pallas_call(smooth_last_kernel, out_shape=jax.ShapeDtypeStruct((rows_d...  9.81 us
    ppermute x1, starting transfers between devices, per_device(): got_a = lax.ppermute(send_a, 'slab', pairs_a)  5.79 us
  transfers between devices with their start and end apart: 6, of which 4 were waited for; matrix products, arithmetic and copies ran while one was open for 7% of the time, Pallas kernels for 1%

profile of v2, /device:TPU:0, one launch (start us, length us, event | category | flops | bytes accessed | tf_op | source)
XLA Modules:
  0.0 114.1 jit_solution(5763609186580926537)
XLA Ops:
  0.0 1.1 convert_multiply_fusion.2
  1.1 0.7 collective-permute-start
  1.8 5.8 %collective-permute-start.1 = (f32[8,2048]{1,0:T(8,128)S(1)}, f32[8,2048]{1,0:T(8,128)S(1)}, u32[]{:S(2)}, u32[]{:S(2)}) collective-permute-start(f32[8,2048]{1,0:T(8,128)S(1)} %get-tuple-element.85), channel_id=1, source_target_pairs={{0,2},{2,0},{4,6},{6,4},{8,10},{10,8},{12,14},{14,12},{16,18},{18,... | collective-permute-start | bytes 196616 | tf_op jit(solution)/shard_map/ppermute | solution.py:485
  7.6 1.0 convert_multiply_fusion
  8.6 2.1 %collective-permute-done.1.got_a_ref = f32[8,2048]{1,0:T(8,128)S(1)} collective-permute-done((f32[8,2048]{1,0:T(8,128)S(1)}, f32[8,2048]{1,0:T(8,128)S(1)}, u32[]{:S(2)}, u32[]{:S(2)}) %collective-permute-start.1) | collective-permute-done | bytes 65568 | tf_op jit(solution)/shard_map/ppermute | solution.py:485
  11.0 1.5 %outbox.1 = f32[48,1,2048]{2,1,0:T(1,128)} custom-call(s32[256]{0:T(256)S(1)} %copy-done, s32[2,128]{1,0:T(2,128)S(1)} %bitcast.35, f32[8,2048]{1,0:T(8,128)S(1)} %copy-done.2), custom_call_target="tpu_custom_call" | custom-call | tf_op jit(solution)/shard_map/outbox/pallas_call | solution.py:492
  12.5 0.7 copy-done.9
  13.2 10.3 %smooth_first.1 = (bf16[16,128,128]{2,1,0:T(8,128)(2,1)}, f32[17,160,128]{2,1,0:T(8,128)}, f32[17,160,128]{2,1,0:T(8,128)}, f32[17,160,128]{2,1,0:T(8,128)}, f32[17,160,128]{2,1,0:T(8,128)}) custom-call(f32[128,2048]{1,0:T(8,128)} %dir_in.3, f32[128,2048]{1,0:T(8,128)} %kap_in.1, s32[128,2048]{1,0:T(8,128)} %mask_in.3, f32[2,144,128]{2,1,0:T(8,128)} %copy-done.9, ...), custom_call_target="tpu_custom_call" | custom-call | flops 40000000 | bytes 8388608 | tf_op jit(solution)/shard_map/smooth_first/pallas_call | solution.py:525
  23.5 5.9 %all-to-all-start.1 = ((bf16[16,128,128]{2,1,0:T(8,128)(2,1)}), bf16[16,128,128]{2,1,0:T(8,128)(2,1)S(1)}, u32[]{:S(2)}, u32[]{:S(2)}) async-start(bf16[16,128,128]{2,1,0:T(8,128)(2,1)} %get-tuple-element.54), calls=%async_computation.1 | async-start | bytes 1048576 | tf_op jit(solution)/shard_map/all_to_all | solution.py:488
  29.7 0.7 convert_reduce_fusion.1
  30.8 0.6 select_reduce_fusion.6
  32.0 12.9 %all-to-all-done.1 = bf16[16,128,128]{2,1,0:T(8,128)(2,1)S(1)} async-done(((bf16[16,128,128]{2,1,0:T(8,128)(2,1)}), bf16[16,128,128]{2,1,0:T(8,128)(2,1)S(1)}, u32[]{:S(2)}, u32[]{:S(2)}) %all-to-all-start.1) | async-done | bytes 524320 | tf_op jit(solution)/shard_map/all_to_all | solution.py:488
  44.9 0.5 slice.115
  46.1 4.3 %all-to-all-start.2 = ((f32[48,1,2048]{2,1,0:T(1,128)}), f32[48,1,2048]{2,1,0:T(1,128)S(1)}, u32[]{:S(2)}, u32[]{:S(2)}) async-start(f32[48,1,2048]{2,1,0:T(1,128)} %outbox.1), calls=%async_computation.2 | async-start | bytes 786432 | tf_op jit(solution)/shard_map/all_to_all | solution.py:488
  51.8 1.4 %pad_add_fusion.1.info_ref = s32[386]{0:T(512)} fusion(s32[384]{0:T(512)S(1)} %reshape.112, s32[1]{0:T(128)} %bitcast.8, s32[1]{0:T(128)} %bitcast.7), kind=kLoop, calls=%fused_computation.44 | loop fusion | flops 772 | bytes 3088 | tf_op jit(solution)/shard_map/concatenate | solution.py:436
  53.5 0.8 pad_maximum_fusion.1.behind_ref
  54.3 0.8 pad_maximum_fusion.ahead_ref
  55.2 7.2 %all-to-all-done.2.few_ref = f32[48,1,2048]{2,1,0:T(1,128)S(1)} async-done(((f32[48,1,2048]{2,1,0:T(1,128)}), f32[48,1,2048]{2,1,0:T(1,128)S(1)}, u32[]{:S(2)}, u32[]{:S(2)}) %all-to-all-start.2) | async-done | bytes 393248 | tf_op jit(solution)/shard_map/all_to_all | solution.py:488
  62.3 0.7 copy-done.6
  63.1 13.9 %segments.1 = bf16[16,144,128]{2,1,0:T(8,128)(2,1)} custom-call(s32[386]{0:T(512)} %pad_add_fusion.1.info_ref, s32[32,128]{1,0:T(8,128)} %bitcast.44, bf16[2048,128]{1,0:T(8,128)(2,1)} %bitcast.38, bf16[2,16,64,128]{3,2,1,0:T(8,128)(2,1)} %pad_maximum_fusion.ahead_ref, bf16[2,16,64,128]{3,2,1,0:T(8,128)(2,1)} %pad_maximum_fusion.1.behind_ref, ...), custom_call_target="tpu_custom_call" | custom-call | flops 8589934592 | bytes 12582912 | tf_op jit(solution)/shard_map/segments/pallas_call | solution.py:582
  77.0 25.3 %all_to_all.20.ret_ref = bf16[16,144,128]{2,1,0:T(8,128)(2,1)S(1)} all-to-all(bf16[16,144,128]{2,1,0:T(8,128)(2,1)} %segments.1), channel_id=1, replica_groups=mesh['slab'=16,'col'=2] {'slab'}, dimensions={0} | all-to-all | bytes 1179648 | tf_op jit(solution)/shard_map/all_to_all | solution.py:488
  102.4 1.2 %collective-permute-done.3.nbr_ref = bf16[144,128]{1,0:T(8,128)(2,1)S(1)} collective-permute-done((bf16[144,128]{1,0:T(8,128)(2,1)S(1)}, bf16[144,128]{1,0:T(8,128)(2,1)S(1)}, u32[]{:S(2)}, u32[]{:S(2)}) %collective-permute-start.3) | collective-permute-done | bytes 36896 | tf_op jit(solution)/shard_map/ppermute | solution.py:615
  103.6 0.6 copy-done.10
  104.2 9.8 %smooth_last.1 = f32[128,2048]{1,0:T(8,128)} custom-call(bf16[16,144,128]{2,1,0:T(8,128)(2,1)} %copy-done.3, bf16[144,128]{1,0:T(8,128)(2,1)} %copy-done.10, f32[17,160,128]{2,1,0:T(8,128)} %get-tuple-element.57.own_in, f32[17,160,128]{2,1,0:T(8,128)} %get-tuple-element.58.fn_in, f32[17,160,128]{2,1,0:T(8,128)} %get-tuple-element.59.fw_in, ...), custom_call_target="tpu_custom_call" | custom-call | flops 40000000 | bytes 8388608 | tf_op jit(solution)/shard_map/smooth_last/pallas_call | solution.py:616
  (58 shorter events, 2.6 us)
Async XLA Ops:
  0.0 11.0 %copy-start = (s32[256]{0:T(256)S(1)}, s32[256]{0:T(256)}, u32[]{:S(2)}) copy-start(s32[256]{0:T(256)} %owned_ref.1) | copy-start | bytes 3076
  0.0 11.0 %copy-start.2 = (f32[8,2048]{1,0:T(8,128)S(1)}, f32[8,2048]{1,0:T(8,128)}, u32[]{:S(2)}) copy-start(f32[8,2048]{1,0:T(8,128)} %scale_ref.1) | copy-start | bytes 196612
  0.0 11.0 %copy-start.1 = (s32[128,2]{0,1:T(2,128)S(1)}, s32[128,2]{0,1:T(2,128)}, u32[]{:S(2)}) copy-start(s32[128,2]{0,1:T(2,128)} %param.15) | copy-start | bytes 3076
  1.1 7.5 %collective-permute-start = (f32[8,2048]{1,0:T(8,128)S(1)}, f32[8,2048]{1,0:T(8,128)S(1)}, u32[]{:S(2)}, u32[]{:S(2)}) collective-permute-start(f32[8,2048]{1,0:T(8,128)S(1)} %get-tuple-element.86), channel_id=1, source_target_pairs={{2,4},{6,8},{10,12},{14,16},{18,20},{22,24},{26,28},{4,2},{8,6},{1... | collective-permute-start | bytes 196616 | tf_op jit(solution)/shard_map/ppermute | solution.py:484
  1.8 8.9 %collective-permute-start.1 = (f32[8,2048]{1,0:T(8,128)S(1)}, f32[8,2048]{1,0:T(8,128)S(1)}, u32[]{:S(2)}, u32[]{:S(2)}) collective-permute-start(f32[8,2048]{1,0:T(8,128)S(1)} %get-tuple-element.85), channel_id=1, source_target_pairs={{0,2},{2,0},{4,6},{6,4},{8,10},{10,8},{12,14},{14,12},{16,18},{18,... | collective-permute-start | bytes 196616 | tf_op jit(solution)/shard_map/ppermute | solution.py:485
  8.6 3.9 %copy-start.7 = (f32[8,2048]{1,0:T(8,128)}, f32[8,2048]{1,0:T(8,128)S(1)}, u32[]{:S(2)}) copy-start(f32[8,2048]{1,0:T(8,128)S(1)} %collective-permute-done.got_b_ref) | copy-start | bytes 196612
  10.7 1.8 %copy-start.8 = (f32[8,2048]{1,0:T(8,128)}, f32[8,2048]{1,0:T(8,128)S(1)}, u32[]{:S(2)}) copy-start(f32[8,2048]{1,0:T(8,128)S(1)} %collective-permute-done.1.got_a_ref) | copy-start | bytes 196612
  10.9 1.6 %collective-permute-start.2 = (f32[2,144,128]{2,1,0:T(8,128)S(1)}, f32[2,144,128]{2,1,0:T(8,128)S(1)}, u32[]{:S(2)}, u32[]{:S(2)}) collective-permute-start(f32[2,144,128]{2,1,0:T(8,128)S(1)} %pad_maximum_fusion.2), channel_id=1, source_target_pairs={{0,1},{1,0},{2,3},{3,2},{4,5},{5,4},{6,7},{7,6},{8,9},{9,8},{10,11... | collective-permute-start | bytes 442376 | tf_op jit(solution)/shard_map/ppermute | solution.py:517
  12.5 0.7 copy-start.9
  23.5 21.4 %all-to-all-start.1 = ((bf16[16,128,128]{2,1,0:T(8,128)(2,1)}), bf16[16,128,128]{2,1,0:T(8,128)(2,1)S(1)}, u32[]{:S(2)}, u32[]{:S(2)}) async-start(bf16[16,128,128]{2,1,0:T(8,128)(2,1)} %get-tuple-element.54), calls=%async_computation.1 | async-start | bytes 1048576 | tf_op jit(solution)/shard_map/all_to_all | solution.py:488
  44.9 1.2 %copy-start.5 = (bf16[16,128,128]{2,1,0:T(8,128)(2,1)}, bf16[16,128,128]{2,1,0:T(8,128)(2,1)S(1)}, u32[]{:S(2)}) copy-start(bf16[16,128,128]{2,1,0:T(8,128)(2,1)S(1)} %all-to-all-done.1) | copy-start | bytes 1572868
  46.1 5.2 %copy-start.4 = (bf16[16,64,64]{2,1,0:T(8,128)(2,1)S(1)}, bf16[16,64,64]{2,1,0:T(8,128)(2,1)}, u32[]{:S(2)}) copy-start(bf16[16,64,64]{2,1,0:T(8,128)(2,1)} %param.17) | copy-start | bytes 393220
  46.1 16.2 %all-to-all-start.2 = ((f32[48,1,2048]{2,1,0:T(1,128)}), f32[48,1,2048]{2,1,0:T(1,128)S(1)}, u32[]{:S(2)}, u32[]{:S(2)}) async-start(f32[48,1,2048]{2,1,0:T(1,128)} %outbox.1), calls=%async_computation.2 | async-start | bytes 786432 | tf_op jit(solution)/shard_map/all_to_all | solution.py:488
  62.3 0.7 copy-start.6
  102.3 1.3 %copy-start.3 = (bf16[16,144,128]{2,1,0:T(8,128)(2,1)}, bf16[16,144,128]{2,1,0:T(8,128)(2,1)S(1)}, u32[]{:S(2)}) copy-start(bf16[16,144,128]{2,1,0:T(8,128)(2,1)S(1)} %all_to_all.20.ret_ref) | copy-start | bytes 1769476
  102.3 1.3 %collective-permute-start.3 = (bf16[144,128]{1,0:T(8,128)(2,1)S(1)}, bf16[144,128]{1,0:T(8,128)(2,1)S(1)}, u32[]{:S(2)}, u32[]{:S(2)}) collective-permute-start(bf16[144,128]{1,0:T(8,128)(2,1)S(1)} %fusion.5), channel_id=1, source_target_pairs={{0,1},{1,0},{2,3},{3,2},{4,5},{5,4},{6,7},{7,6},{8,9},{9,8},{10,11... | collective-permute-start | bytes 110600 | tf_op jit(solution)/shard_map/ppermute | solution.py:615
  103.6 0.6 copy-start.10

commit v3 on v2

--- a/solution.py
+++ b/solution.py
@@ -13,7 +13,7 @@
 HALO = 8
 PAD = 16
 CHUNKS = 4
-CAP = 3
+CAP = 4
 
 
 def lane_iota(shape):
@@ -35,15 +35,34 @@
 
 
 def face(own, other):
-    return jnp.where((own > 0) & (other > 0), 0.5 * (own + other), 0.0)
-
-
-def sweeps(tiles, rows, bufs, own_ref, fn_ref, fw_ref, fe_ref, finish, ready=None, part_done=None):
+    return jnp.where(jnp.minimum(own, other) > 0, own + other, 0.0)
+
+
+def derive(tiles, rows, own_ref, fn_ref, fw_ref, fe_ref):
+    def tile(c, right):
+        body = pl.ds(HALO, rows)
+        west = fw_ref[c, body, :]
+        east = from_right(west, fw_ref[right, body, :])
+        fe_ref[c, body, :] = east
+        vertical = fn_ref[c, body, :] + fn_ref[c, pl.ds(HALO + 1, rows), :]
+        own_ref[c, body, :] = 1.0 - (vertical + (west + east))
+
+    def step(c, carry):
+        tile(c, c + 1)
+        return carry
+
+    lax.fori_loop(0, tiles - 1, step, 0, unroll=2)
+    tile(tiles - 1, 0)
+
+
+def sweeps(tiles, rows, bufs, own_ref, fn_ref, fw_ref, fe_ref, finish, before_last=None, part_done=None):
     for step in range(SWEEPS):
         src, dst = bufs[step % 2], bufs[1 - step % 2]
         last = step == SWEEPS - 1
         first_row = PAD if last else HALO
         parts = 2 if last else 3
+        if last and before_last is not None:
+            before_last()
         length = (rows - 2 * (PAD - HALO) if last else rows) // parts
 
         for index in range(parts):
@@ -68,13 +87,7 @@
                 return tile(c, c + 1, *carry)
 
             carry = src[tiles - 1, body, :], src[0, body, :]
-            if ready is not None and step == 0 and index == 0:
-                for k in range(CHUNKS):
-                    ready(k)
-                    low, high = chunk_of(tiles - 1, k)
-                    carry = lax.fori_loop(low, high, step_tile, carry, unroll=True)
-            else:
-                carry = lax.fori_loop(0, tiles - 1, step_tile, carry, unroll=8)
+            carry = lax.fori_loop(0, tiles - 1, step_tile, carry, unroll=8)
             if not last:
                 tile(tiles - 1, 0, *carry)
             elif part_done is not None:
@@ -99,7 +112,7 @@
 
 def smooth_first_kernel(
     dir_in, kap_in, mask_in, nbr_ref, got_a_ref, got_b_ref,
-    out_ref, own_out, fn_out, fw_out, fe_out,
+    out_ref, fn_out, fw_out,
     dir_ref, kap_ref, mask_ref, done, own_ref, fn_ref, fw_ref, fe_ref, u0, u1, kbuf,
     load_sems, sems,
 ):
@@ -116,7 +129,16 @@
     even = lax.rem(lax.axis_index("slab"), 2) == 0
     low = row_iota(edge) < HALO // 2
 
-    def ends(c):
+    def edges(c, cols):
+        got_a, got_b = got_a_ref[:, cols], got_b_ref[:, cols]
+        top = jnp.where(even, got_b, got_a)
+        bot = jnp.where(even, got_a, got_b)
+        u0[c, pl.ds(HALO, HALO), :] = jnp.where(low, 0.0, pltpu.roll(top, HALO // 2, 0))
+        kbuf[c, pl.ds(HALO, HALO), :] = jnp.where(low, 0.0, 0.5 * top)
+        u0[c, pl.ds(PAD + own, HALO), :] = jnp.where(low, bot, 0.0)
+        kbuf[c, pl.ds(PAD + own, HALO), :] = jnp.where(
+            low, 0.5 * pltpu.roll(bot, HALO // 2, 0), 0.0
+        )
         for part in (pl.ds(0, HALO), pl.ds(PAD + own + HALO, HALO)):
             u0[c, part, :] = zero
             u1[c, part, :] = zero
@@ -127,53 +149,36 @@
         cols = pl.ds(pl.multiple_of(c * lanes, lanes), lanes)
         maskf = mask_ref[:, cols].astype(jnp.float32)
         u0[c, pl.ds(PAD, own), :] = dir_ref[:, cols] * maskf
-        kbuf[c, pl.ds(PAD, own), :] = kap_ref[:, cols] * maskf
-        got_a, got_b = got_a_ref[:, cols], got_b_ref[:, cols]
-        top = jnp.where(even, got_b, got_a)
-        bot = jnp.where(even, got_a, got_b)
-        u0[c, pl.ds(HALO, HALO), :] = jnp.where(low, 0.0, pltpu.roll(top, HALO // 2, 0))
-        kbuf[c, pl.ds(HALO, HALO), :] = jnp.where(low, 0.0, top)
-        u0[c, pl.ds(PAD + own, HALO), :] = jnp.where(low, bot, 0.0)
-        kbuf[c, pl.ds(PAD + own, HALO), :] = jnp.where(low, pltpu.roll(bot, HALO // 2, 0), 0.0)
-        ends(c)
+        kbuf[c, pl.ds(PAD, own), :] = kap_ref[:, cols] * (0.5 * maskf)
+        edges(c, cols)
         return carry
 
+    u0[tiles - 1, pl.ds(PAD, own), :] = nbr_ref[0]
+    kbuf[tiles - 1, pl.ds(PAD, own), :] = 0.5 * nbr_ref[1]
+    edges(tiles - 1, pl.ds((tiles - 1) * lanes, lanes))
+
+    def faces(c, k_left):
+        body = pl.ds(HALO, rows)
+        k = kbuf[c, body, :]
+        fn_ref[c, body, :] = face(k, kbuf[c, pl.ds(HALO - 1, rows), :])
+        fw_ref[c, body, :] = face(k, from_left(k, k_left))
+        return k
+
+    k_left = kbuf[tiles - 1, pl.ds(HALO, rows), :]
     for k in range(CHUNKS):
         for load in loads[k]:
             load.wait()
-        lax.fori_loop(*chunk_of(tiles - 1, k), fill, 0)
-    body = pl.ds(HALO, rows)
-    lane = lane_iota((rows, lanes))
-    near = jnp.where(lax.axis_index("col") == 0, lanes - 1 - lane, lane) >= lanes - SWEEPS
-    u0[tiles - 1, body, :] = nbr_ref[0]
-    kbuf[tiles - 1, body, :] = jnp.where(near, nbr_ref[1], 0.0)
-    ends(tiles - 1)
-
-    def faces(c, right, k_left, k):
-        body = pl.ds(HALO, rows)
-        k_right = kbuf[right, body, :]
-        north = face(k, kbuf[c, pl.ds(HALO - 1, rows), :])
-        south = face(k, kbuf[c, pl.ds(HALO + 1, rows), :])
-        west = face(k, from_left(k, k_left))
-        east = face(k, from_right(k, k_right))
-        fn_ref[c, body, :] = north
-        fw_ref[c, body, :] = west
-        fe_ref[c, body, :] = east
-        own_ref[c, body, :] = 1.0 - ((north + south) + (west + east))
-        return k, k_right
-
-    body = pl.ds(HALO, rows)
-    carry = kbuf[tiles - 1, body, :], kbuf[0, body, :]
-    carry = lax.fori_loop(0, tiles - 1, lambda c, carry: faces(c, c + 1, *carry), carry)
-    faces(tiles - 1, 0, *carry)
+        low_tile, high_tile = chunk_of(tiles - 1, k)
+        lax.fori_loop(low_tile, high_tile, fill, 0)
+        k_left = lax.fori_loop(low_tile, high_tile, faces, k_left)
+    faces(tiles - 1, k_left)
     copies = [
         pltpu.make_async_copy(ref, out, sems.at[i])
-        for i, (ref, out) in enumerate(
-            ((own_ref, own_out), (fn_ref, fn_out), (fw_ref, fw_out), (fe_ref, fe_out))
-        )
+        for i, (ref, out) in enumerate(((fn_ref, fn_out), (fw_ref, fw_out)))
     ]
     for copy in copies:
         copy.start()
+    derive(tiles, rows, own_ref, fn_ref, fw_ref, fe_ref)
 
     def finish(c, row, value):
         done[c, pl.ds(row, value.shape[0]), :] = value.astype(jnp.bfloat16)
@@ -192,39 +197,38 @@
 
 
 def smooth_last_kernel(
-    ret_ref, nbr_ref, own_in, fn_in, fw_in, fe_in, dir_in, mask_in, out_ref,
+    ret_ref, nbr_ref, fn_in, fw_in, dir_in, mask_in, out_ref,
     own_ref, fn_ref, fw_ref, fe_ref, dir_ref, mask_ref, u0, u1, load_sems, sems,
 ):
     tiles, _, lanes = u0.shape
-    pairs = ((own_in, own_ref), (fn_in, fn_ref), (fw_in, fw_ref), (fe_in, fe_ref))
-    faces = []
-    for k in range(CHUNKS):
-        low, high = chunk_of(tiles - 1, k)
-        part = pl.ds(low, high - low + (1 if k == CHUNKS - 1 else 0))
-        faces.append([
-            pltpu.make_async_copy(ref.at[part], buf.at[part], sems.at[i, k])
-            for i, (ref, buf) in enumerate(pairs)
-        ])
-    loads = column_chunks((dir_in, mask_in), (dir_ref, mask_ref), load_sems, tiles - 1, lanes)
-    for load in sum(faces + loads, []):
+    faces = [
+        pltpu.make_async_copy(ref, buf, sems.at[i])
+        for i, (ref, buf) in enumerate(((fn_in, fn_ref), (fw_in, fw_ref)))
+    ]
+    loads = sum(
+        column_chunks((dir_in, mask_in), (dir_ref, mask_ref), load_sems, tiles - 1, lanes), []
+    )
+    for load in faces + loads:
         load.start()
-    own = dir_ref.shape[0]
+    own, chunk = dir_ref.shape[0], ret_ref.shape[1]
     rows = own + 2 * HALO
-    zero = jnp.zeros((HALO, lanes), jnp.float32)
-
-    def ends(c):
-        for buf in (u0, u1):
-            buf[c, pl.ds(0, HALO), :] = zero
-            buf[c, pl.ds(PAD + own + HALO, HALO), :] = zero
+    zero = jnp.zeros((PAD, lanes), jnp.float32)
+
+    def put(c, value):
+        for part in (pl.ds(0, PAD), pl.ds(PAD + own, PAD)):
+            u0[c, part, :] = zero
+            u1[c, part, :] = zero
+        u0[c, pl.ds(PAD - (chunk - own) // 2, chunk), :] = value.astype(jnp.float32)
 
     def fill(c, carry):
-        u0[c, pl.ds(HALO, rows), :] = ret_ref[c].astype(jnp.float32)
-        ends(c)
+        put(c, ret_ref[c])
         return carry
 
     lax.fori_loop(0, tiles - 1, fill, 0)
-    u0[tiles - 1, pl.ds(HALO, rows), :] = nbr_ref[...].astype(jnp.float32)
-    ends(tiles - 1)
+    put(tiles - 1, nbr_ref[...])
+    for load in faces:
+        load.wait()
+    derive(tiles, rows, own_ref, fn_ref, fw_ref, fe_ref)
 
     def finish(c, row, value):
         cols = pl.ds(pl.multiple_of(c * lanes, lanes), lanes)
@@ -232,17 +236,25 @@
         maskf = mask_ref[part, cols].astype(jnp.float32)
         out_ref[part, cols] = maskf * (dir_ref[part, cols] * maskf + value)
 
-    def ready(k):
-        for load in faces[k]:
+    def before_last():
+        for load in loads:
             load.wait()
-        if k == CHUNKS - 1:
-            for load in sum(loads, []):
-                load.wait()
-
-    sweeps(tiles, rows, (u0, u1), own_ref, fn_ref, fw_ref, fe_ref, finish, ready=ready)
-
-
-def outbox_kernel(owned_ref, anchor_ref, scale_ref, out_ref, *, seg_tiles, col_tiles, span):
+
+    sweeps(tiles, rows, (u0, u1), own_ref, fn_ref, fw_ref, fe_ref, finish, before_last)
+
+
+def outbox_kernel(
+    owned_in, anchor_in, scale_ref, out_ref, owned_ref, anchor_ref, sems,
+    *, seg_tiles, col_tiles, span,
+):
+    copies = [
+        pltpu.make_async_copy(owned_in, owned_ref, sems.at[0]),
+        pltpu.make_async_copy(anchor_in, anchor_ref, sems.at[1]),
+    ]
+    for copy in copies:
+        copy.start()
+    for copy in copies:
+        copy.wait()
     seg_max = scale_ref.shape[0]
     me = lax.axis_index("slab") * lax.axis_size("col") + lax.axis_index("col")
     owners = []
@@ -383,9 +395,10 @@
         return carry
 
     lax.fori_loop(0, blocks, unturn, 0, unroll=4)
-    own = chunk - 2 * HALO
+    own = order // parts
+    first = HALO - (chunk - own) // 2
     for s in range(parts):
-        out_ref[s] = grid[pl.ds(s * own, chunk), :].astype(jnp.bfloat16)
+        out_ref[s] = grid[pl.ds(s * own + first, chunk), :].astype(jnp.bfloat16)
 
 
 def vmem_spec():
@@ -469,20 +482,31 @@
     my_device = my_slab * col_count + my_col
     is_low = my_col == 0
 
+    def edge_cols(array):
+        return jnp.where(is_low, array[:, cols_dev - lanes :], array[:, :lanes])
+
+    edge_mask = edge_cols(land_mask).astype(jnp.float32)
+    edge = jnp.stack([edge_cols(direction) * edge_mask, edge_cols(kappa) * edge_mask])
+    nbr = lax.ppermute(edge, "col", [(0, 1), (1, 0)])
+    near = jnp.where(
+        is_low, lane_iota((1, lanes)) < SWEEPS, lane_iota((1, lanes)) >= lanes - SWEEPS
+    )
+    nbr = jnp.where(near[None], nbr, 0.0)
+
     def edge_rows(start):
         part = slice(start, start + SWEEPS)
         maskf = land_mask[part].astype(jnp.float32)
-        return jnp.concatenate([direction[part] * maskf, kappa[part] * maskf], axis=0)
+        field = jnp.concatenate([direction[part] * maskf, nbr[0, part]], axis=1)
+        coeff = jnp.concatenate([kappa[part] * maskf, nbr[1, part]], axis=1)
+        return jnp.concatenate([field, coeff], axis=0)
 
     first_rows, last_rows = edge_rows(0), edge_rows(rows_dev - SWEEPS)
     even = my_slab % 2 == 0
     pairs_a = [(i, i ^ 1) for i in range(slab_count)]
     pairs_b = [(i, i + 1) for i in range(1, slab_count - 1, 2)]
     pairs_b = pairs_b + [(j, i) for i, j in pairs_b]
-    send_a = jnp.where(even, last_rows, first_rows)
-    send_b = jnp.where(even, first_rows, last_rows)
-    got_b = lax.ppermute(send_b, "slab", pairs_b)
-    got_a = lax.ppermute(send_a, "slab", pairs_a)
+    got_b = lax.ppermute(jnp.where(even, first_rows, last_rows), "slab", pairs_b)
+    got_a = lax.ppermute(jnp.where(even, last_rows, first_rows), "slab", pairs_a)
 
     def swap(array, groups=None):
         return lax.all_to_all(
@@ -492,29 +516,16 @@
     scales_out = pl.pallas_call(
         functools.partial(outbox_kernel, seg_tiles=seg_tiles, col_tiles=col_tiles, span=span),
         out_shape=jax.ShapeDtypeStruct((slab_count * CAP, 1, order), jnp.float32),
-        in_specs=[smem_spec(), smem_spec(), vmem_spec()],
+        in_specs=[hbm_spec(), hbm_spec(), vmem_spec()],
         out_specs=vmem_spec(),
-        compiler_params=pltpu.CompilerParams(vmem_limit_bytes=2 << 20),
+        scratch_shapes=[
+            pltpu.SMEM(owned_segments.shape, jnp.int32),
+            pltpu.SMEM(seg_anchor.shape[::-1], jnp.int32),
+            pltpu.SemaphoreType.DMA((2,)),
+        ],
         name="outbox",
     )(owned_segments, seg_anchor.T, obs_scale)
     few = swap(scales_out)
-
-    def edge_cols(array):
-        return jnp.where(is_low, array[:, cols_dev - lanes :], array[:, :lanes])
-
-    edge_mask = edge_cols(land_mask).astype(jnp.float32)
-    above = edge_cols(jnp.where(even, got_b, got_a))
-    below = edge_cols(jnp.where(even, got_a, got_b))
-    blank = jnp.zeros((HALO - SWEEPS, lanes), jnp.float32)
-
-    def with_halo(array, part):
-        return jnp.concatenate([blank, above[part], array, below[part], blank], axis=0)
-
-    edge = jnp.stack([
-        with_halo(edge_cols(direction) * edge_mask, slice(0, SWEEPS)),
-        with_halo(edge_cols(kappa) * edge_mask, slice(SWEEPS, 2 * SWEEPS)),
-    ])
-    nbr = lax.ppermute(edge, "col", [(0, 1), (1, 0)])
 
     tiles = col_tiles + 1
     height = rows_dev + 2 * PAD
@@ -522,18 +533,18 @@
     own_float = pltpu.VMEM((rows_dev, cols_dev), jnp.float32)
     own_int = pltpu.VMEM((rows_dev, cols_dev), jnp.int32)
     face_shape = jax.ShapeDtypeStruct((tiles, height, lanes), jnp.float32)
-    smoothed, own, fn, fw, fe = pl.pallas_call(
+    smoothed, fn, fw = pl.pallas_call(
         smooth_first_kernel,
         out_shape=(
             jax.ShapeDtypeStruct((col_tiles, rows_dev, lanes), jnp.bfloat16),
-            face_shape, face_shape, face_shape, face_shape,
+            face_shape, face_shape,
         ),
         in_specs=[hbm_spec()] * 3 + [vmem_spec()] * 3,
-        out_specs=(hbm_spec(),) * 5,
+        out_specs=(hbm_spec(),) * 3,
         scratch_shapes=[own_float, own_float, own_int]
         + [pltpu.VMEM((col_tiles, rows_dev, lanes), jnp.bfloat16)]
         + [buf] * 7
-        + [pltpu.SemaphoreType.DMA((3, CHUNKS)), pltpu.SemaphoreType.DMA((6,))],
+        + [pltpu.SemaphoreType.DMA((3, CHUNKS)), pltpu.SemaphoreType.DMA((4,))],
         cost_estimate=pl.CostEstimate(flops=40000000, bytes_accessed=8 << 20, transcendentals=0),
         name="smooth_first",
     )(direction, kappa, land_mask, nbr, got_a, got_b)
@@ -563,7 +574,6 @@
         return obs_scale[slot].reshape(slab_count * cap, 1, order)
 
     many = (slab_count * seg_max, 1, order)
-    overflow = overflow & (gathered[0, 0, 0] < jnp.inf)
     everything = lax.cond(
         overflow,
         lambda: swap(outbox(seg_max, slot_in)),
@@ -575,7 +585,7 @@
         )(),
     )
 
-    chunk = rows_dev + 2 * HALO
+    chunk = rows_dev + 2 * SWEEPS
     width = min(512, order)
     batch = 4
 
@@ -616,28 +626,28 @@
     return pl.pallas_call(
         smooth_last_kernel,
         out_shape=jax.ShapeDtypeStruct((rows_dev, cols_dev), jnp.float32),
-        in_specs=[vmem_spec()] * 2 + [hbm_spec()] * 6,
+        in_specs=[vmem_spec()] * 2 + [hbm_spec()] * 4,
         out_specs=vmem_spec(),
         scratch_shapes=[buf] * 4
         + [own_float, own_int, buf, buf]
-        + [pltpu.SemaphoreType.DMA((2, CHUNKS)), pltpu.SemaphoreType.DMA((4, CHUNKS))],
+        + [pltpu.SemaphoreType.DMA((2, CHUNKS)), pltpu.SemaphoreType.DMA((2,))],
         cost_estimate=pl.CostEstimate(flops=40000000, bytes_accessed=8 << 20, transcendentals=0),
         name="smooth_last",
-    )(returned, border, own, fn, fw, fe, direction, land_mask)
+    )(returned, border, fn, fw, direction, land_mask)
 
 
 def lane_edges(returned, slab_count, span, my_slab, rows_dev):
+    halo = SWEEPS
     up = [(i, i + 1) for i in range(span - 1, slab_count - 1, span)]
     down = [(j, i) for i, j in up]
-    own_last = returned[:, rows_dev : rows_dev + HALO]
-    own_first = returned[:, HALO : 2 * HALO]
-    above = lax.ppermute(own_last, "slab", up)
-    below = lax.ppermute(own_first, "slab", down)
-    first = (my_slab % span == 0)
-    last = (my_slab % span == span - 1)
-    head = jnp.where(first, above, returned[:, :HALO])
-    tail = jnp.where(last, below, returned[:, rows_dev + HALO :])
-    return jnp.concatenate([head, returned[:, HALO : rows_dev + HALO], tail], axis=1)
+    own = returned[:, halo : halo + rows_dev]
+    above = lax.ppermute(own[:, rows_dev - halo :], "slab", up)
+    below = lax.ppermute(own[:, :halo], "slab", down)
+    first = my_slab % span == 0
+    last = my_slab % span == span - 1
+    head = jnp.where(first, above, returned[:, :halo])
+    tail = jnp.where(last, below, returned[:, halo + rows_dev :])
+    return jnp.concatenate([head, own, tail], axis=1)
 
 
 def solution(mesh):

time: 115 us -> 120 us (1.043)
  waiting for transfers between devices: 23.3 us -> 28.1 us
  Pallas kernels: 35.5 us -> 37 us
    all_to_all x2, waiting for transfers between devices: 20 us -> 24.7 us  [swap(): lax.all_to_all(array, 'slab', split_axis=0, concat_axis=0, tiled=True, ax...]
    all_to_all x2, starting transfers between devices: 10.2 us -> 13.6 us  [swap(): lax.all_to_all(array, 'slab', split_axis=0, concat_axis=0, tiled=True, ax...]
    ppermute x2, starting transfers between devices: 6.45 us -> 3.2 us  [the longest x1 2.55 us: per_device(): lax.ppermute(jnp.where(even, last_rows, first_rows), 'slab', pairs_a)]
  transfers between devices with their start and end apart: 6 -> 6, of which waited for: 4 -> 4; matrix products, arithmetic and copies ran while one was open for 7% -> 4% of each run, Pallas kernels for 1% -> 2%
where the time goes in v3:
time: 120 us; the launch traced here: 119 us
  Pallas kernels  37 us (31%)
  waiting for transfers between devices  28.1 us (23%)
  blocking collectives  24.8 us (21%)
  starting transfers between devices  17.4 us (14%)
  other arithmetic  6.79 us (6%)
  local copies, waits for them, and re-layouts  4.02 us (3%)
    all_to_all x1, blocking collectives, swap(): lax.all_to_all(array, 'slab', split_axis=0, concat_axis=0, tiled=True, ax...  24.8 us
    all_to_all x2, waiting for transfers between devices, swap(): lax.all_to_all(array, 'slab', split_axis=0, concat_axis=0, tiled=True, ax...  24.7 us
    pallas_call x1, Pallas kernels, per_device(): pl.pallas_call(functools.partial(segments_kernel, width=width, batch=batc...  13.9 us
    all_to_all x2, starting transfers between devices, swap(): lax.all_to_all(array, 'slab', split_axis=0, concat_axis=0, tiled=True, ax...  13.6 us
    pallas_call x1, Pallas kernels, per_device(): pl.pallas_call(smooth_first_kernel, out_shape=(jax.ShapeDtypeStruct((col_...  10.5 us
    pallas_call x1, Pallas kernels, per_device(): pl.pallas_call(smooth_last_kernel, out_shape=jax.ShapeDtypeStruct((rows_d...  10.1 us
    unnamed x22, local copies, waits for them, and re-layouts  2.67 us
    pallas_call x1, Pallas kernels, per_device(): pl.pallas_call(functools.partial(outbox_kernel, seg_tiles=seg_tiles, col_...  2.57 us
  transfers between devices with their start and end apart: 6, of which 4 were waited for; matrix products, arithmetic and copies ran while one was open for 4% of the time, Pallas kernels for 2%

profile of v3, /device:TPU:0, one launch (start us, length us, event | category | flops | bytes accessed | tf_op | source)
XLA Modules:
  0.0 119.1 jit_solution(6637107028927043711)
XLA Ops:
  0.0 1.0 multiply_bitcast_fusion.1
  1.0 0.6 collective-permute-start
  1.6 1.0 convert_multiply_fusion.1
  2.7 2.6 %outbox.1 = f32[64,1,2048]{2,1,0:T(1,128)} custom-call(s32[256]{0:T(256)} %owned_in.1, s32[2,128]{1,0:T(2,128)} %bitcast.47, f32[8,2048]{1,0:T(8,128)} %scale_ref.1), custom_call_target="tpu_custom_call" | custom-call | tf_op jit(solution)/shard_map/outbox/pallas_call | solution.py:516
  5.3 2.5 %collective-permute-start.1 = (f32[8,2176]{1,0:T(8,128)S(1)}, f32[8,2176]{1,0:T(8,128)S(1)}, u32[]{:S(2)}, u32[]{:S(2)}) collective-permute-start(f32[8,2176]{1,0:T(8,128)S(1)} %get-tuple-element.80), channel_id=1, source_target_pairs={{0,2},{2,0},{4,6},{6,4},{8,10},{10,8},{12,14},{14,12},{16,18},{18,... | collective-permute-start | bytes 208904 | tf_op jit(solution)/shard_map/ppermute | solution.py:509
  7.9 0.7 collective-permute-start.2
  8.6 2.1 %collective-permute-done.1.got_a_ref = f32[8,2176]{1,0:T(8,128)S(1)} collective-permute-done((f32[8,2176]{1,0:T(8,128)S(1)}, f32[8,2176]{1,0:T(8,128)S(1)}, u32[]{:S(2)}, u32[]{:S(2)}) %collective-permute-start.1) | collective-permute-done | bytes 69664 | tf_op jit(solution)/shard_map/ppermute | solution.py:509
  10.7 0.6 copy-done.6
  11.4 0.6 copy-done.7
  12.0 10.5 %smooth_first.1 = (bf16[16,128,128]{2,1,0:T(8,128)(2,1)}, f32[17,160,128]{2,1,0:T(8,128)}, f32[17,160,128]{2,1,0:T(8,128)}) custom-call(f32[128,2048]{1,0:T(8,128)} %dir_in.3, f32[128,2048]{1,0:T(8,128)} %kap_in.1, s32[128,2048]{1,0:T(8,128)} %mask_in.3, f32[2,128,128]{2,1,0:T(8,128)} %copy-done.3, f32[8,2176]{1,0:T(8,128)} %copy-done.6, f32[8,2176]{1,0:T(8,128)} %copy-done.7), custom_call_target="tpu_custom_call" | custom-call | flops 40000000 | bytes 8388608 | tf_op jit(solution)/shard_map/smooth_first/pallas_call | solution.py:536
  22.7 0.7 convert_reduce_fusion.1
  23.8 0.6 select_reduce_fusion.6
  25.1 9.7 %all-to-all-start.2 = ((f32[64,1,2048]{2,1,0:T(1,128)}), f32[64,1,2048]{2,1,0:T(1,128)S(1)}, u32[]{:S(2)}, u32[]{:S(2)}) async-start(f32[64,1,2048]{2,1,0:T(1,128)} %outbox.1), calls=%async_computation.2 | async-start | bytes 1048576 | tf_op jit(solution)/shard_map/all_to_all | solution.py:512
  35.3 14.0 %all-to-all-done.2.few_ref = f32[64,1,2048]{2,1,0:T(1,128)S(1)} async-done(((f32[64,1,2048]{2,1,0:T(1,128)}), f32[64,1,2048]{2,1,0:T(1,128)S(1)}, u32[]{:S(2)}, u32[]{:S(2)}) %all-to-all-start.2) | async-done | bytes 524320 | tf_op jit(solution)/shard_map/all_to_all | solution.py:512
  49.2 3.9 %all-to-all-start.1 = ((bf16[16,128,128]{2,1,0:T(8,128)(2,1)}), bf16[16,128,128]{2,1,0:T(8,128)(2,1)S(1)}, u32[]{:S(2)}, u32[]{:S(2)}) async-start(bf16[16,128,128]{2,1,0:T(8,128)(2,1)} %get-tuple-element.52), calls=%async_computation.1 | async-start | bytes 1048576 | tf_op jit(solution)/shard_map/all_to_all | solution.py:512
  54.0 1.3 %pad_add_fusion.1.info_ref = s32[386]{0:T(512)} fusion(s32[384]{0:T(512)S(1)} %reshape.122, s32[1]{0:T(128)} %bitcast.12, s32[1]{0:T(128)} %bitcast.11), kind=kLoop, calls=%fused_computation.45 | loop fusion | flops 772 | bytes 3088 | tf_op jit(solution)/shard_map/concatenate | solution.py:449
  55.6 1.1 pad_maximum_fusion
  56.7 10.8 %all-to-all-done.1 = bf16[16,128,128]{2,1,0:T(8,128)(2,1)S(1)} async-done(((bf16[16,128,128]{2,1,0:T(8,128)(2,1)}), bf16[16,128,128]{2,1,0:T(8,128)(2,1)S(1)}, u32[]{:S(2)}, u32[]{:S(2)}) %all-to-all-start.1) | async-done | bytes 524320 | tf_op jit(solution)/shard_map/all_to_all | solution.py:512
  67.5 0.8 copy-done.5
  68.3 13.9 %segments.1 = bf16[16,136,128]{2,1,0:T(8,128)(2,1)} custom-call(s32[386]{0:T(512)} %pad_add_fusion.1.info_ref, s32[32,128]{1,0:T(8,128)} %bitcast.51, bf16[2048,128]{1,0:T(8,128)(2,1)} %bitcast.46, bf16[2,16,64,128]{3,2,1,0:T(8,128)(2,1)} %get-tuple-element.90.ahead_ref, bf16[2,16,64,128]{3,2,1,0:T(8,128)(2,1)} %get-tuple-element.91.behind_ref, ...), custom_call_target="tpu_custom_call" | custom-call | flops 8589934592 | bytes 12582912 | tf_op jit(solution)/shard_map/segments/pallas_call | solution.py:592
  82.1 24.8 %all_to_all.20.ret_ref = bf16[16,136,128]{2,1,0:T(8,128)(2,1)S(1)} all-to-all(bf16[16,136,128]{2,1,0:T(8,128)(2,1)} %segments.1), channel_id=1, replica_groups=mesh['slab'=16,'col'=2] {'slab'}, dimensions={0} | all-to-all | bytes 1114112 | tf_op jit(solution)/shard_map/all_to_all | solution.py:512
  107.0 1.2 %collective-permute-done.3.nbr_ref = bf16[136,128]{1,0:T(8,128)(2,1)S(1)} collective-permute-done((bf16[136,128]{1,0:T(8,128)(2,1)S(1)}, bf16[136,128]{1,0:T(8,128)(2,1)S(1)}, u32[]{:S(2)}, u32[]{:S(2)}) %collective-permute-start.3) | collective-permute-done | bytes 34848 | tf_op jit(solution)/shard_map/ppermute | solution.py:625
  108.2 0.6 copy-done.8
  108.8 10.1 %smooth_last.1 = f32[128,2048]{1,0:T(8,128)} custom-call(bf16[16,136,128]{2,1,0:T(8,128)(2,1)} %copy-done.1, bf16[136,128]{1,0:T(8,128)(2,1)} %copy-done.8, f32[17,160,128]{2,1,0:T(8,128)} %get-tuple-element.55.fn_in, f32[17,160,128]{2,1,0:T(8,128)} %get-tuple-element.56.fw_in, f32[128,2048]{1,0:T(8,128)} %dir_in.3, s32[128,2048]{1,0:T(8,128)} %mask_in.3), custom_call_target="tpu_custom_call" | custom-call | flops 40000000 | bytes 8388608 | tf_op jit(solution)/shard_map/smooth_last/pallas_call | solution.py:626
  (51 shorter events, 2.5 us)
Async XLA Ops:
  1.0 4.2 %collective-permute-start = (f32[2,128,128]{2,1,0:T(8,128)S(1)}, f32[2,128,128]{2,1,0:T(8,128)S(1)}, u32[]{:S(2)}, u32[]{:S(2)}) collective-permute-start(f32[2,128,128]{2,1,0:T(8,128)S(1)} %pad_maximum_fusion.2), channel_id=1, source_target_pairs={{0,1},{1,0},{2,3},{3,2},{4,5},{5,4},{6,7},{7,6},{8,9},{9,8},{10,11... | collective-permute-start | bytes 393224 | tf_op jit(solution)/shard_map/ppermute | solution.py:490
  5.3 5.5 %copy-start.3 = (f32[2,128,128]{2,1,0:T(8,128)}, f32[2,128,128]{2,1,0:T(8,128)S(1)}, u32[]{:S(2)}) copy-start(f32[2,128,128]{2,1,0:T(8,128)S(1)} %broadcast_select_fusion.nbr_ref) | copy-start | bytes 393220
  5.3 5.4 %collective-permute-start.1 = (f32[8,2176]{1,0:T(8,128)S(1)}, f32[8,2176]{1,0:T(8,128)S(1)}, u32[]{:S(2)}, u32[]{:S(2)}) collective-permute-start(f32[8,2176]{1,0:T(8,128)S(1)} %get-tuple-element.80), channel_id=1, source_target_pairs={{0,2},{2,0},{4,6},{6,4},{8,10},{10,8},{12,14},{14,12},{16,18},{18,... | collective-permute-start | bytes 208904 | tf_op jit(solution)/shard_map/ppermute | solution.py:509
  7.9 2.9 %collective-permute-start.2 = (f32[8,2176]{1,0:T(8,128)S(1)}, f32[8,2176]{1,0:T(8,128)S(1)}, u32[]{:S(2)}, u32[]{:S(2)}) collective-permute-start(f32[8,2176]{1,0:T(8,128)S(1)} %get-tuple-element.79), channel_id=1, source_target_pairs={{2,4},{6,8},{10,12},{14,16},{18,20},{22,24},{26,28},{4,2},{8,6},{1... | collective-permute-start | bytes 208904 | tf_op jit(solution)/shard_map/ppermute | solution.py:508
  8.6 13.9 %copy-start.10 = (s32[128,2]{0,1:T(2,128)S(1)}, s32[128,2]{0,1:T(2,128)}, u32[]{:S(2)}) copy-start(s32[128,2]{0,1:T(2,128)} %param.15) | copy-start | bytes 3076
  8.6 13.9 %copy-start.9 = (s32[256]{0:T(256)S(1)}, s32[256]{0:T(256)}, u32[]{:S(2)}) copy-start(s32[256]{0:T(256)} %owned_in.1) | copy-start | bytes 3076
  8.6 16.5 %copy-start = (f32[8,2048]{1,0:T(8,128)S(1)}, f32[8,2048]{1,0:T(8,128)}, u32[]{:S(2)}) copy-start(f32[8,2048]{1,0:T(8,128)} %scale_ref.1) | copy-start | bytes 196612
  10.7 0.6 copy-start.6
  11.4 0.6 copy-start.7
  25.1 28.1 %copy-start.2 = (bf16[16,64,64]{2,1,0:T(8,128)(2,1)S(1)}, bf16[16,64,64]{2,1,0:T(8,128)(2,1)}, u32[]{:S(2)}) copy-start(bf16[16,64,64]{2,1,0:T(8,128)(2,1)} %param.17) | copy-start | bytes 393220
  25.1 24.1 %all-to-all-start.2 = ((f32[64,1,2048]{2,1,0:T(1,128)}), f32[64,1,2048]{2,1,0:T(1,128)S(1)}, u32[]{:S(2)}, u32[]{:S(2)}) async-start(f32[64,1,2048]{2,1,0:T(1,128)} %outbox.1), calls=%async_computation.2 | async-start | bytes 1048576 | tf_op jit(solution)/shard_map/all_to_all | solution.py:512
  49.2 6.4 %copy-start.4 = (f32[64,1,2048]{2,1,0:T(1,128)}, f32[64,1,2048]{2,1,0:T(1,128)S(1)}, u32[]{:S(2)}) copy-start(f32[64,1,2048]{2,1,0:T(1,128)S(1)} %all-to-all-done.2.few_ref) | copy-start | bytes 1572868
  49.2 18.2 %all-to-all-start.1 = ((bf16[16,128,128]{2,1,0:T(8,128)(2,1)}), bf16[16,128,128]{2,1,0:T(8,128)(2,1)S(1)}, u32[]{:S(2)}, u32[]{:S(2)}) async-start(bf16[16,128,128]{2,1,0:T(8,128)(2,1)} %get-tuple-element.52), calls=%async_computation.1 | async-start | bytes 1048576 | tf_op jit(solution)/shard_map/all_to_all | solution.py:512
  67.5 0.8 copy-start.5
  106.9 1.3 %copy-start.1 = (bf16[16,136,128]{2,1,0:T(8,128)(2,1)}, bf16[16,136,128]{2,1,0:T(8,128)(2,1)S(1)}, u32[]{:S(2)}) copy-start(bf16[16,136,128]{2,1,0:T(8,128)(2,1)S(1)} %all_to_all.20.ret_ref) | copy-start | bytes 1671172
  107.0 1.3 %collective-permute-start.3 = (bf16[136,128]{1,0:T(8,128)(2,1)S(1)}, bf16[136,128]{1,0:T(8,128)(2,1)S(1)}, u32[]{:S(2)}, u32[]{:S(2)}) collective-permute-start(bf16[136,128]{1,0:T(8,128)(2,1)S(1)} %fusion.5), channel_id=1, source_target_pairs={{0,1},{1,0},{2,3},{3,2},{4,5},{5,4},{6,7},{7,6},{8,9},{9,8},{10,11... | collective-permute-start | bytes 104456 | tf_op jit(solution)/shard_map/ppermute | solution.py:625
  108.2 0.6 copy-start.8

commit v4 on v3

--- a/solution.py
+++ b/solution.py
@@ -277,36 +277,42 @@
 def segments_kernel(
     info_ref, index_ref, x_ref, ahead_ref, behind_ref, prec_in, few_ref, all_ref,
     out_ref, prec_ref, turned, weighted, zbuf, scale_row, adj, grid, prec_sem, scale_sem,
-    *, width, batch,
+    *, width, sizes,
 ):
     parts, chunk, lanes = out_ref.shape
     order = prec_ref.shape[0]
     blocks = order // lanes
+    pieces = order // width
+    batch = sizes[-1]
     count = info_ref[0]
     full = info_ref[1]
 
-    def scale_copy(source, row, slot, j):
-        return pltpu.make_async_copy(source.at[row], scale_row.at[slot, j], scale_sem.at[slot, j])
-
-    def fetch(g, slot):
+    def prec_copy(i):
+        cols = pl.ds(pl.multiple_of(i * width, width), width)
+        return pltpu.make_async_copy(prec_in.at[:, cols], prec_ref.at[:, cols], prec_sem.at[i])
+
+    def scale_copy(source, row, j):
+        return pltpu.make_async_copy(source.at[row], scale_row.at[j], scale_sem.at[j])
+
+    def fetch(g):
         for j in range(batch):
             e = g * batch + j
 
             @pl.when((e < count) & (full == 0))
             def _(e=e, j=j):
-                scale_copy(few_ref, info_ref[3 + 3 * e], slot, j).start()
+                scale_copy(few_ref, info_ref[3 + 3 * e], j).start()
 
             @pl.when((e < count) & (full != 0))
             def _(e=e, j=j):
-                scale_copy(all_ref, info_ref[4 + 3 * e], slot, j).start()
-
-    def prec_copy(i):
-        cols = pl.ds(i * width, width)
-        return pltpu.make_async_copy(prec_in.at[:, cols], prec_ref.at[:, cols], prec_sem.at[i])
-
-    for i in range(order // width):
-        prec_copy(i).start()
-    fetch(0, 0)
+                scale_copy(all_ref, info_ref[4 + 3 * e], j).start()
+
+            @pl.when(e >= count)
+            def _(j=j):
+                scale_row[j] = jnp.zeros((1, order), jnp.float32)
+
+    prec_copy(0).start()
+    fetch(0)
+    prec_copy(1).start()
 
     def turn(q, carry):
         part = pl.ds(pl.multiple_of(q * lanes, lanes), lanes)
@@ -316,12 +322,15 @@
 
     lax.fori_loop(0, blocks, turn, 0, unroll=4)
 
-    def work(g, size):
-        slot = lax.rem(g, 2)
-        ids = [info_ref[2 + 3 * (g * batch + j)] for j in range(size)]
+    def work(g, size, live):
+        ids = []
         for j in range(size):
-            scale_copy(few_ref, 0, slot, j).wait()
-        fetch(g + 1, 1 - slot)
+            e = g * batch + j
+            ids.append(info_ref[2 + 3 * jnp.minimum(e, count - 1)])
+
+            @pl.when(j < live)
+            def _(j=j):
+                scale_copy(few_ref, 0, j).wait()
 
         def pair_of(table, q):
             sides = []
@@ -337,18 +346,22 @@
             seg = jnp.dot(turned[:, part], right, preferred_element_type=jnp.float32)
             seg = seg.astype(jnp.bfloat16).astype(jnp.float32)
             for j in range(size):
-                value = seg[:, j * lanes : (j + 1) * lanes] * scale_row[slot, j, :, part]
+                value = seg[:, j * lanes : (j + 1) * lanes] * scale_row[j, :, part]
                 weighted[j * lanes : (j + 1) * lanes, part] = value.astype(jnp.bfloat16)
             return carry
 
-        lax.fori_loop(0, blocks, interp, 0, unroll=4)
-
-        for i in range(order // width):
-            cols = pl.ds(i * width, width)
+        lax.fori_loop(0, blocks, interp, 0, unroll=4 if size <= 4 else 2)
+
+        def product(i, carry):
+            cols = pl.ds(pl.multiple_of(i * width, width), width)
 
             @pl.when(g == 0)
-            def _(i=i):
+            def _():
                 prec_copy(i).wait()
+
+            @pl.when((g == 0) & (i + 2 < pieces))
+            def _():
+                prec_copy(i + 2).start()
 
             prod = jnp.dot(
                 weighted[: size * lanes, :], prec_ref[:, cols],
@@ -356,7 +369,10 @@
             )
             for j in range(size):
                 rows = slice(j * lanes, (j + 1) * lanes)
-                zbuf[rows, cols] = (prod[rows] * scale_row[slot, j, :, cols]).astype(jnp.bfloat16)
+                zbuf[rows, cols] = (prod[rows] * scale_row[j, :, cols]).astype(jnp.bfloat16)
+            return carry
+
+        lax.fori_loop(0, pieces, product, 0)
 
         def back(q, carry):
             part = pl.ds(pl.multiple_of(q * lanes, lanes), lanes)
@@ -367,22 +383,27 @@
             adj[:, part] = adj[:, part] + jnp.dot(left, right, preferred_element_type=jnp.float32)
             return carry
 
-        lax.fori_loop(0, blocks, back, 0, unroll=4)
+        lax.fori_loop(0, blocks, back, 0, unroll=4 if size <= 4 else 2)
 
     def whole_group(g, carry):
-        work(g, batch)
+        work(g, batch, batch)
+        fetch(g + 1)
         return carry
 
     lax.fori_loop(0, count // batch, whole_group, 0)
-    for size in range(1, batch):
-
-        @pl.when(lax.rem(count, batch) == size)
+    rest = lax.rem(count, batch)
+    smaller = 0
+    for size in sizes:
+
+        @pl.when((rest > smaller) & (rest <= size))
         def _(size=size):
-            work(count // batch, size)
+            work(count // batch, size, rest)
+
+        smaller = size
 
     @pl.when(count == 0)
     def _():
-        for i in range(order // width):
+        for i in range(2):
             prec_copy(i).wait()
 
     zero = jnp.zeros((HALO, lanes), jnp.float32)
@@ -586,11 +607,12 @@
     )
 
     chunk = rows_dev + 2 * SWEEPS
-    width = min(512, order)
-    batch = 4
+    width = order // 4
+    sizes = (1, 2, 3, 4, 6, 8, 10)
+    batch = sizes[-1]
 
     returning = pl.pallas_call(
-        functools.partial(segments_kernel, width=width, batch=batch),
+        functools.partial(segments_kernel, width=width, sizes=sizes),
         out_shape=jax.ShapeDtypeStruct((span, chunk, lanes), jnp.bfloat16),
         in_specs=[smem_spec(), smem_spec(), vmem_spec(), vmem_spec(), vmem_spec()]
         + [hbm_spec()] * 3,
@@ -600,11 +622,11 @@
             pltpu.VMEM((lanes, order), jnp.bfloat16),
             pltpu.VMEM((batch * lanes, order), jnp.bfloat16),
             pltpu.VMEM((batch * lanes, order), jnp.bfloat16),
-            pltpu.VMEM((2, batch, 1, order), jnp.float32),
+            pltpu.VMEM((batch, 1, order), jnp.float32),
             pltpu.VMEM((lanes, order), jnp.float32),
             pltpu.VMEM((order + 2 * HALO, lanes), jnp.float32),
             pltpu.SemaphoreType.DMA((order // width,)),
-            pltpu.SemaphoreType.DMA((2, batch)),
+            pltpu.SemaphoreType.DMA((batch,)),
         ],
         compiler_params=pltpu.CompilerParams(vmem_limit_bytes=57 << 20),
         cost_estimate=pl.CostEstimate(

time: 120 us -> 119 us (level)
  Pallas kernels: 37 us -> 35.1 us
    pallas_call x1, Pallas kernels: 13.9 us -> 11.9 us  [per_device(): pl.pallas_call(functools.partial(segments_kernel, width=width, sizes=size...]
where the time goes in v4:
time: 119 us; the launch traced here: 118 us
  Pallas kernels  35.1 us (29%)
  waiting for transfers between devices  28.1 us (24%)
  blocking collectives  25.5 us (21%)
  starting transfers between devices  17.4 us (15%)
  other arithmetic  6.79 us (6%)
  local copies, waits for them, and re-layouts  4.02 us (3%)
    all_to_all x1, blocking collectives, swap(): lax.all_to_all(array, 'slab', split_axis=0, concat_axis=0, tiled=True, ax...  25.5 us
    all_to_all x2, waiting for transfers between devices, swap(): lax.all_to_all(array, 'slab', split_axis=0, concat_axis=0, tiled=True, ax...  24.7 us
    all_to_all x2, starting transfers between devices, swap(): lax.all_to_all(array, 'slab', split_axis=0, concat_axis=0, tiled=True, ax...  13.6 us
    pallas_call x1, Pallas kernels, per_device(): pl.pallas_call(functools.partial(segments_kernel, width=width, sizes=size...  11.9 us
    pallas_call x1, Pallas kernels, per_device(): pl.pallas_call(smooth_first_kernel, out_shape=(jax.ShapeDtypeStruct((col_...  10.5 us
    pallas_call x1, Pallas kernels, per_device(): pl.pallas_call(smooth_last_kernel, out_shape=jax.ShapeDtypeStruct((rows_d...  10.1 us
    unnamed x22, local copies, waits for them, and re-layouts  2.67 us
    pallas_call x1, Pallas kernels, per_device(): pl.pallas_call(functools.partial(outbox_kernel, seg_tiles=seg_tiles, col_...  2.57 us
  transfers between devices with their start and end apart: 6, of which 4 were waited for; matrix products, arithmetic and copies ran while one was open for 4% of the time, Pallas kernels for 2%

profile of v4, /device:TPU:0, one launch (start us, length us, event | category | flops | bytes accessed | tf_op | source)
XLA Modules:
  0.0 117.8 jit_solution(7415581772224254244)
XLA Ops:
  0.0 1.0 multiply_bitcast_fusion.1
  1.0 0.6 collective-permute-start
  1.6 1.0 convert_multiply_fusion.1
  2.7 2.6 %outbox.1 = f32[64,1,2048]{2,1,0:T(1,128)} custom-call(s32[256]{0:T(256)} %owned_in.1, s32[2,128]{1,0:T(2,128)} %bitcast.47, f32[8,2048]{1,0:T(8,128)} %scale_ref.1), custom_call_target="tpu_custom_call" | custom-call | tf_op jit(solution)/shard_map/outbox/pallas_call | solution.py:537
  5.3 2.5 %collective-permute-start.1 = (f32[8,2176]{1,0:T(8,128)S(1)}, f32[8,2176]{1,0:T(8,128)S(1)}, u32[]{:S(2)}, u32[]{:S(2)}) collective-permute-start(f32[8,2176]{1,0:T(8,128)S(1)} %get-tuple-element.80), channel_id=1, source_target_pairs={{0,2},{2,0},{4,6},{6,4},{8,10},{10,8},{12,14},{14,12},{16,18},{18,... | collective-permute-start | bytes 208904 | tf_op jit(solution)/shard_map/ppermute | solution.py:530
  7.9 0.7 collective-permute-start.2
  8.6 2.1 %collective-permute-done.1.got_a_ref = f32[8,2176]{1,0:T(8,128)S(1)} collective-permute-done((f32[8,2176]{1,0:T(8,128)S(1)}, f32[8,2176]{1,0:T(8,128)S(1)}, u32[]{:S(2)}, u32[]{:S(2)}) %collective-permute-start.1) | collective-permute-done | bytes 69664 | tf_op jit(solution)/shard_map/ppermute | solution.py:530
  10.7 0.6 copy-done.6
  11.4 0.6 copy-done.7
  12.0 10.5 %smooth_first.1 = (bf16[16,128,128]{2,1,0:T(8,128)(2,1)}, f32[17,160,128]{2,1,0:T(8,128)}, f32[17,160,128]{2,1,0:T(8,128)}) custom-call(f32[128,2048]{1,0:T(8,128)} %dir_in.3, f32[128,2048]{1,0:T(8,128)} %kap_in.1, s32[128,2048]{1,0:T(8,128)} %mask_in.3, f32[2,128,128]{2,1,0:T(8,128)} %copy-done.3, f32[8,2176]{1,0:T(8,128)} %copy-done.6, f32[8,2176]{1,0:T(8,128)} %copy-done.7), custom_call_target="tpu_custom_call" | custom-call | flops 40000000 | bytes 8388608 | tf_op jit(solution)/shard_map/smooth_first/pallas_call | solution.py:557
  22.7 0.7 convert_reduce_fusion.1
  23.8 0.6 select_reduce_fusion.6
  25.1 9.7 %all-to-all-start.2 = ((f32[64,1,2048]{2,1,0:T(1,128)}), f32[64,1,2048]{2,1,0:T(1,128)S(1)}, u32[]{:S(2)}, u32[]{:S(2)}) async-start(f32[64,1,2048]{2,1,0:T(1,128)} %outbox.1), calls=%async_computation.2 | async-start | bytes 1048576 | tf_op jit(solution)/shard_map/all_to_all | solution.py:533
  35.3 14.0 %all-to-all-done.2.few_ref = f32[64,1,2048]{2,1,0:T(1,128)S(1)} async-done(((f32[64,1,2048]{2,1,0:T(1,128)}), f32[64,1,2048]{2,1,0:T(1,128)S(1)}, u32[]{:S(2)}, u32[]{:S(2)}) %all-to-all-start.2) | async-done | bytes 524320 | tf_op jit(solution)/shard_map/all_to_all | solution.py:533
  49.2 3.9 %all-to-all-start.1 = ((bf16[16,128,128]{2,1,0:T(8,128)(2,1)}), bf16[16,128,128]{2,1,0:T(8,128)(2,1)S(1)}, u32[]{:S(2)}, u32[]{:S(2)}) async-start(bf16[16,128,128]{2,1,0:T(8,128)(2,1)} %get-tuple-element.52), calls=%async_computation.1 | async-start | bytes 1048576 | tf_op jit(solution)/shard_map/all_to_all | solution.py:533
  54.0 1.3 %pad_add_fusion.1.info_ref = s32[386]{0:T(512)} fusion(s32[384]{0:T(512)S(1)} %reshape.122, s32[1]{0:T(128)} %bitcast.12, s32[1]{0:T(128)} %bitcast.11), kind=kLoop, calls=%fused_computation.45 | loop fusion | flops 772 | bytes 3088 | tf_op jit(solution)/shard_map/concatenate | solution.py:470
  55.6 1.1 pad_maximum_fusion
  56.7 10.8 %all-to-all-done.1 = bf16[16,128,128]{2,1,0:T(8,128)(2,1)S(1)} async-done(((bf16[16,128,128]{2,1,0:T(8,128)(2,1)}), bf16[16,128,128]{2,1,0:T(8,128)(2,1)S(1)}, u32[]{:S(2)}, u32[]{:S(2)}) %all-to-all-start.1) | async-done | bytes 524320 | tf_op jit(solution)/shard_map/all_to_all | solution.py:533
  67.5 0.8 copy-done.5
  68.3 11.9 %segments.1 = bf16[16,136,128]{2,1,0:T(8,128)(2,1)} custom-call(s32[386]{0:T(512)} %pad_add_fusion.1.info_ref, s32[32,128]{1,0:T(8,128)} %bitcast.51, bf16[2048,128]{1,0:T(8,128)(2,1)} %bitcast.46, bf16[2,16,64,128]{3,2,1,0:T(8,128)(2,1)} %get-tuple-element.90.ahead_ref, bf16[2,16,64,128]{3,2,1,0:T(8,128)(2,1)} %get-tuple-element.91.behind_ref, ...), custom_call_target="tpu_custom_call" | custom-call | flops 8589934592 | bytes 12582912 | tf_op jit(solution)/shard_map/segments/pallas_call | solution.py:614
  80.2 25.5 %all_to_all.20.ret_ref = bf16[16,136,128]{2,1,0:T(8,128)(2,1)S(1)} all-to-all(bf16[16,136,128]{2,1,0:T(8,128)(2,1)} %segments.1), channel_id=1, replica_groups=mesh['slab'=16,'col'=2] {'slab'}, dimensions={0} | all-to-all | bytes 1114112 | tf_op jit(solution)/shard_map/all_to_all | solution.py:533
  105.8 1.2 %collective-permute-done.3.nbr_ref = bf16[136,128]{1,0:T(8,128)(2,1)S(1)} collective-permute-done((bf16[136,128]{1,0:T(8,128)(2,1)S(1)}, bf16[136,128]{1,0:T(8,128)(2,1)S(1)}, u32[]{:S(2)}, u32[]{:S(2)}) %collective-permute-start.3) | collective-permute-done | bytes 34848 | tf_op jit(solution)/shard_map/ppermute | solution.py:647
  107.0 0.6 copy-done.8
  107.6 10.1 %smooth_last.1 = f32[128,2048]{1,0:T(8,128)} custom-call(bf16[16,136,128]{2,1,0:T(8,128)(2,1)} %copy-done.1, bf16[136,128]{1,0:T(8,128)(2,1)} %copy-done.8, f32[17,160,128]{2,1,0:T(8,128)} %get-tuple-element.55.fn_in, f32[17,160,128]{2,1,0:T(8,128)} %get-tuple-element.56.fw_in, f32[128,2048]{1,0:T(8,128)} %dir_in.3, s32[128,2048]{1,0:T(8,128)} %mask_in.3), custom_call_target="tpu_custom_call" | custom-call | flops 40000000 | bytes 8388608 | tf_op jit(solution)/shard_map/smooth_last/pallas_call | solution.py:648
  (51 shorter events, 2.5 us)
Async XLA Ops:
  1.0 4.2 %collective-permute-start = (f32[2,128,128]{2,1,0:T(8,128)S(1)}, f32[2,128,128]{2,1,0:T(8,128)S(1)}, u32[]{:S(2)}, u32[]{:S(2)}) collective-permute-start(f32[2,128,128]{2,1,0:T(8,128)S(1)} %pad_maximum_fusion.2), channel_id=1, source_target_pairs={{0,1},{1,0},{2,3},{3,2},{4,5},{5,4},{6,7},{7,6},{8,9},{9,8},{10,11... | collective-permute-start | bytes 393224 | tf_op jit(solution)/shard_map/ppermute | solution.py:511
  5.3 5.5 %copy-start.3 = (f32[2,128,128]{2,1,0:T(8,128)}, f32[2,128,128]{2,1,0:T(8,128)S(1)}, u32[]{:S(2)}) copy-start(f32[2,128,128]{2,1,0:T(8,128)S(1)} %broadcast_select_fusion.nbr_ref) | copy-start | bytes 393220
  5.3 5.4 %collective-permute-start.1 = (f32[8,2176]{1,0:T(8,128)S(1)}, f32[8,2176]{1,0:T(8,128)S(1)}, u32[]{:S(2)}, u32[]{:S(2)}) collective-permute-start(f32[8,2176]{1,0:T(8,128)S(1)} %get-tuple-element.80), channel_id=1, source_target_pairs={{0,2},{2,0},{4,6},{6,4},{8,10},{10,8},{12,14},{14,12},{16,18},{18,... | collective-permute-start | bytes 208904 | tf_op jit(solution)/shard_map/ppermute | solution.py:530
  7.9 2.9 %collective-permute-start.2 = (f32[8,2176]{1,0:T(8,128)S(1)}, f32[8,2176]{1,0:T(8,128)S(1)}, u32[]{:S(2)}, u32[]{:S(2)}) collective-permute-start(f32[8,2176]{1,0:T(8,128)S(1)} %get-tuple-element.79), channel_id=1, source_target_pairs={{2,4},{6,8},{10,12},{14,16},{18,20},{22,24},{26,28},{4,2},{8,6},{1... | collective-permute-start | bytes 208904 | tf_op jit(solution)/shard_map/ppermute | solution.py:529
  8.6 13.9 %copy-start.10 = (s32[128,2]{0,1:T(2,128)S(1)}, s32[128,2]{0,1:T(2,128)}, u32[]{:S(2)}) copy-start(s32[128,2]{0,1:T(2,128)} %param.15) | copy-start | bytes 3076
  8.6 13.9 %copy-start.9 = (s32[256]{0:T(256)S(1)}, s32[256]{0:T(256)}, u32[]{:S(2)}) copy-start(s32[256]{0:T(256)} %owned_in.1) | copy-start | bytes 3076
  8.6 16.5 %copy-start = (f32[8,2048]{1,0:T(8,128)S(1)}, f32[8,2048]{1,0:T(8,128)}, u32[]{:S(2)}) copy-start(f32[8,2048]{1,0:T(8,128)} %scale_ref.1) | copy-start | bytes 196612
  10.7 0.6 copy-start.6
  11.4 0.6 copy-start.7
  25.1 28.1 %copy-start.2 = (bf16[16,64,64]{2,1,0:T(8,128)(2,1)S(1)}, bf16[16,64,64]{2,1,0:T(8,128)(2,1)}, u32[]{:S(2)}) copy-start(bf16[16,64,64]{2,1,0:T(8,128)(2,1)} %param.17) | copy-start | bytes 393220
  25.1 24.1 %all-to-all-start.2 = ((f32[64,1,2048]{2,1,0:T(1,128)}), f32[64,1,2048]{2,1,0:T(1,128)S(1)}, u32[]{:S(2)}, u32[]{:S(2)}) async-start(f32[64,1,2048]{2,1,0:T(1,128)} %outbox.1), calls=%async_computation.2 | async-start | bytes 1048576 | tf_op jit(solution)/shard_map/all_to_all | solution.py:533
  49.2 6.4 %copy-start.4 = (f32[64,1,2048]{2,1,0:T(1,128)}, f32[64,1,2048]{2,1,0:T(1,128)S(1)}, u32[]{:S(2)}) copy-start(f32[64,1,2048]{2,1,0:T(1,128)S(1)} %all-to-all-done.2.few_ref) | copy-start | bytes 1572868
  49.2 18.2 %all-to-all-start.1 = ((bf16[16,128,128]{2,1,0:T(8,128)(2,1)}), bf16[16,128,128]{2,1,0:T(8,128)(2,1)S(1)}, u32[]{:S(2)}, u32[]{:S(2)}) async-start(bf16[16,128,128]{2,1,0:T(8,128)(2,1)} %get-tuple-element.52), calls=%async_computation.1 | async-start | bytes 1048576 | tf_op jit(solution)/shard_map/all_to_all | solution.py:533
  67.5 0.8 copy-start.5
  105.7 1.3 %copy-start.1 = (bf16[16,136,128]{2,1,0:T(8,128)(2,1)}, bf16[16,136,128]{2,1,0:T(8,128)(2,1)S(1)}, u32[]{:S(2)}) copy-start(bf16[16,136,128]{2,1,0:T(8,128)(2,1)S(1)} %all_to_all.20.ret_ref) | copy-start | bytes 1671172
  105.7 1.3 %collective-permute-start.3 = (bf16[136,128]{1,0:T(8,128)(2,1)S(1)}, bf16[136,128]{1,0:T(8,128)(2,1)S(1)}, u32[]{:S(2)}, u32[]{:S(2)}) collective-permute-start(bf16[136,128]{1,0:T(8,128)(2,1)S(1)} %fusion.5), channel_id=1, source_target_pairs={{0,1},{1,0},{2,3},{3,2},{4,5},{5,4},{6,7},{7,6},{8,9},{9,8},{10,11... | collective-permute-start | bytes 104456 | tf_op jit(solution)/shard_map/ppermute | solution.py:647
  107.0 0.6 copy-start.8

commit v5 on v4

--- a/solution.py
+++ b/solution.py
@@ -275,17 +275,18 @@
 
 
 def segments_kernel(
-    info_ref, index_ref, x_ref, ahead_ref, behind_ref, prec_in, few_ref, all_ref,
-    out_ref, prec_ref, turned, weighted, zbuf, scale_row, adj, grid, prec_sem, scale_sem,
-    *, width, sizes,
+    count_ref, full_ref, seg_ref, few_row_ref, all_row_ref, index_ref, x_ref, table_ref,
+    prec_in, few_ref, all_ref, out_ref,
+    prec_ref, ahead_ref, behind_ref, turned, weighted, zbuf, scale_row, adj, grid,
+    prec_sem, scale_sem, *, width, sizes,
 ):
     parts, chunk, lanes = out_ref.shape
     order = prec_ref.shape[0]
     blocks = order // lanes
     pieces = order // width
     batch = sizes[-1]
-    count = info_ref[0]
-    full = info_ref[1]
+    count = count_ref[0]
+    full = full_ref[0]
 
     def prec_copy(i):
         cols = pl.ds(pl.multiple_of(i * width, width), width)
@@ -300,11 +301,11 @@
 
             @pl.when((e < count) & (full == 0))
             def _(e=e, j=j):
-                scale_copy(few_ref, info_ref[3 + 3 * e], j).start()
+                scale_copy(few_ref, few_row_ref[e], j).start()
 
             @pl.when((e < count) & (full != 0))
             def _(e=e, j=j):
-                scale_copy(all_ref, info_ref[4 + 3 * e], j).start()
+                scale_copy(all_ref, all_row_ref[e], j).start()
 
             @pl.when(e >= count)
             def _(j=j):
@@ -313,6 +314,16 @@
     prec_copy(0).start()
     fetch(0)
     prec_copy(1).start()
+
+    def side(b, carry):
+        block = table_ref[b].astype(jnp.float32)
+        blank = jnp.zeros_like(block)
+        for ref, value in ((ahead_ref, block.T), (behind_ref, block)):
+            ref[0, b] = jnp.concatenate([value, blank], axis=1).astype(jnp.bfloat16)
+            ref[1, b] = jnp.concatenate([blank, value], axis=1).astype(jnp.bfloat16)
+        return carry
+
+    lax.fori_loop(0, table_ref.shape[0], side, 0, unroll=4)
 
     def turn(q, carry):
         part = pl.ds(pl.multiple_of(q * lanes, lanes), lanes)
@@ -326,7 +337,7 @@
         ids = []
         for j in range(size):
             e = g * batch + j
-            ids.append(info_ref[2 + 3 * jnp.minimum(e, count - 1)])
+            ids.append(seg_ref[jnp.minimum(e, count - 1)])
 
             @pl.when(j < live)
             def _(j=j):
@@ -363,13 +374,16 @@
             def _():
                 prec_copy(i + 2).start()
 
-            prod = jnp.dot(
-                weighted[: size * lanes, :], prec_ref[:, cols],
-                preferred_element_type=jnp.float32,
-            )
-            for j in range(size):
-                rows = slice(j * lanes, (j + 1) * lanes)
-                zbuf[rows, cols] = (prod[rows] * scale_row[j, :, cols]).astype(jnp.bfloat16)
+            cuts = (0, size) if size <= 8 else (0, size // 2, size)
+            for low, high in zip(cuts, cuts[1:]):
+                prod = jnp.dot(
+                    weighted[low * lanes : high * lanes, :], prec_ref[:, cols],
+                    preferred_element_type=jnp.float32,
+                )
+                for j in range(low, high):
+                    value = prod[(j - low) * lanes : (j - low + 1) * lanes]
+                    rows = slice(j * lanes, (j + 1) * lanes)
+                    zbuf[rows, cols] = (value * scale_row[j, :, cols]).astype(jnp.bfloat16)
             return carry
 
         lax.fori_loop(0, pieces, product, 0)
@@ -464,20 +478,8 @@
         src_slab * CAP + jnp.minimum(place, CAP - 1),
         src_slab * seg_max + slot_ids % seg_max,
     ]
-    listed = jnp.stack(
-        [jnp.sum(jnp.where(pick, col[None, :], 0), axis=1) for col in columns], axis=1
-    )
-    info = jnp.concatenate(
-        [count[None], overflow.astype(jnp.int32)[None], listed.reshape(-1)]
-    )
-    return info, overflow, owner_slab, used, slot_in
-
-
-def sides(table):
-    empty = jnp.zeros_like(table)
-    return jnp.stack(
-        [jnp.concatenate([table, empty], axis=2), jnp.concatenate([empty, table], axis=2)]
-    )
+    listed = [jnp.sum(jnp.where(pick, col[None, :], 0), axis=1) for col in columns]
+    return count, listed, overflow, owner_slab, used, slot_in
 
 
 def per_device(
@@ -485,6 +487,7 @@
     interp_index, interp_table, precision, obs_scale,
 ):
     rows_dev, cols_dev = direction.shape
+    blocks, tile_r, _ = interp_table.shape
     order = precision.shape[0]
     _, seg_tiles = interp_index.shape
     seg_max = obs_scale.shape[0]
@@ -547,6 +550,11 @@
         name="outbox",
     )(owned_segments, seg_anchor.T, obs_scale)
     few = swap(scales_out)
+
+    count, listed, overflow, owner_slab, used, slot_in = owner_tables(
+        owned_segments, seg_anchor, seg_tiles, seg_max, dev_count, col_count, span,
+        col_tiles, my_device,
+    )
 
     tiles = col_tiles + 1
     height = rows_dev + 2 * PAD
@@ -570,18 +578,7 @@
         name="smooth_first",
     )(direction, kappa, land_mask, nbr, got_a, got_b)
 
-    smoothed, owned_segments, seg_anchor, interp_index, interp_table, obs_scale = (
-        lax.optimization_barrier(
-            (smoothed, owned_segments, seg_anchor, interp_index, interp_table, obs_scale)
-        )
-    )
     gathered = swap(smoothed, groups)
-
-    info, overflow, owner_slab, used, slot_in = owner_tables(
-        owned_segments, seg_anchor, seg_tiles, seg_max, dev_count, col_count, span,
-        col_tiles, my_device,
-    )
-    ahead, behind = sides(interp_table.transpose(0, 2, 1)), sides(interp_table)
 
     my_owner = lax.dynamic_slice_in_dim(owner_slab, my_device * seg_max, seg_max)
     my_used = lax.dynamic_slice_in_dim(used, my_device * seg_max, seg_max)
@@ -608,17 +605,18 @@
 
     chunk = rows_dev + 2 * SWEEPS
     width = order // 4
-    sizes = (1, 2, 3, 4, 6, 8, 10)
+    sizes = tuple(range(1, 11))
     batch = sizes[-1]
 
     returning = pl.pallas_call(
         functools.partial(segments_kernel, width=width, sizes=sizes),
         out_shape=jax.ShapeDtypeStruct((span, chunk, lanes), jnp.bfloat16),
-        in_specs=[smem_spec(), smem_spec(), vmem_spec(), vmem_spec(), vmem_spec()]
-        + [hbm_spec()] * 3,
+        in_specs=[smem_spec()] * 6 + [vmem_spec()] * 2 + [hbm_spec()] * 3,
         out_specs=vmem_spec(),
         scratch_shapes=[
             pltpu.VMEM((order, order), jnp.bfloat16),
+            pltpu.VMEM((2, blocks, tile_r, 2 * tile_r), jnp.bfloat16),
+            pltpu.VMEM((2, blocks, tile_r, 2 * tile_r), jnp.bfloat16),
             pltpu.VMEM((lanes, order), jnp.bfloat16),
             pltpu.VMEM((batch * lanes, order), jnp.bfloat16),
             pltpu.VMEM((batch * lanes, order), jnp.bfloat16),
@@ -634,8 +632,8 @@
         ),
         name="segments",
     )(
-        info, interp_index.T, gathered.reshape(order, lanes),
-        ahead, behind, precision, few, everything,
+        count.reshape(1), overflow.astype(jnp.int32).reshape(1), *listed, interp_index.T,
+        gathered.reshape(order, lanes), interp_table, precision, few, everything,
     )
 
     returned = swap(returning, groups)

time: 119 us -> 114 us (0.958)
  waiting for transfers between devices: 28.1 us -> 20.3 us
  starting transfers between devices: 17.4 us -> 22.1 us
    all_to_all x2, waiting for transfers between devices: 24.7 us -> 12.9 us  [swap(): lax.all_to_all(array, 'slab', split_axis=0, concat_axis=0, tiled=True, ax...]
    ppermute x1, waiting for transfers between devices: 2.14 us -> 6.16 us  [per_device(): lax.ppermute(jnp.where(even, last_rows, first_rows), 'slab', pairs_a)]
    all_to_all x2, starting transfers between devices: 13.6 us -> 16.1 us  [swap(): lax.all_to_all(array, 'slab', split_axis=0, concat_axis=0, tiled=True, ax...]
    ppermute x1, starting transfers between devices: 2.55 us -> 4.69 us  [per_device(): lax.ppermute(jnp.where(even, last_rows, first_rows), 'slab', pairs_a)]
    concatenate x1 -> x0, other arithmetic: 1.3 us -> none  [owner_tables(): jnp.concatenate([count[None], overflow.astype(jnp.int32)[None], listed.re...]
    unnamed x22 -> x18, local copies, waits for them, and re-layouts: 2.67 us -> 2.05 us
  transfers between devices with their start and end apart: 6 -> 6, of which waited for: 4 -> 3; matrix products, arithmetic and copies ran while one was open for 4% -> 6% of each run, Pallas kernels for 2% -> 11%
where the time goes in v5:
time: 114 us; the launch traced here: 113 us
  Pallas kernels  35.8 us (31%)
  blocking collectives  24.5 us (21%)
  starting transfers between devices  22.1 us (19%)
  waiting for transfers between devices  20.3 us (18%)
  other arithmetic  6.39 us (6%)
  local copies, waits for them, and re-layouts  3.32 us (3%)
    all_to_all x1, blocking collectives, swap(): lax.all_to_all(array, 'slab', split_axis=0, concat_axis=0, tiled=True, ax...  24.5 us
    all_to_all x2, starting transfers between devices, swap(): lax.all_to_all(array, 'slab', split_axis=0, concat_axis=0, tiled=True, ax...  16.1 us
    all_to_all x2, waiting for transfers between devices, swap(): lax.all_to_all(array, 'slab', split_axis=0, concat_axis=0, tiled=True, ax...  12.9 us
    pallas_call x1, Pallas kernels, per_device(): pl.pallas_call(functools.partial(segments_kernel, width=width, sizes=size...  12.6 us
    pallas_call x1, Pallas kernels, per_device(): pl.pallas_call(smooth_first_kernel, out_shape=(jax.ShapeDtypeStruct((col_...  10.5 us
    pallas_call x1, Pallas kernels, per_device(): pl.pallas_call(smooth_last_kernel, out_shape=jax.ShapeDtypeStruct((rows_d...  10.1 us
    ppermute x1, waiting for transfers between devices, per_device(): lax.ppermute(jnp.where(even, last_rows, first_rows), 'slab', pairs_a)  6.16 us
    ppermute x1, starting transfers between devices, per_device(): lax.ppermute(jnp.where(even, last_rows, first_rows), 'slab', pairs_a)  4.69 us
  transfers between devices with their start and end apart: 6, of which 3 were waited for; matrix products, arithmetic and copies ran while one was open for 6% of the time, Pallas kernels for 11%

profile of v5, /device:TPU:0, one launch (start us, length us, event | category | flops | bytes accessed | tf_op | source)
XLA Modules:
  0.0 113.4 jit_solution(16512867351335972084)
XLA Ops:
  0.0 1.1 multiply_bitcast_fusion.1
  1.1 0.6 collective-permute-start
  1.6 0.8 slice_bitcast_fusion.4
  2.4 0.9 select_reduce_fusion.5
  3.3 0.7 convert_bitcast_fusion
  4.4 0.7 minimum_add_fusion
  5.9 2.6 %outbox.1 = f32[64,1,2048]{2,1,0:T(1,128)} custom-call(s32[256]{0:T(256)} %owned_in.1, s32[2,128]{1,0:T(2,128)} %bitcast.34, f32[8,2048]{1,0:T(8,128)} %scale_ref.1), custom_call_target="tpu_custom_call" | custom-call | tf_op jit(solution)/shard_map/outbox/pallas_call | solution.py:540
  8.5 7.9 %all-to-all-start.2 = ((f32[64,1,2048]{2,1,0:T(1,128)}), f32[64,1,2048]{2,1,0:T(1,128)S(1)}, u32[]{:S(2)}, u32[]{:S(2)}) async-start(f32[64,1,2048]{2,1,0:T(1,128)} %outbox.1), calls=%async_computation.2 | async-start | bytes 1048576 | tf_op jit(solution)/shard_map/all_to_all | solution.py:536
  16.4 1.0 convert_multiply_fusion.1
  17.5 0.7 collective-permute-start.2
  18.2 4.7 %collective-permute-start.1 = (f32[8,2176]{1,0:T(8,128)S(1)}, f32[8,2176]{1,0:T(8,128)S(1)}, u32[]{:S(2)}, u32[]{:S(2)}) collective-permute-start(f32[8,2176]{1,0:T(8,128)S(1)} %get-tuple-element.64), channel_id=1, source_target_pairs={{0,2},{2,0},{4,6},{6,4},{8,10},{10,8},{12,14},{14,12},{16,18},{18,... | collective-permute-start | bytes 208904 | tf_op jit(solution)/shard_map/ppermute | solution.py:533
  22.9 6.2 %collective-permute-done.1.got_a_ref = f32[8,2176]{1,0:T(8,128)S(1)} collective-permute-done((f32[8,2176]{1,0:T(8,128)S(1)}, f32[8,2176]{1,0:T(8,128)S(1)}, u32[]{:S(2)}, u32[]{:S(2)}) %collective-permute-start.1) | collective-permute-done | bytes 69664 | tf_op jit(solution)/shard_map/ppermute | solution.py:533
  29.1 0.6 copy-done.6
  29.7 10.5 %smooth_first.1 = (bf16[16,128,128]{2,1,0:T(8,128)(2,1)}, f32[17,160,128]{2,1,0:T(8,128)}, f32[17,160,128]{2,1,0:T(8,128)}) custom-call(f32[128,2048]{1,0:T(8,128)} %dir_in.3, f32[128,2048]{1,0:T(8,128)} %kap_in.1, s32[128,2048]{1,0:T(8,128)} %mask_in.3, f32[2,128,128]{2,1,0:T(8,128)} %copy-done.2, f32[8,2176]{1,0:T(8,128)} %copy-done.6, f32[8,2176]{1,0:T(8,128)} %copy-done.5), custom_call_target="tpu_custom_call" | custom-call | flops 40000000 | bytes 8388608 | tf_op jit(solution)/shard_map/smooth_first/pallas_call | solution.py:565
  40.2 8.2 %all-to-all-start.1 = ((bf16[16,128,128]{2,1,0:T(8,128)(2,1)}), bf16[16,128,128]{2,1,0:T(8,128)(2,1)S(1)}, u32[]{:S(2)}, u32[]{:S(2)}) async-start(bf16[16,128,128]{2,1,0:T(8,128)(2,1)} %get-tuple-element.42), calls=%async_computation.1 | async-start | bytes 1048576 | tf_op jit(solution)/shard_map/all_to_all | solution.py:536
  48.8 0.6 convert_reduce_fusion.1
  49.7 0.7 select_reduce_fusion.1
  50.4 12.9 %all-to-all-done.1 = bf16[16,128,128]{2,1,0:T(8,128)(2,1)S(1)} async-done(((bf16[16,128,128]{2,1,0:T(8,128)(2,1)}), bf16[16,128,128]{2,1,0:T(8,128)(2,1)S(1)}, u32[]{:S(2)}, u32[]{:S(2)}) %all-to-all-start.1) | async-done | bytes 524320 | tf_op jit(solution)/shard_map/all_to_all | solution.py:536
  63.3 0.8 copy-done.4
  64.1 12.6 %segments.1 = bf16[16,136,128]{2,1,0:T(8,128)(2,1)} custom-call(s32[1]{0:T(128)} %bitcast.5.count_ref, s32[1]{0:T(128)} %bitcast.6.full_ref, s32[128]{0:T(128)} %get-tuple-element.47.seg_ref, s32[128]{0:T(128)} %get-tuple-element.46.few_row_ref, s32[128]{0:T(128)} %get-tuple-element.45.all_row_ref, s32[32,128]{1,0:T(8,128)} %bitcast.35, ...), custom_call_target="tpu_custom_call" | custom-call | flops 8589934592 | bytes 12582912 | tf_op jit(solution)/shard_map/segments/pallas_call | solution.py:611
  76.7 24.5 %all_to_all.20.ret_ref = bf16[16,136,128]{2,1,0:T(8,128)(2,1)S(1)} all-to-all(bf16[16,136,128]{2,1,0:T(8,128)(2,1)} %segments.1), channel_id=1, replica_groups=mesh['slab'=16,'col'=2] {'slab'}, dimensions={0} | all-to-all | bytes 1114112 | tf_op jit(solution)/shard_map/all_to_all | solution.py:536
  101.3 1.2 %collective-permute-done.3.nbr_ref = bf16[136,128]{1,0:T(8,128)(2,1)S(1)} collective-permute-done((bf16[136,128]{1,0:T(8,128)(2,1)S(1)}, bf16[136,128]{1,0:T(8,128)(2,1)S(1)}, u32[]{:S(2)}, u32[]{:S(2)}) %collective-permute-start.3) | collective-permute-done | bytes 34848 | tf_op jit(solution)/shard_map/ppermute | solution.py:645
  102.5 0.6 copy-done.7
  103.1 10.1 %smooth_last.1 = f32[128,2048]{1,0:T(8,128)} custom-call(bf16[16,136,128]{2,1,0:T(8,128)(2,1)} %copy-done.1, bf16[136,128]{1,0:T(8,128)(2,1)} %copy-done.7, f32[17,160,128]{2,1,0:T(8,128)} %get-tuple-element.43.fn_in, f32[17,160,128]{2,1,0:T(8,128)} %get-tuple-element.44.fw_in, f32[128,2048]{1,0:T(8,128)} %dir_in.3, s32[128,2048]{1,0:T(8,128)} %mask_in.3), custom_call_target="tpu_custom_call" | custom-call | flops 40000000 | bytes 8388608 | tf_op jit(solution)/shard_map/smooth_last/pallas_call | solution.py:646
  (39 shorter events, 1.3 us)
Async XLA Ops:
  0.0 8.4 %copy-start = (f32[8,2048]{1,0:T(8,128)S(1)}, f32[8,2048]{1,0:T(8,128)}, u32[]{:S(2)}) copy-start(f32[8,2048]{1,0:T(8,128)} %scale_ref.1) | copy-start | bytes 196612
  1.1 16.4 %collective-permute-start = (f32[2,128,128]{2,1,0:T(8,128)S(1)}, f32[2,128,128]{2,1,0:T(8,128)S(1)}, u32[]{:S(2)}, u32[]{:S(2)}) collective-permute-start(f32[2,128,128]{2,1,0:T(8,128)S(1)} %pad_maximum_fusion), channel_id=1, source_target_pairs={{0,1},{1,0},{2,3},{3,2},{4,5},{5,4},{6,7},{7,6},{8,9},{9,8},{10,11... | collective-permute-start | bytes 393224 | tf_op jit(solution)/shard_map/ppermute | solution.py:514
  8.5 31.7 %all-to-all-start.2 = ((f32[64,1,2048]{2,1,0:T(1,128)}), f32[64,1,2048]{2,1,0:T(1,128)S(1)}, u32[]{:S(2)}, u32[]{:S(2)}) async-start(f32[64,1,2048]{2,1,0:T(1,128)} %outbox.1), calls=%async_computation.2 | async-start | bytes 1048576 | tf_op jit(solution)/shard_map/all_to_all | solution.py:536
  17.5 11.6 %copy-start.2 = (f32[2,128,128]{2,1,0:T(8,128)}, f32[2,128,128]{2,1,0:T(8,128)S(1)}, u32[]{:S(2)}) copy-start(f32[2,128,128]{2,1,0:T(8,128)S(1)} %broadcast_select_fusion.nbr_ref) | copy-start | bytes 393220
  17.5 5.4 %collective-permute-start.2 = (f32[8,2176]{1,0:T(8,128)S(1)}, f32[8,2176]{1,0:T(8,128)S(1)}, u32[]{:S(2)}, u32[]{:S(2)}) collective-permute-start(f32[8,2176]{1,0:T(8,128)S(1)} %get-tuple-element.63), channel_id=1, source_target_pairs={{2,4},{6,8},{10,12},{14,16},{18,20},{22,24},{26,28},{4,2},{8,6},{1... | collective-permute-start | bytes 208904 | tf_op jit(solution)/shard_map/ppermute | solution.py:532
  18.2 31.4 %copy-start.8 = (s32[256]{0:T(256)S(1)}, s32[256]{0:T(256)}, u32[]{:S(2)}) copy-start(s32[256]{0:T(256)} %owned_in.1) | copy-start | bytes 3076
  18.2 10.9 %collective-permute-start.1 = (f32[8,2176]{1,0:T(8,128)S(1)}, f32[8,2176]{1,0:T(8,128)S(1)}, u32[]{:S(2)}, u32[]{:S(2)}) collective-permute-start(f32[8,2176]{1,0:T(8,128)S(1)} %get-tuple-element.64), channel_id=1, source_target_pairs={{0,2},{2,0},{4,6},{6,4},{8,10},{10,8},{12,14},{14,12},{16,18},{18,... | collective-permute-start | bytes 208904 | tf_op jit(solution)/shard_map/ppermute | solution.py:533
  22.9 6.2 %copy-start.5 = (f32[8,2176]{1,0:T(8,128)}, f32[8,2176]{1,0:T(8,128)S(1)}, u32[]{:S(2)}) copy-start(f32[8,2176]{1,0:T(8,128)S(1)} %collective-permute-done.2.got_b_ref) | copy-start | bytes 208900
  29.1 0.6 copy-start.6
  40.2 23.1 %copy-start.3 = (f32[64,1,2048]{2,1,0:T(1,128)}, f32[64,1,2048]{2,1,0:T(1,128)S(1)}, u32[]{:S(2)}) copy-start(f32[64,1,2048]{2,1,0:T(1,128)S(1)} %all-to-all-done.2.few_ref) | copy-start | bytes 1572868
  40.2 23.1 %all-to-all-start.1 = ((bf16[16,128,128]{2,1,0:T(8,128)(2,1)}), bf16[16,128,128]{2,1,0:T(8,128)(2,1)S(1)}, u32[]{:S(2)}, u32[]{:S(2)}) async-start(bf16[16,128,128]{2,1,0:T(8,128)(2,1)} %get-tuple-element.42), calls=%async_computation.1 | async-start | bytes 1048576 | tf_op jit(solution)/shard_map/all_to_all | solution.py:536
  63.3 0.8 copy-start.4
  101.2 1.3 %copy-start.1 = (bf16[16,136,128]{2,1,0:T(8,128)(2,1)}, bf16[16,136,128]{2,1,0:T(8,128)(2,1)S(1)}, u32[]{:S(2)}) copy-start(bf16[16,136,128]{2,1,0:T(8,128)(2,1)S(1)} %all_to_all.20.ret_ref) | copy-start | bytes 1671172
  101.3 1.3 %collective-permute-start.3 = (bf16[136,128]{1,0:T(8,128)(2,1)S(1)}, bf16[136,128]{1,0:T(8,128)(2,1)S(1)}, u32[]{:S(2)}, u32[]{:S(2)}) collective-permute-start(bf16[136,128]{1,0:T(8,128)(2,1)S(1)} %fusion.5), channel_id=1, source_target_pairs={{0,1},{1,0},{2,3},{3,2},{4,5},{5,4},{6,7},{7,6},{8,9},{9,8},{10,11... | collective-permute-start | bytes 104456 | tf_op jit(solution)/shard_map/ppermute | solution.py:645
  102.5 0.6 copy-start.7

commit v6 on v5

--- a/solution.py
+++ b/solution.py
@@ -197,18 +197,14 @@
 
 
 def smooth_last_kernel(
-    ret_ref, nbr_ref, fn_in, fw_in, dir_in, mask_in, out_ref,
-    own_ref, fn_ref, fw_ref, fe_ref, dir_ref, mask_ref, u0, u1, load_sems, sems,
+    ret_ref, nbr_ref, fn_ref, fw_ref, dir_in, mask_in, out_ref,
+    own_ref, fe_ref, dir_ref, mask_ref, u0, u1, load_sems,
 ):
     tiles, _, lanes = u0.shape
-    faces = [
-        pltpu.make_async_copy(ref, buf, sems.at[i])
-        for i, (ref, buf) in enumerate(((fn_in, fn_ref), (fw_in, fw_ref)))
-    ]
     loads = sum(
         column_chunks((dir_in, mask_in), (dir_ref, mask_ref), load_sems, tiles - 1, lanes), []
     )
-    for load in faces + loads:
+    for load in loads:
         load.start()
     own, chunk = dir_ref.shape[0], ret_ref.shape[1]
     rows = own + 2 * HALO
@@ -226,8 +222,6 @@
 
     lax.fori_loop(0, tiles - 1, fill, 0)
     put(tiles - 1, nbr_ref[...])
-    for load in faces:
-        load.wait()
     derive(tiles, rows, own_ref, fn_ref, fw_ref, fe_ref)
 
     def finish(c, row, value):
@@ -551,11 +545,6 @@
     )(owned_segments, seg_anchor.T, obs_scale)
     few = swap(scales_out)
 
-    count, listed, overflow, owner_slab, used, slot_in = owner_tables(
-        owned_segments, seg_anchor, seg_tiles, seg_max, dev_count, col_count, span,
-        col_tiles, my_device,
-    )
-
     tiles = col_tiles + 1
     height = rows_dev + 2 * PAD
     buf = pltpu.VMEM((tiles, height, lanes), jnp.float32)
@@ -574,11 +563,20 @@
         + [pltpu.VMEM((col_tiles, rows_dev, lanes), jnp.bfloat16)]
         + [buf] * 7
         + [pltpu.SemaphoreType.DMA((3, CHUNKS)), pltpu.SemaphoreType.DMA((4,))],
+        compiler_params=pltpu.CompilerParams(vmem_limit_bytes=58 << 20),
         cost_estimate=pl.CostEstimate(flops=40000000, bytes_accessed=8 << 20, transcendentals=0),
         name="smooth_first",
     )(direction, kappa, land_mask, nbr, got_a, got_b)
 
+    smoothed, owned_segments, seg_anchor, obs_scale = lax.optimization_barrier(
+        (smoothed, owned_segments, seg_anchor, obs_scale)
+    )
     gathered = swap(smoothed, groups)
+
+    count, listed, overflow, owner_slab, used, slot_in = owner_tables(
+        owned_segments, seg_anchor, seg_tiles, seg_max, dev_count, col_count, span,
+        col_tiles, my_device,
+    )
 
     my_owner = lax.dynamic_slice_in_dim(owner_slab, my_device * seg_max, seg_max)
     my_used = lax.dynamic_slice_in_dim(used, my_device * seg_max, seg_max)
@@ -626,7 +624,7 @@
             pltpu.SemaphoreType.DMA((order // width,)),
             pltpu.SemaphoreType.DMA((batch,)),
         ],
-        compiler_params=pltpu.CompilerParams(vmem_limit_bytes=57 << 20),
+        compiler_params=pltpu.CompilerParams(vmem_limit_bytes=45 << 20),
         cost_estimate=pl.CostEstimate(
             flops=8 * 2 * order * order * lanes, bytes_accessed=12 << 20, transcendentals=0
         ),
@@ -646,11 +644,12 @@
     return pl.pallas_call(
         smooth_last_kernel,
         out_shape=jax.ShapeDtypeStruct((rows_dev, cols_dev), jnp.float32),
-        in_specs=[vmem_spec()] * 2 + [hbm_spec()] * 4,
+        in_specs=[vmem_spec()] * 4 + [hbm_spec()] * 2,
         out_specs=vmem_spec(),
-        scratch_shapes=[buf] * 4
+        scratch_shapes=[buf] * 2
         + [own_float, own_int, buf, buf]
-        + [pltpu.SemaphoreType.DMA((2, CHUNKS)), pltpu.SemaphoreType.DMA((2,))],
+        + [pltpu.SemaphoreType.DMA((2, CHUNKS))],
+        compiler_params=pltpu.CompilerParams(vmem_limit_bytes=45 << 20),
         cost_estimate=pl.CostEstimate(flops=40000000, bytes_accessed=8 << 20, transcendentals=0),
         name="smooth_last",
     )(returned, border, fn, fw, direction, land_mask)

time: 114 us -> 113 us (level)
  blocking collectives: 24.5 us -> 47.9 us
  starting transfers between devices: 22.1 us -> 7.69 us
  waiting for transfers between devices: 20.3 us -> 16.2 us
  Pallas kernels: 35.8 us -> 31.9 us
  other arithmetic: 6.39 us -> 4.47 us
    all_to_all x1 -> x2, blocking collectives: 24.5 us -> 47.9 us  [swap(): lax.all_to_all(array, 'slab', split_axis=0, concat_axis=0, tiled=True, ax...]
    all_to_all x2 -> x1, starting transfers between devices: 16.1 us -> 3.86 us  [swap(): lax.all_to_all(array, 'slab', split_axis=0, concat_axis=0, tiled=True, ax...]
    ppermute x1, waiting for transfers between devices: 6.16 us -> 2.14 us  [per_device(): lax.ppermute(jnp.where(even, last_rows, first_rows), 'slab', pairs_a)]
    pallas_call x1, Pallas kernels: 10.1 us -> 6.99 us  [per_device(): pl.pallas_call(smooth_last_kernel, out_shape=jax.ShapeDtypeStruct((rows_d...]
    ppermute x1, starting transfers between devices: 4.69 us -> 2.55 us  [per_device(): lax.ppermute(jnp.where(even, last_rows, first_rows), 'slab', pairs_a)]
    all_to_all x2 -> x1, waiting for transfers between devices: 12.9 us -> 12.9 us  [swap(): lax.all_to_all(array, 'slab', split_axis=0, concat_axis=0, tiled=True, ax...]
  transfers between devices with their start and end apart: 6 -> 5, of which waited for: 3 -> 3; matrix products, arithmetic and copies ran while one was open for 6% -> 2% of each run, Pallas kernels for 11% -> 2%
where the time goes in v6:
time: 113 us; the launch traced here: 112 us
  blocking collectives  47.9 us (42%)
  Pallas kernels  31.9 us (28%)
  waiting for transfers between devices  16.2 us (14%)
  starting transfers between devices  7.69 us (7%)
  other arithmetic  4.47 us (4%)
  local copies, waits for them, and re-layouts  2.79 us (2%)
    all_to_all x2, blocking collectives, swap(): lax.all_to_all(array, 'slab', split_axis=0, concat_axis=0, tiled=True, ax...  47.9 us
    all_to_all x1, waiting for transfers between devices, swap(): lax.all_to_all(array, 'slab', split_axis=0, concat_axis=0, tiled=True, ax...  12.9 us
    pallas_call x1, Pallas kernels, per_device(): pl.pallas_call(functools.partial(segments_kernel, width=width, sizes=size...  11.9 us
    pallas_call x1, Pallas kernels, per_device(): pl.pallas_call(smooth_first_kernel, out_shape=(jax.ShapeDtypeStruct((col_...  10.5 us
    pallas_call x1, Pallas kernels, per_device(): pl.pallas_call(smooth_last_kernel, out_shape=jax.ShapeDtypeStruct((rows_d...  6.99 us
    all_to_all x1, starting transfers between devices, swap(): lax.all_to_all(array, 'slab', split_axis=0, concat_axis=0, tiled=True, ax...  3.86 us
    pallas_call x1, Pallas kernels, per_device(): pl.pallas_call(functools.partial(outbox_kernel, seg_tiles=seg_tiles, col_...  2.57 us
    ppermute x1, starting transfers between devices, per_device(): lax.ppermute(jnp.where(even, last_rows, first_rows), 'slab', pairs_a)  2.55 us
  transfers between devices with their start and end apart: 5, of which 3 were waited for; matrix products, arithmetic and copies ran while one was open for 2% of the time, Pallas kernels for 2%

profile of v6, /device:TPU:0, one launch (start us, length us, event | category | flops | bytes accessed | tf_op | source)
XLA Modules:
  0.0 112.1 jit_solution(5581461686362732625)
XLA Ops:
  0.0 1.0 multiply_bitcast_fusion.1
  1.0 0.6 collective-permute-start
  1.6 1.0 convert_multiply_fusion.1
  2.7 2.6 %outbox.1 = f32[64,1,2048]{2,1,0:T(1,128)} custom-call(s32[256]{0:T(256)} %owned_in.1, s32[2,128]{1,0:T(2,128)} %bitcast.35, f32[8,2048]{1,0:T(8,128)} %scale_ref.1), custom_call_target="tpu_custom_call" | custom-call | tf_op jit(solution)/shard_map/outbox/pallas_call | solution.py:534
  5.3 2.5 %collective-permute-start.1 = (f32[8,2176]{1,0:T(8,128)S(1)}, f32[8,2176]{1,0:T(8,128)S(1)}, u32[]{:S(2)}, u32[]{:S(2)}) collective-permute-start(f32[8,2176]{1,0:T(8,128)S(1)} %get-tuple-element.72), channel_id=1, source_target_pairs={{0,2},{2,0},{4,6},{6,4},{8,10},{10,8},{12,14},{14,12},{16,18},{18,... | collective-permute-start | bytes 208904 | tf_op jit(solution)/shard_map/ppermute | solution.py:527
  7.9 0.7 collective-permute-start.2
  8.6 2.1 %collective-permute-done.1.got_a_ref = f32[8,2176]{1,0:T(8,128)S(1)} collective-permute-done((f32[8,2176]{1,0:T(8,128)S(1)}, f32[8,2176]{1,0:T(8,128)S(1)}, u32[]{:S(2)}, u32[]{:S(2)}) %collective-permute-start.1) | collective-permute-done | bytes 69664 | tf_op jit(solution)/shard_map/ppermute | solution.py:527
  10.7 0.6 copy-done.9
  11.4 0.6 copy-done.10
  12.0 10.5 %smooth_first.1 = (bf16[16,128,128]{2,1,0:T(8,128)(2,1)}, f32[17,160,128]{2,1,0:T(8,128)}, f32[17,160,128]{2,1,0:T(8,128)}) custom-call(f32[128,2048]{1,0:T(8,128)} %dir_in.3, f32[128,2048]{1,0:T(8,128)} %kap_in.1, s32[128,2048]{1,0:T(8,128)} %mask_in.3, f32[2,128,128]{2,1,0:T(8,128)} %copy-done.8, f32[8,2176]{1,0:T(8,128)} %copy-done.9, f32[8,2176]{1,0:T(8,128)} %copy-done.10), custom_call_target="tpu_custom_call" | custom-call | flops 40000000 | bytes 8388608 | tf_op jit(solution)/shard_map/smooth_first/pallas_call | solution.py:554
  22.5 0.2 select_reduce_fusion.5
  23.2 0.7 minimum_add_fusion
  24.6 1.0 copy-done.7
  25.6 23.8 %all_to_all.20.few_ref = f32[64,1,2048]{2,1,0:T(1,128)S(1)} all-to-all(f32[64,1,2048]{2,1,0:T(1,128)S(1)} %copy-done.7), channel_id=1, replica_groups=mesh['slab'=16,'col'=2] {'slab'}, dimensions={0} | all-to-all | bytes 1048576 | tf_op jit(solution)/shard_map/all_to_all | solution.py:530
  49.3 3.9 %all-to-all-start.1 = ((bf16[16,128,128]{2,1,0:T(8,128)(2,1)}), bf16[16,128,128]{2,1,0:T(8,128)(2,1)S(1)}, u32[]{:S(2)}, u32[]{:S(2)}) async-start(bf16[16,128,128]{2,1,0:T(8,128)(2,1)} %get-tuple-element.49), calls=%async_computation.1 | async-start | bytes 1048576 | tf_op jit(solution)/shard_map/all_to_all | solution.py:530
  53.2 0.3 reduce-window.9
  53.6 0.7 convert_reduce_fusion.1
  54.3 0.1 slice_reduce_fusion
  54.5 0.2 select_reduce_fusion.1
  54.7 12.9 %all-to-all-done.1 = bf16[16,128,128]{2,1,0:T(8,128)(2,1)S(1)} async-done(((bf16[16,128,128]{2,1,0:T(8,128)(2,1)}), bf16[16,128,128]{2,1,0:T(8,128)(2,1)S(1)}, u32[]{:S(2)}, u32[]{:S(2)}) %all-to-all-start.1) | async-done | bytes 524320 | tf_op jit(solution)/shard_map/all_to_all | solution.py:530
  67.6 11.9 %segments.1 = bf16[16,136,128]{2,1,0:T(8,128)(2,1)S(1)} custom-call(s32[1]{0:T(128)} %bitcast.11.count_ref, s32[1]{0:T(128)} %bitcast.12.full_ref, s32[128]{0:T(128)S(1)} %get-tuple-element.55.seg_ref, s32[128]{0:T(128)S(1)} %get-tuple-element.54.few_row_ref, s32[128]{0:T(128)S(1)} %get-tuple-element.53.all_row_ref, s32[32,128]{1,0:T(8,128)S(1)} %bitcast.33, ...), custom_call_target="tpu_custom_call" | custom-call | flops 8589934592 | bytes 12582912 | tf_op jit(solution)/shard_map/segments/pallas_call | solution.py:609
  79.5 24.1 %all_to_all.21.ret_ref = bf16[16,136,128]{2,1,0:T(8,128)(2,1)S(1)} all-to-all(bf16[16,136,128]{2,1,0:T(8,128)(2,1)S(1)} %segments.1), channel_id=1, replica_groups=mesh['slab'=16,'col'=2] {'slab'}, dimensions={0} | all-to-all | bytes 1114112 | tf_op jit(solution)/shard_map/all_to_all | solution.py:530
  103.7 1.2 %collective-permute-done.3.nbr_ref = bf16[136,128]{1,0:T(8,128)(2,1)S(1)} collective-permute-done((bf16[136,128]{1,0:T(8,128)(2,1)S(1)}, bf16[136,128]{1,0:T(8,128)(2,1)S(1)}, u32[]{:S(2)}, u32[]{:S(2)}) %collective-permute-start.3) | collective-permute-done | bytes 34848 | tf_op jit(solution)/shard_map/ppermute | solution.py:643
  104.9 7.0 %smooth_last.1 = f32[128,2048]{1,0:T(8,128)} custom-call(bf16[16,136,128]{2,1,0:T(8,128)(2,1)S(1)} %all_to_all.21.ret_ref, bf16[136,128]{1,0:T(8,128)(2,1)S(1)} %collective-permute-done.3.nbr_ref, f32[17,160,128]{2,1,0:T(8,128)S(1)} %copy-done.2, f32[17,160,128]{2,1,0:T(8,128)S(1)} %copy-done.3, f32[128,2048]{1,0:T(8,128)S(1)} %copy-done, ...), custom_call_target="tpu_custom_call" | custom-call | flops 40000000 | bytes 8388608 | tf_op jit(solution)/shard_map/smooth_last/pallas_call | solution.py:644
  (46 shorter events, 0.9 us)
Async XLA Ops:
  1.0 4.2 %collective-permute-start = (f32[2,128,128]{2,1,0:T(8,128)S(1)}, f32[2,128,128]{2,1,0:T(8,128)S(1)}, u32[]{:S(2)}, u32[]{:S(2)}) collective-permute-start(f32[2,128,128]{2,1,0:T(8,128)S(1)} %pad_maximum_fusion), channel_id=1, source_target_pairs={{0,1},{1,0},{2,3},{3,2},{4,5},{5,4},{6,7},{7,6},{8,9},{9,8},{10,11... | collective-permute-start | bytes 393224 | tf_op jit(solution)/shard_map/ppermute | solution.py:508
  5.3 5.5 %copy-start.8 = (f32[2,128,128]{2,1,0:T(8,128)}, f32[2,128,128]{2,1,0:T(8,128)S(1)}, u32[]{:S(2)}) copy-start(f32[2,128,128]{2,1,0:T(8,128)S(1)} %broadcast_select_fusion.nbr_ref) | copy-start | bytes 393220
  5.3 5.4 %collective-permute-start.1 = (f32[8,2176]{1,0:T(8,128)S(1)}, f32[8,2176]{1,0:T(8,128)S(1)}, u32[]{:S(2)}, u32[]{:S(2)}) collective-permute-start(f32[8,2176]{1,0:T(8,128)S(1)} %get-tuple-element.72), channel_id=1, source_target_pairs={{0,2},{2,0},{4,6},{6,4},{8,10},{10,8},{12,14},{14,12},{16,18},{18,... | collective-permute-start | bytes 208904 | tf_op jit(solution)/shard_map/ppermute | solution.py:527
  7.9 2.9 %collective-permute-start.2 = (f32[8,2176]{1,0:T(8,128)S(1)}, f32[8,2176]{1,0:T(8,128)S(1)}, u32[]{:S(2)}, u32[]{:S(2)}) collective-permute-start(f32[8,2176]{1,0:T(8,128)S(1)} %get-tuple-element.71), channel_id=1, source_target_pairs={{2,4},{6,8},{10,12},{14,16},{18,20},{22,24},{26,28},{4,2},{8,6},{1... | collective-permute-start | bytes 208904 | tf_op jit(solution)/shard_map/ppermute | solution.py:526
  8.6 13.9 %copy-start.12 = (s32[128,2]{0,1:T(2,128)S(1)}, s32[128,2]{0,1:T(2,128)}, u32[]{:S(2)}) copy-start(s32[128,2]{0,1:T(2,128)} %param.15) | copy-start | bytes 3076
  8.6 13.9 %copy-start.11 = (s32[256]{0:T(256)S(1)}, s32[256]{0:T(256)}, u32[]{:S(2)}) copy-start(s32[256]{0:T(256)} %owned_in.1) | copy-start | bytes 3076
  8.6 15.9 %copy-start.6 = (f32[8,2048]{1,0:T(8,128)S(1)}, f32[8,2048]{1,0:T(8,128)}, u32[]{:S(2)}) copy-start(f32[8,2048]{1,0:T(8,128)} %scale_ref.1) | copy-start | bytes 196612
  10.7 0.6 copy-start.9
  11.4 0.6 copy-start.10
  24.5 1.0 copy-start.7
  24.6 43.0 %copy-start.4 = (bf16[16,64,64]{2,1,0:T(8,128)(2,1)S(1)}, bf16[16,64,64]{2,1,0:T(8,128)(2,1)}, u32[]{:S(2)}) copy-start(bf16[16,64,64]{2,1,0:T(8,128)(2,1)} %table_ref.1) | copy-start | bytes 393220
  24.6 43.0 %copy-start.5 = (s32[128,32]{0,1:T(8,128)S(1)}, s32[128,32]{0,1:T(8,128)}, u32[]{:S(2)}) copy-start(s32[128,32]{0,1:T(8,128)} %param.16) | copy-start | bytes 49156
  49.3 18.2 %all-to-all-start.1 = ((bf16[16,128,128]{2,1,0:T(8,128)(2,1)}), bf16[16,128,128]{2,1,0:T(8,128)(2,1)S(1)}, u32[]{:S(2)}, u32[]{:S(2)}) async-start(bf16[16,128,128]{2,1,0:T(8,128)(2,1)} %get-tuple-element.49), calls=%async_computation.1 | async-start | bytes 1048576 | tf_op jit(solution)/shard_map/all_to_all | solution.py:530
  67.6 37.3 %copy-start.1 = (s32[128,2048]{1,0:T(8,128)S(1)}, s32[128,2048]{1,0:T(8,128)}, u32[]{:S(2)}) copy-start(s32[128,2048]{1,0:T(8,128)} %mask_in.3) | copy-start | bytes 3145732
  67.6 37.3 %copy-start.2 = (f32[17,160,128]{2,1,0:T(8,128)S(1)}, f32[17,160,128]{2,1,0:T(8,128)}, u32[]{:S(2)}) copy-start(f32[17,160,128]{2,1,0:T(8,128)} %get-tuple-element.51.fn_ref) | copy-start | bytes 4177924
  67.6 37.3 %copy-start.3 = (f32[17,160,128]{2,1,0:T(8,128)S(1)}, f32[17,160,128]{2,1,0:T(8,128)}, u32[]{:S(2)}) copy-start(f32[17,160,128]{2,1,0:T(8,128)} %get-tuple-element.52.fw_ref) | copy-start | bytes 4177924
  79.5 25.4 %copy-start = (f32[128,2048]{1,0:T(8,128)S(1)}, f32[128,2048]{1,0:T(8,128)}, u32[]{:S(2)}) copy-start(f32[128,2048]{1,0:T(8,128)} %dir_in.3) | copy-start | bytes 3145732
  103.6 1.3 %collective-permute-start.3 = (bf16[136,128]{1,0:T(8,128)(2,1)S(1)}, bf16[136,128]{1,0:T(8,128)(2,1)S(1)}, u32[]{:S(2)}, u32[]{:S(2)}) collective-permute-start(bf16[136,128]{1,0:T(8,128)(2,1)S(1)} %fusion.5), channel_id=1, source_target_pairs={{0,1},{1,0},{2,3},{3,2},{4,5},{5,4},{6,7},{7,6},{8,9},{9,8},{10,11... | collective-permute-start | bytes 104456 | tf_op jit(solution)/shard_map/ppermute | solution.py:643

commit v7 on v6

--- a/solution.py
+++ b/solution.py
@@ -13,7 +13,7 @@
 HALO = 8
 PAD = 16
 CHUNKS = 4
-CAP = 4
+CAP = 3
 
 
 def lane_iota(shape):
@@ -51,7 +51,7 @@
         tile(c, c + 1)
         return carry
 
-    lax.fori_loop(0, tiles - 1, step, 0, unroll=2)
+    lax.fori_loop(0, tiles - 1, step, 0, unroll=4)
     tile(tiles - 1, 0)
 
 
@@ -60,7 +60,7 @@
         src, dst = bufs[step % 2], bufs[1 - step % 2]
         last = step == SWEEPS - 1
         first_row = PAD if last else HALO
-        parts = 2 if last else 3
+        parts = 4 if last else 6
         if last and before_last is not None:
             before_last()
         length = (rows - 2 * (PAD - HALO) if last else rows) // parts
@@ -87,7 +87,7 @@
                 return tile(c, c + 1, *carry)
 
             carry = src[tiles - 1, body, :], src[0, body, :]
-            carry = lax.fori_loop(0, tiles - 1, step_tile, carry, unroll=8)
+            carry = lax.fori_loop(0, tiles - 1, step_tile, carry, unroll=True)
             if not last:
                 tile(tiles - 1, 0, *carry)
             elif part_done is not None:
@@ -111,7 +111,7 @@
 
 
 def smooth_first_kernel(
-    dir_in, kap_in, mask_in, nbr_ref, got_a_ref, got_b_ref,
+    dir_in, kap_in, mask_in, nbr_ref, got_a_ref, got_b_ref, corner_ref,
     out_ref, fn_out, fw_out,
     dir_ref, kap_ref, mask_ref, done, own_ref, fn_ref, fw_ref, fe_ref, u0, u1, kbuf,
     load_sems, sems,
@@ -129,8 +129,7 @@
     even = lax.rem(lax.axis_index("slab"), 2) == 0
     low = row_iota(edge) < HALO // 2
 
-    def edges(c, cols):
-        got_a, got_b = got_a_ref[:, cols], got_b_ref[:, cols]
+    def edges(c, got_a, got_b):
         top = jnp.where(even, got_b, got_a)
         bot = jnp.where(even, got_a, got_b)
         u0[c, pl.ds(HALO, HALO), :] = jnp.where(low, 0.0, pltpu.roll(top, HALO // 2, 0))
@@ -150,12 +149,16 @@
         maskf = mask_ref[:, cols].astype(jnp.float32)
         u0[c, pl.ds(PAD, own), :] = dir_ref[:, cols] * maskf
         kbuf[c, pl.ds(PAD, own), :] = kap_ref[:, cols] * (0.5 * maskf)
-        edges(c, cols)
+        edges(c, got_a_ref[:, cols], got_b_ref[:, cols])
         return carry
 
     u0[tiles - 1, pl.ds(PAD, own), :] = nbr_ref[0]
     kbuf[tiles - 1, pl.ds(PAD, own), :] = 0.5 * nbr_ref[1]
-    edges(tiles - 1, pl.ds((tiles - 1) * lanes, lanes))
+    edges(tiles - 1, corner_ref[0], corner_ref[1])
+    lane = lane_iota((rows, lanes))
+    near = jnp.where(lax.axis_index("col") == 0, lanes - 1 - lane, lane) >= lanes - SWEEPS
+    body = pl.ds(HALO, rows)
+    kbuf[tiles - 1, body, :] = jnp.where(near, kbuf[tiles - 1, body, :], 0.0)
 
     def faces(c, k_left):
         body = pl.ds(HALO, rows)
@@ -169,8 +172,8 @@
         for load in loads[k]:
             load.wait()
         low_tile, high_tile = chunk_of(tiles - 1, k)
-        lax.fori_loop(low_tile, high_tile, fill, 0)
-        k_left = lax.fori_loop(low_tile, high_tile, faces, k_left)
+        lax.fori_loop(low_tile, high_tile, fill, 0, unroll=True)
+        k_left = lax.fori_loop(low_tile, high_tile, faces, k_left, unroll=True)
     faces(tiles - 1, k_left)
     copies = [
         pltpu.make_async_copy(ref, out, sems.at[i])
@@ -237,18 +240,43 @@
     sweeps(tiles, rows, (u0, u1), own_ref, fn_ref, fw_ref, fe_ref, finish, before_last)
 
 
-def outbox_kernel(
-    owned_in, anchor_in, scale_ref, out_ref, owned_ref, anchor_ref, sems,
-    *, seg_tiles, col_tiles, span,
+def prepare_kernel(
+    dir_in, kap_in, mask_in, owned_in, anchor_in, scale_in,
+    edge_ref, send_a_ref, send_b_ref, out_ref,
+    edges, edge_mask, tops, top_mask, bottoms, bottom_mask, owned_ref, anchor_ref, scale_ref,
+    sems, *, seg_tiles, col_tiles, span,
 ):
-    copies = [
-        pltpu.make_async_copy(owned_in, owned_ref, sems.at[0]),
-        pltpu.make_async_copy(anchor_in, anchor_ref, sems.at[1]),
-    ]
+    rows, cols = dir_in.shape
+    lanes = edge_ref.shape[-1]
+    is_low = lax.axis_index("col") == 0
+    at = pl.ds(pl.multiple_of(jnp.where(is_low, cols - lanes, 0), lanes), lanes)
+    low, high = pl.ds(0, HALO), pl.ds(rows - HALO, HALO)
+    pairs = [(owned_in, owned_ref), (anchor_in, anchor_ref), (scale_in, scale_ref)]
+    for i, source in enumerate((dir_in, kap_in)):
+        pairs.append((source.at[:, at], edges.at[i]))
+        pairs.append((source.at[low, :], tops.at[i]))
+        pairs.append((source.at[high, :], bottoms.at[i]))
+    pairs.append((mask_in.at[:, at], edge_mask))
+    pairs.append((mask_in.at[low, :], top_mask))
+    pairs.append((mask_in.at[high, :], bottom_mask))
+    copies = [pltpu.make_async_copy(a, b, sems.at[i]) for i, (a, b) in enumerate(pairs)]
     for copy in copies:
         copy.start()
     for copy in copies:
         copy.wait()
+
+    maskf = edge_mask[...].astype(jnp.float32)
+    edge_ref[0] = edges[0] * maskf
+    edge_ref[1] = edges[1] * maskf
+    upper = row_iota((HALO, cols)) < HALO // 2
+    maskf = top_mask[...].astype(jnp.float32)
+    first = jnp.where(upper, tops[0] * maskf, pltpu.roll(tops[1] * maskf, HALO // 2, 0))
+    maskf = bottom_mask[...].astype(jnp.float32)
+    last = jnp.where(upper, pltpu.roll(bottoms[0] * maskf, HALO // 2, 0), bottoms[1] * maskf)
+    even = lax.rem(lax.axis_index("slab"), 2) == 0
+    send_a_ref[...] = jnp.where(even, last, first)
+    send_b_ref[...] = jnp.where(even, first, last)
+
     seg_max = scale_ref.shape[0]
     me = lax.axis_index("slab") * lax.axis_size("col") + lax.axis_index("col")
     owners = []
@@ -269,7 +297,7 @@
 
 
 def segments_kernel(
-    count_ref, full_ref, seg_ref, few_row_ref, all_row_ref, index_ref, x_ref, table_ref,
+    count_ref, seg_ref, second_ref, row_ref, index_ref, x_ref, table_ref,
     prec_in, few_ref, all_ref, out_ref,
     prec_ref, ahead_ref, behind_ref, turned, weighted, zbuf, scale_row, adj, grid,
     prec_sem, scale_sem, *, width, sizes,
@@ -280,7 +308,6 @@
     pieces = order // width
     batch = sizes[-1]
     count = count_ref[0]
-    full = full_ref[0]
 
     def prec_copy(i):
         cols = pl.ds(pl.multiple_of(i * width, width), width)
@@ -293,13 +320,15 @@
         for j in range(batch):
             e = g * batch + j
 
-            @pl.when((e < count) & (full == 0))
+            second = second_ref[jnp.minimum(e, seg_ref.shape[0] - 1)]
+
+            @pl.when((e < count) & (second == 0))
             def _(e=e, j=j):
-                scale_copy(few_ref, few_row_ref[e], j).start()
-
-            @pl.when((e < count) & (full != 0))
+                scale_copy(few_ref, row_ref[e], j).start()
+
+            @pl.when((e < count) & (second != 0))
             def _(e=e, j=j):
-                scale_copy(all_ref, all_row_ref[e], j).start()
+                scale_copy(all_ref, row_ref[e], j).start()
 
             @pl.when(e >= count)
             def _(j=j):
@@ -355,7 +384,7 @@
                 weighted[j * lanes : (j + 1) * lanes, part] = value.astype(jnp.bfloat16)
             return carry
 
-        lax.fori_loop(0, blocks, interp, 0, unroll=4 if size <= 4 else 2)
+        lax.fori_loop(0, blocks, interp, 0, unroll=4)
 
         def product(i, carry):
             cols = pl.ds(pl.multiple_of(i * width, width), width)
@@ -391,7 +420,7 @@
             adj[:, part] = adj[:, part] + jnp.dot(left, right, preferred_element_type=jnp.float32)
             return carry
 
-        lax.fori_loop(0, blocks, back, 0, unroll=4 if size <= 4 else 2)
+        lax.fori_loop(0, blocks, back, 0, unroll=4)
 
     def whole_group(g, carry):
         work(g, batch, batch)
@@ -460,20 +489,21 @@
     before = slot_in[None, :] < slot_in[:, None]
     same = (by_dev[:, :, None] == by_dev[:, None, :]) & before[None]
     place = jnp.sum(same.astype(jnp.int32), axis=2).reshape(slots)
-    overflow = jnp.max(jnp.where(used, place, 0)) >= CAP
+    worst = jnp.max(jnp.where(used, place, 0))
+    mode = (worst >= CAP).astype(jnp.int32) + (worst > CAP).astype(jnp.int32)
     mine = owner == my_device
     rank = jnp.cumsum(mine.astype(jnp.int32)) - 1
     count = jnp.sum(mine.astype(jnp.int32))
     longest = segs
     pick = mine[None, :] & (rank[None, :] == jnp.arange(longest, dtype=jnp.int32)[:, None])
     src_slab = slot_ids // (seg_max * col_count)
-    columns = [
-        owned_segments,
-        src_slab * CAP + jnp.minimum(place, CAP - 1),
-        src_slab * seg_max + slot_ids % seg_max,
-    ]
+    second = (mode == 2) | ((mode == 1) & (place >= CAP))
+    whole = src_slab * seg_max + slot_ids % seg_max
+    row = jnp.where(mode == 2, whole, src_slab)
+    row = jnp.where(second, row, src_slab * CAP + jnp.minimum(place, CAP - 1))
+    columns = [owned_segments, second.astype(jnp.int32), row]
     listed = [jnp.sum(jnp.where(pick, col[None, :], 0), axis=1) for col in columns]
-    return count, listed, overflow, owner_slab, used, slot_in
+    return count, listed, mode, owner_slab, used, place, slot_in
 
 
 def per_device(
@@ -500,49 +530,46 @@
     my_device = my_slab * col_count + my_col
     is_low = my_col == 0
 
-    def edge_cols(array):
-        return jnp.where(is_low, array[:, cols_dev - lanes :], array[:, :lanes])
-
-    edge_mask = edge_cols(land_mask).astype(jnp.float32)
-    edge = jnp.stack([edge_cols(direction) * edge_mask, edge_cols(kappa) * edge_mask])
-    nbr = lax.ppermute(edge, "col", [(0, 1), (1, 0)])
-    near = jnp.where(
-        is_low, lane_iota((1, lanes)) < SWEEPS, lane_iota((1, lanes)) >= lanes - SWEEPS
-    )
-    nbr = jnp.where(near[None], nbr, 0.0)
-
-    def edge_rows(start):
-        part = slice(start, start + SWEEPS)
-        maskf = land_mask[part].astype(jnp.float32)
-        field = jnp.concatenate([direction[part] * maskf, nbr[0, part]], axis=1)
-        coeff = jnp.concatenate([kappa[part] * maskf, nbr[1, part]], axis=1)
-        return jnp.concatenate([field, coeff], axis=0)
-
-    first_rows, last_rows = edge_rows(0), edge_rows(rows_dev - SWEEPS)
-    even = my_slab % 2 == 0
-    pairs_a = [(i, i ^ 1) for i in range(slab_count)]
-    pairs_b = [(i, i + 1) for i in range(1, slab_count - 1, 2)]
-    pairs_b = pairs_b + [(j, i) for i, j in pairs_b]
-    got_b = lax.ppermute(jnp.where(even, first_rows, last_rows), "slab", pairs_b)
-    got_a = lax.ppermute(jnp.where(even, last_rows, first_rows), "slab", pairs_a)
-
     def swap(array, groups=None):
         return lax.all_to_all(
             array, "slab", split_axis=0, concat_axis=0, tiled=True, axis_index_groups=groups
         )
 
-    scales_out = pl.pallas_call(
-        functools.partial(outbox_kernel, seg_tiles=seg_tiles, col_tiles=col_tiles, span=span),
-        out_shape=jax.ShapeDtypeStruct((slab_count * CAP, 1, order), jnp.float32),
-        in_specs=[hbm_spec(), hbm_spec(), vmem_spec()],
-        out_specs=vmem_spec(),
+    vm = pltpu.VMEM
+    edge, send_a, send_b, scales_out = pl.pallas_call(
+        functools.partial(
+            prepare_kernel, seg_tiles=seg_tiles, col_tiles=col_tiles, span=span
+        ),
+        out_shape=(
+            jax.ShapeDtypeStruct((2, rows_dev, lanes), jnp.float32),
+            jax.ShapeDtypeStruct((HALO, cols_dev), jnp.float32),
+            jax.ShapeDtypeStruct((HALO, cols_dev), jnp.float32),
+            jax.ShapeDtypeStruct((slab_count * CAP, 1, order), jnp.float32),
+        ),
+        in_specs=[hbm_spec()] * 6,
+        out_specs=(vmem_spec(),) * 4,
         scratch_shapes=[
+            vm((2, rows_dev, lanes), jnp.float32), vm((rows_dev, lanes), jnp.int32),
+            vm((2, HALO, cols_dev), jnp.float32), vm((HALO, cols_dev), jnp.int32),
+            vm((2, HALO, cols_dev), jnp.float32), vm((HALO, cols_dev), jnp.int32),
             pltpu.SMEM(owned_segments.shape, jnp.int32),
             pltpu.SMEM(seg_anchor.shape[::-1], jnp.int32),
-            pltpu.SemaphoreType.DMA((2,)),
+            vm(obs_scale.shape, jnp.float32),
+            pltpu.SemaphoreType.DMA((12,)),
         ],
-        name="outbox",
-    )(owned_segments, seg_anchor.T, obs_scale)
+        compiler_params=pltpu.CompilerParams(vmem_limit_bytes=60 << 20),
+        name="prepare",
+    )(direction, kappa, land_mask, owned_segments, seg_anchor.T, obs_scale)
+    nbr = lax.ppermute(edge, "col", [(0, 1), (1, 0)])
+    pairs_a = [(i, i ^ 1) for i in range(slab_count)]
+    pairs_b = [(i, i + 1) for i in range(1, slab_count - 1, 2)]
+    pairs_b = pairs_b + [(j, i) for i, j in pairs_b]
+    got_b = lax.ppermute(send_b, "slab", pairs_b)
+    got_a = lax.ppermute(send_a, "slab", pairs_a)
+
+    corners = jnp.stack([got_a, got_b])
+    corners = jnp.where(is_low, corners[:, :, cols_dev - lanes :], corners[:, :, :lanes])
+    corners = lax.ppermute(corners, "col", [(0, 1), (1, 0)])
     few = swap(scales_out)
 
     tiles = col_tiles + 1
@@ -557,48 +584,54 @@
             jax.ShapeDtypeStruct((col_tiles, rows_dev, lanes), jnp.bfloat16),
             face_shape, face_shape,
         ),
-        in_specs=[hbm_spec()] * 3 + [vmem_spec()] * 3,
+        in_specs=[hbm_spec()] * 3 + [vmem_spec()] * 4,
         out_specs=(hbm_spec(),) * 3,
         scratch_shapes=[own_float, own_float, own_int]
         + [pltpu.VMEM((col_tiles, rows_dev, lanes), jnp.bfloat16)]
         + [buf] * 7
-        + [pltpu.SemaphoreType.DMA((3, CHUNKS)), pltpu.SemaphoreType.DMA((4,))],
-        compiler_params=pltpu.CompilerParams(vmem_limit_bytes=58 << 20),
+        + [pltpu.SemaphoreType.DMA((3, CHUNKS)), pltpu.SemaphoreType.DMA((6,))],
+        compiler_params=pltpu.CompilerParams(vmem_limit_bytes=52 << 20),
         cost_estimate=pl.CostEstimate(flops=40000000, bytes_accessed=8 << 20, transcendentals=0),
         name="smooth_first",
-    )(direction, kappa, land_mask, nbr, got_a, got_b)
+    )(direction, kappa, land_mask, nbr, got_a, got_b, corners)
 
     smoothed, owned_segments, seg_anchor, obs_scale = lax.optimization_barrier(
         (smoothed, owned_segments, seg_anchor, obs_scale)
     )
     gathered = swap(smoothed, groups)
 
-    count, listed, overflow, owner_slab, used, slot_in = owner_tables(
+    count, listed, mode, owner_slab, used, place, slot_in = owner_tables(
         owned_segments, seg_anchor, seg_tiles, seg_max, dev_count, col_count, span,
         col_tiles, my_device,
     )
 
     my_owner = lax.dynamic_slice_in_dim(owner_slab, my_device * seg_max, seg_max)
     my_used = lax.dynamic_slice_in_dim(used, my_device * seg_max, seg_max)
+    my_place = lax.dynamic_slice_in_dim(place, my_device * seg_max, seg_max)
 
     def outbox(cap, position):
         target = jnp.arange(slab_count * cap, dtype=jnp.int32)
-        hit = (
-            (my_owner * cap + position)[None, :] == target[:, None]
-        ) & (my_used & (position < cap))[None, :]
+        hit = (my_owner * cap + position)[None, :] == target[:, None]
+        hit = hit & (my_used & (position >= 0) & (position < cap))[None, :]
         slot = jnp.sum(jnp.where(hit, slot_in[None, :], 0), axis=1)
         return obs_scale[slot].reshape(slab_count * cap, 1, order)
 
     many = (slab_count * seg_max, 1, order)
-    everything = lax.cond(
-        overflow,
-        lambda: swap(outbox(seg_max, slot_in)),
-        lambda: pl.pallas_call(
+
+    def one_more():
+        extra = swap(outbox(1, my_place - CAP))
+        return lax.pad(extra, jnp.float32(0), ((0, many[0] - slab_count, 0), (0, 0, 0), (0, 0, 0)))
+
+    def no_more():
+        return pl.pallas_call(
             lambda out_ref: None,
             out_shape=jax.ShapeDtypeStruct(many, jnp.float32),
             out_specs=hbm_spec(),
             name="unread",
-        )(),
+        )()
+
+    everything = lax.switch(
+        mode, [no_more, one_more, lambda: swap(outbox(seg_max, slot_in))]
     )
 
     chunk = rows_dev + 2 * SWEEPS
@@ -609,7 +642,7 @@
     returning = pl.pallas_call(
         functools.partial(segments_kernel, width=width, sizes=sizes),
         out_shape=jax.ShapeDtypeStruct((span, chunk, lanes), jnp.bfloat16),
-        in_specs=[smem_spec()] * 6 + [vmem_spec()] * 2 + [hbm_spec()] * 3,
+        in_specs=[smem_spec()] * 5 + [vmem_spec()] * 2 + [hbm_spec()] * 3,
         out_specs=vmem_spec(),
         scratch_shapes=[
             pltpu.VMEM((order, order), jnp.bfloat16),
@@ -630,7 +663,7 @@
         ),
         name="segments",
     )(
-        count.reshape(1), overflow.astype(jnp.int32).reshape(1), *listed, interp_index.T,
+        count.reshape(1), *listed, interp_index.T,
         gathered.reshape(order, lanes), interp_table, precision, few, everything,
     )
 

time: 113 us -> 101 us (0.89)
  blocking collectives: 47.9 us -> 23.1 us
  waiting for transfers between devices: 16.2 us -> 30 us
  starting transfers between devices: 7.69 us -> 18.3 us
  Pallas kernels: 31.9 us -> 24.8 us
  other arithmetic: 4.47 us -> 2.31 us
  local copies, waits for them, and re-layouts: 2.79 us -> 0.71 us
    all_to_all x2 -> x1, blocking collectives: 47.9 us -> 23.1 us  [swap(): lax.all_to_all(array, 'slab', split_axis=0, concat_axis=0, tiled=True, ax...]
    all_to_all x1 -> x2, waiting for transfers between devices: 12.9 us -> 26 us  [swap(): lax.all_to_all(array, 'slab', split_axis=0, concat_axis=0, tiled=True, ax...]
    all_to_all x1 -> x2, starting transfers between devices: 3.86 us -> 14.5 us  [swap(): lax.all_to_all(array, 'slab', split_axis=0, concat_axis=0, tiled=True, ax...]
    pallas_call x1, Pallas kernels: 10.5 us -> 5.93 us  [per_device(): pl.pallas_call(smooth_first_kernel, out_shape=(jax.ShapeDtypeStruct((col_...]
    pallas_call x1, Pallas kernels: 6.99 us -> 4.56 us  [per_device(): pl.pallas_call(smooth_last_kernel, out_shape=jax.ShapeDtypeStruct((rows_d...]
    unnamed x26 -> x18, local copies, waits for them, and re-layouts: 2.28 us -> 0.05 us
    ppermute x2 -> x3, waiting for transfers between devices: 2.14 us -> 2.82 us  [the longest x1 1.71 us: per_device(): got_a = lax.ppermute(send_a, 'slab', pairs_a)]
    ppermute x2 -> x3, starting transfers between devices: 3.2 us -> 3.68 us  [the longest x1 3.03 us: per_device(): got_a = lax.ppermute(send_a, 'slab', pairs_a)]
  transfers between devices with their start and end apart: 5 -> 7, of which waited for: 3 -> 5; matrix products, arithmetic and copies ran while one was open for 2% -> 1% of each run, Pallas kernels for 2% -> 0%
where the time goes in v7:
time: 101 us
  waiting for transfers between devices  30 us (30%)
  Pallas kernels  24.8 us (25%)
  blocking collectives  23.1 us (23%)
  starting transfers between devices  18.3 us (18%)
  other arithmetic  2.31 us (2%)
  between operations  1.56 us (2%)
    all_to_all x2, waiting for transfers between devices, swap(): lax.all_to_all(array, 'slab', split_axis=0, concat_axis=0, tiled=True, ax...  26 us
    all_to_all x1, blocking collectives, swap(): lax.all_to_all(array, 'slab', split_axis=0, concat_axis=0, tiled=True, ax...  23.1 us
    all_to_all x2, starting transfers between devices, swap(): lax.all_to_all(array, 'slab', split_axis=0, concat_axis=0, tiled=True, ax...  14.5 us
    pallas_call x1, Pallas kernels, per_device(): pl.pallas_call(functools.partial(segments_kernel, width=width, sizes=size...  11.9 us
    pallas_call x1, Pallas kernels, per_device(): pl.pallas_call(smooth_first_kernel, out_shape=(jax.ShapeDtypeStruct((col_...  5.93 us
    pallas_call x1, Pallas kernels, per_device(): pl.pallas_call(smooth_last_kernel, out_shape=jax.ShapeDtypeStruct((rows_d...  4.56 us
    ppermute x1, starting transfers between devices, per_device(): got_a = lax.ppermute(send_a, 'slab', pairs_a)  3.03 us
    pallas_call x1, Pallas kernels, per_device(): pl.pallas_call(functools.partial(prepare_kernel, seg_tiles=seg_tiles, col...  2.37 us
  transfers between devices with their start and end apart: 7, of which 5 were waited for; matrix products, arithmetic and copies ran while one was open for 1% of the time, Pallas kernels for 0%

profile of v7, /device:TPU:0, one launch (start us, length us, event | category | flops | bytes accessed | tf_op | source)
XLA Modules:
  0.0 100.8 jit_solution(10706797867576691243)
XLA Ops:
  0.0 2.4 %prepare.1 = (f32[2,128,128]{2,1,0:T(8,128)}, f32[8,2048]{1,0:T(8,128)}, f32[8,2048]{1,0:T(8,128)}, f32[48,1,2048]{2,1,0:T(1,128)}) custom-call(f32[128,2048]{1,0:T(8,128)} %dir_in.5, f32[128,2048]{1,0:T(8,128)} %kap_in.3, s32[128,2048]{1,0:T(8,128)} %mask_in.5, s32[256]{0:T(256)} %owned_in.1, s32[2,128]{1,0:T(2,128)} %bitcast.32, f32[8,2048]{1,0:T(8,128)} %scale_in.1), custom_call_target="tpu_custom_call" | custom-call | tf_op jit(solution)/shard_map/prepare/pallas_call | solution.py:539
  2.4 3.0 %collective-permute-start.1 = (f32[8,2048]{1,0:T(8,128)}, f32[8,2048]{1,0:T(8,128)S(1)}, u32[]{:S(2)}, u32[]{:S(2)}) collective-permute-start(f32[8,2048]{1,0:T(8,128)} %get-tuple-element.58), channel_id=1, source_target_pairs={{0,2},{2,0},{4,6},{6,4},{8,10},{10,8},{12,14},{14,12},{16,18},{18,... | collective-permute-start | bytes 196616 | tf_op jit(solution)/shard_map/ppermute | solution.py:568
  5.4 0.7 collective-permute-start.2
  6.2 1.7 %collective-permute-done.1.got_a_ref = f32[8,2048]{1,0:T(8,128)S(1)} collective-permute-done((f32[8,2048]{1,0:T(8,128)}, f32[8,2048]{1,0:T(8,128)S(1)}, u32[]{:S(2)}, u32[]{:S(2)}) %collective-permute-start.1) | collective-permute-done | bytes 65568 | tf_op jit(solution)/shard_map/ppermute | solution.py:568
  7.9 1.1 %collective-permute-done.3.corner_ref = f32[2,8,128]{2,1,0:T(8,128)S(1)} collective-permute-done((f32[2,8,128]{2,1,0:T(8,128)S(1)}, f32[2,8,128]{2,1,0:T(8,128)S(1)}, u32[]{:S(2)}, u32[]{:S(2)}) %collective-permute-start.3) | collective-permute-done | bytes 8224 | tf_op jit(solution)/shard_map/ppermute | solution.py:572
  9.1 5.9 %smooth_first.1 = (bf16[16,128,128]{2,1,0:T(8,128)(2,1)}, f32[17,160,128]{2,1,0:T(8,128)}, f32[17,160,128]{2,1,0:T(8,128)}) custom-call(f32[128,2048]{1,0:T(8,128)S(1)} %copy-done, f32[128,2048]{1,0:T(8,128)} %kap_in.3, s32[128,2048]{1,0:T(8,128)} %mask_in.5, f32[2,128,128]{2,1,0:T(8,128)S(1)} %collective-permute-done.nbr_ref, ...), custom_call_target="tpu_custom_call" | custom-call | flops 40000000 | bytes 8388608 | tf_op jit(solution)/shard_map/smooth_first/pallas_call | solution.py:581
  15.0 0.2 select_reduce_fusion.6
  15.3 0.1 eq.95
  15.4 0.1 convert_reduce_fusion
  15.6 0.1 reshape.138
  15.7 0.6 select_reduce_fusion.7
  17.5 0.1 dynamic_slice.11
  17.7 10.9 %all-to-all-start.3 = ((f32[48,1,2048]{2,1,0:T(1,128)}), f32[48,1,2048]{2,1,0:T(1,128)S(1)}, u32[]{:S(2)}, u32[]{:S(2)}) async-start(f32[48,1,2048]{2,1,0:T(1,128)} %get-tuple-element.64), calls=%async_computation.3 | async-start | bytes 786432 | tf_op jit(solution)/shard_map/all_to_all | solution.py:534
  28.6 0.3 reduce-window.9
  29.0 12.5 %all-to-all-done.3.few_ref = f32[48,1,2048]{2,1,0:T(1,128)S(1)} async-done(((f32[48,1,2048]{2,1,0:T(1,128)}), f32[48,1,2048]{2,1,0:T(1,128)S(1)}, u32[]{:S(2)}, u32[]{:S(2)}) %all-to-all-start.3) | async-done | bytes 393248 | tf_op jit(solution)/shard_map/all_to_all | solution.py:534
  41.5 3.6 %all-to-all-start.2 = ((bf16[16,128,128]{2,1,0:T(8,128)(2,1)}), bf16[16,128,128]{2,1,0:T(8,128)(2,1)S(1)}, u32[]{:S(2)}, u32[]{:S(2)}) async-start(bf16[16,128,128]{2,1,0:T(8,128)(2,1)} %get-tuple-element.63), calls=%async_computation.2 | async-start | bytes 1048576 | tf_op jit(solution)/shard_map/all_to_all | solution.py:534
  45.1 0.7 convert_reduce_fusion.1
  45.9 0.1 slice_reduce_fusion
  46.1 0.2 select_reduce_fusion.2
  46.2 13.5 %all-to-all-done.2 = bf16[16,128,128]{2,1,0:T(8,128)(2,1)S(1)} async-done(((bf16[16,128,128]{2,1,0:T(8,128)(2,1)}), bf16[16,128,128]{2,1,0:T(8,128)(2,1)S(1)}, u32[]{:S(2)}, u32[]{:S(2)}) %all-to-all-start.2) | async-done | bytes 524320 | tf_op jit(solution)/shard_map/all_to_all | solution.py:534
  59.7 11.9 %segments.1 = bf16[16,136,128]{2,1,0:T(8,128)(2,1)S(1)} custom-call(s32[1]{0:T(128)} %bitcast.11.count_ref, s32[128]{0:T(128)S(1)} %get-tuple-element.70.seg_ref, s32[128]{0:T(128)S(1)} %get-tuple-element.69.second_ref, s32[128]{0:T(128)S(1)} %get-tuple-element.68.row_ref, s32[32,128]{1,0:T(8,128)S(1)} %bitcast.29, bf16[2048,128]{1,0:T(8,128)(2,1)S(1)} %bitcast.26, ...), custom_call_target="tpu_custom_call" | custom-call | flops 8589934592 | bytes 12582912 | tf_op jit(solution)/shard_map/segments/pallas_call | solution.py:642
  71.6 23.1 %all_to_all.25.ret_ref = bf16[16,136,128]{2,1,0:T(8,128)(2,1)S(1)} all-to-all(bf16[16,136,128]{2,1,0:T(8,128)(2,1)S(1)} %segments.1), channel_id=1, replica_groups=mesh['slab'=16,'col'=2] {'slab'}, dimensions={0} | all-to-all | bytes 1114112 | tf_op jit(solution)/shard_map/all_to_all | solution.py:534
  94.8 1.2 %collective-permute-done.4.nbr_ref = bf16[136,128]{1,0:T(8,128)(2,1)S(1)} collective-permute-done((bf16[136,128]{1,0:T(8,128)(2,1)S(1)}, bf16[136,128]{1,0:T(8,128)(2,1)S(1)}, u32[]{:S(2)}, u32[]{:S(2)}) %collective-permute-start.4) | collective-permute-done | bytes 34848 | tf_op jit(solution)/shard_map/ppermute | solution.py:676
  96.0 4.6 %smooth_last.1 = f32[128,2048]{1,0:T(8,128)} custom-call(bf16[16,136,128]{2,1,0:T(8,128)(2,1)S(1)} %all_to_all.25.ret_ref, bf16[136,128]{1,0:T(8,128)(2,1)S(1)} %collective-permute-done.4.nbr_ref, f32[17,160,128]{2,1,0:T(8,128)S(1)} %copy-done.2, f32[17,160,128]{2,1,0:T(8,128)S(1)} %copy-done.3, f32[128,2048]{1,0:T(8,128)S(1)} %copy-done, ...), custom_call_target="tpu_custom_call" | custom-call | flops 40000000 | bytes 8388608 | tf_op jit(solution)/shard_map/smooth_last/pallas_call | solution.py:677
  (40 shorter events, 0.7 us)
Async XLA Ops:
  0.0 9.1 %copy-start = (f32[128,2048]{1,0:T(8,128)S(1)}, f32[128,2048]{1,0:T(8,128)}, u32[]{:S(2)}) copy-start(f32[128,2048]{1,0:T(8,128)} %dir_in.5) | copy-start | bytes 3145732
  2.4 5.5 %collective-permute-start.1 = (f32[8,2048]{1,0:T(8,128)}, f32[8,2048]{1,0:T(8,128)S(1)}, u32[]{:S(2)}, u32[]{:S(2)}) collective-permute-start(f32[8,2048]{1,0:T(8,128)} %get-tuple-element.58), channel_id=1, source_target_pairs={{0,2},{2,0},{4,6},{6,4},{8,10},{10,8},{12,14},{14,12},{16,18},{18,... | collective-permute-start | bytes 196616 | tf_op jit(solution)/shard_map/ppermute | solution.py:568
  5.4 2.5 %collective-permute-start.2 = (f32[8,2048]{1,0:T(8,128)}, f32[8,2048]{1,0:T(8,128)S(1)}, u32[]{:S(2)}, u32[]{:S(2)}) collective-permute-start(f32[8,2048]{1,0:T(8,128)} %get-tuple-element.59), channel_id=1, source_target_pairs={{2,4},{6,8},{10,12},{14,16},{18,20},{22,24},{26,28},{4,2},{8,6},{1... | collective-permute-start | bytes 196616 | tf_op jit(solution)/shard_map/ppermute | solution.py:567
  6.1 3.0 %collective-permute-start = (f32[2,128,128]{2,1,0:T(8,128)}, f32[2,128,128]{2,1,0:T(8,128)S(1)}, u32[]{:S(2)}, u32[]{:S(2)}) collective-permute-start(f32[2,128,128]{2,1,0:T(8,128)} %get-tuple-element.57), channel_id=1, source_target_pairs={{0,1},{1,0},{2,3},{3,2},{4,5},{5,4},{6,7},{7,6},{8,9},{9,8},{10,11... | collective-permute-start | bytes 393224 | tf_op jit(solution)/shard_map/ppermute | solution.py:563
  7.9 1.2 %collective-permute-start.3 = (f32[2,8,128]{2,1,0:T(8,128)S(1)}, f32[2,8,128]{2,1,0:T(8,128)S(1)}, u32[]{:S(2)}, u32[]{:S(2)}) collective-permute-start(f32[2,8,128]{2,1,0:T(8,128)S(1)} %fusion.7), channel_id=1, source_target_pairs={{0,1},{1,0},{2,3},{3,2},{4,5},{5,4},{6,7},{7,6},{8,9},{9,8},{10,11... | collective-permute-start | bytes 24584 | tf_op jit(solution)/shard_map/ppermute | solution.py:572
  7.9 7.1 %copy-start.8 = (s32[128,2]{0,1:T(2,128)S(1)}, s32[128,2]{0,1:T(2,128)}, u32[]{:S(2)}) copy-start(s32[128,2]{0,1:T(2,128)} %param.16) | copy-start | bytes 3076
  7.9 7.1 %copy-start.7 = (s32[256]{0:T(256)S(1)}, s32[256]{0:T(256)}, u32[]{:S(2)}) copy-start(s32[256]{0:T(256)} %owned_in.1) | copy-start | bytes 3076
  7.9 9.7 %copy-start.6 = (f32[8,2048]{1,0:T(8,128)S(1)}, f32[8,2048]{1,0:T(8,128)}, u32[]{:S(2)}) copy-start(f32[8,2048]{1,0:T(8,128)} %scale_in.1) | copy-start | bytes 196612
  17.7 42.0 %copy-start.4 = (bf16[16,64,64]{2,1,0:T(8,128)(2,1)S(1)}, bf16[16,64,64]{2,1,0:T(8,128)(2,1)}, u32[]{:S(2)}) copy-start(bf16[16,64,64]{2,1,0:T(8,128)(2,1)} %table_ref.1) | copy-start | bytes 393220
  17.7 42.0 %copy-start.5 = (s32[128,32]{0,1:T(8,128)S(1)}, s32[128,32]{0,1:T(8,128)}, u32[]{:S(2)}) copy-start(s32[128,32]{0,1:T(8,128)} %param.17) | copy-start | bytes 49156
  17.7 23.8 %all-to-all-start.3 = ((f32[48,1,2048]{2,1,0:T(1,128)}), f32[48,1,2048]{2,1,0:T(1,128)S(1)}, u32[]{:S(2)}, u32[]{:S(2)}) async-start(f32[48,1,2048]{2,1,0:T(1,128)} %get-tuple-element.64), calls=%async_computation.3 | async-start | bytes 786432 | tf_op jit(solution)/shard_map/all_to_all | solution.py:534
  41.5 18.2 %all-to-all-start.2 = ((bf16[16,128,128]{2,1,0:T(8,128)(2,1)}), bf16[16,128,128]{2,1,0:T(8,128)(2,1)S(1)}, u32[]{:S(2)}, u32[]{:S(2)}) async-start(bf16[16,128,128]{2,1,0:T(8,128)(2,1)} %get-tuple-element.63), calls=%async_computation.2 | async-start | bytes 1048576 | tf_op jit(solution)/shard_map/all_to_all | solution.py:534
  59.7 36.3 %copy-start.2 = (f32[17,160,128]{2,1,0:T(8,128)S(1)}, f32[17,160,128]{2,1,0:T(8,128)}, u32[]{:S(2)}) copy-start(f32[17,160,128]{2,1,0:T(8,128)} %get-tuple-element.66.fn_ref) | copy-start | bytes 4177924
  59.7 36.3 %copy-start.3 = (f32[17,160,128]{2,1,0:T(8,128)S(1)}, f32[17,160,128]{2,1,0:T(8,128)}, u32[]{:S(2)}) copy-start(f32[17,160,128]{2,1,0:T(8,128)} %get-tuple-element.67.fw_ref) | copy-start | bytes 4177924
  71.6 24.4 %copy-start.1 = (s32[128,2048]{1,0:T(8,128)S(1)}, s32[128,2048]{1,0:T(8,128)}, u32[]{:S(2)}) copy-start(s32[128,2048]{1,0:T(8,128)} %mask_in.5) | copy-start | bytes 3145732
  94.7 1.3 %collective-permute-start.4 = (bf16[136,128]{1,0:T(8,128)(2,1)S(1)}, bf16[136,128]{1,0:T(8,128)(2,1)S(1)}, u32[]{:S(2)}, u32[]{:S(2)}) collective-permute-start(bf16[136,128]{1,0:T(8,128)(2,1)S(1)} %fusion.6), channel_id=1, source_target_pairs={{0,1},{1,0},{2,3},{3,2},{4,5},{5,4},{6,7},{7,6},{8,9},{9,8},{10,11... | collective-permute-start | bytes 104456 | tf_op jit(solution)/shard_map/ppermute | solution.py:676
